TPU v7x, 128 devices: a whole 4x4x4 slice. The times are simulated.
128 devices in a mesh: clip: 32 (over z_hi, y, x), head: 4 (over z_lo, core).
Axes of the slice: x: 4, y: 4, z: 4 (z_hi: 2, z_lo: 2; z = z_hi * 2 + z_lo), core: 2. Of those that a mesh axis runs over, the one named last changes fastest.
Arguments:
- video: bfloat16 [16384, 3072], P(('clip', 'head')), may hold values from -6 to 6
- norm_gain: float32 [2, 3072], replicated, may hold values from 0.25 to 1.75
- w_qkv: bfloat16 [2, 3072, 3, 1536], P(None, None, None, 'head'), may hold values from -0.109375 to 0.109375
- qk_gain: float32 [2, 2, 128], replicated, may hold values from 0.5 to 2
- w_out: bfloat16 [2, 1536, 3072], P(None, 'head'), may hold values from -0.875 to 0.875
- skip_layer: int32 [64], P('clip'), may hold values from 0 to 1
- halo_frames: int32 [64], P('clip'), may hold values from 1 to 2, as said below
- context_index: int32 [64, 8], P('clip'), may hold values from 0 to 255, as said below
Outputs:
- guided: bfloat16 [16384, 3072], P(('clip', 'head'))
Inputs may be any that keep to these rules, and one draw needn't show every extreme that they name: `halo_frames`: every draw holds a clip with 2 and a clip with 1. `context_index`: within a clip the indices increase, one in each run of 32 positions.
All inputs are finite; a program needn't handle non-finite values.
Results may differ from a plain program's by a relative error of at most 0.028.
Values may be sent and summed in bfloat16 or wider, within the bound.
No kernel may reach another device: no remote copies, remote signals or barrier semaphores. Data moves between devices by JAX's collectives and lax.ppermute only.
A program may use at most 128 MiB of HBM per device.

v0:
```python
import functools
import math

import jax
import jax.numpy as jnp
from jax import lax
from jax.experimental import pallas as pl
from jax.experimental.pallas import tpu as pltpu
from jax.sharding import PartitionSpec as P


D = 3072
HD = 128
HL = 3
INNER = HL * HD
BLK = 128
CLIP_TOK = 256
CTX = 8
HALO = 32
QUART = D // 4
GUIDE = 1.5
EPS = 1e-06
AXES = ("clip", "head")
F32, BF16 = jnp.float32, jnp.bfloat16
ANY = pl.BlockSpec(memory_space=pl.ANY)
VM = pl.BlockSpec(memory_space=pltpu.VMEM)
SM = pl.BlockSpec(memory_space=pltpu.SMEM)


def moved(clips, heads, rule):
    pairs = []
    for c in range(clips):
        for h in range(heads):
            to = rule(c, h)
            if to is not None:
                pairs.append((c * heads + h, to[0] * heads + to[1]))
    return pairs


def send(value, rule):
    pairs = moved(lax.axis_size("clip"), lax.axis_size("head"), rule)
    return lax.ppermute(value, AXES, pairs)


def to_sib(c, h):
    return c, h ^ 1


def to_z(c, h):
    return c, h ^ 2


def to_diag(c, h):
    return c, h ^ 3


def to_far(c, h):
    return c ^ 16, h


def to_far_z(c, h):
    return c ^ 16, h ^ 2


def to_x(step):
    return lambda c, h: ((c & ~3) | ((c + step) & 3), h)


def to_y(step):
    return lambda c, h: ((c & ~12) | ((c + 4 * step) & 12), h)


def edge_own(c, h):
    to = c - 1 if h < 2 else c + 1
    return (to, h) if 0 <= to < 32 else None


def edge_par(c, h):
    to = c + 1 if h < 2 else c - 1
    return (to, h) if 0 <= to < 32 else None


def shape(*dims):
    return jax.ShapeDtypeStruct(dims, BF16)


def params(mib):
    return pltpu.CompilerParams(vmem_limit_bytes=mib * 1024 * 1024)


def pack_kernel(*refs):
    out = refs[-1]
    step = out.shape[0] // (len(refs) - 1)
    for i, ref in enumerate(refs[:-1]):
        out[i * step : (i + 1) * step] = ref[...]


def pack(*parts):
    lead, rest = parts[0].shape[0], parts[0].shape[1:]
    return pl.pallas_call(
        pack_kernel,
        out_shape=shape(len(parts) * lead, *rest),
        in_specs=[VM] * len(parts),
        out_specs=VM,
        compiler_params=params(4),
        name="pack",
    )(*parts)


def quarter(turn, k):
    off = jnp.where(k == 0, 0, jnp.where(k == 1, 3, k - 1))
    return pl.multiple_of(((turn + off) & 3) * QUART, QUART)


def stage_kernel(w, out, sems):
    copies = [
        pltpu.make_async_copy(
            w.at[l, c], out.at[l, :, pl.ds(c * INNER, INNER)], sems.at[3 * l + c]
        )
        for l in range(2)
        for c in range(3)
    ]
    for copy in copies:
        copy.start()
    for copy in copies:
        copy.wait()


def stage(w):
    return pl.pallas_call(
        stage_kernel,
        out_shape=pltpu.VMEM((2, D, 3 * INNER), BF16),
        in_specs=[pl.BlockSpec(memory_space=pltpu.HBM)],
        out_specs=VM,
        scratch_shapes=[pltpu.SemaphoreType.DMA((6,))],
        compiler_params=params(2),
        name="stage",
    )(w)


def assemble_kernel(layer, wo, wsib, *refs):
    wz, wzs, out, sems = refs[:4], refs[4:8], refs[8], refs[9]
    copies = []
    for k in range(4):
        cols = pl.ds(quarter(place()[2 + layer], k), QUART)
        for j, src in enumerate(
            (wo.at[layer, :, cols], wsib.at[layer, :, cols], wz[k], wzs[k])
        ):
            dst = out.at[k, pl.ds(j * INNER, INNER)]
            copies.append(pltpu.make_async_copy(src, dst, sems.at[4 * k + j]))
    for copy in copies:
        copy.start()
    for copy in copies:
        copy.wait()


def assemble(layer, wo, wsib, wz, wzs):
    hbm = pl.BlockSpec(memory_space=pltpu.HBM)
    return pl.pallas_call(
        functools.partial(assemble_kernel, layer),
        out_shape=pltpu.VMEM((4, 4 * INNER, QUART), BF16),
        in_specs=[hbm] * 10,
        out_specs=VM,
        scratch_shapes=[pltpu.SemaphoreType.DMA((16,))],
        compiler_params=params(2),
        name="assemble",
    )(wo, wsib, *wz, *wzs)


def norm_rows(src, gain, dst, row0, rows):
    def step(i, carry):
        at = pl.ds(pl.multiple_of(i * 16, 16), 16)
        to = pl.ds(pl.multiple_of(row0 + i * 16, 16), 16)
        v = src[at, :].astype(F32)
        ms = jnp.mean(v * v, axis=-1, keepdims=True)
        dst[to, :] = (v * lax.rsqrt(ms + EPS) * gain[...]).astype(BF16)
        return carry

    lax.fori_loop(0, rows // 16, step, 0)


def head_norm(p, gain):
    parts = []
    for h in range(HL):
        ph = p[:, h * HD : (h + 1) * HD]
        ms = jnp.mean(ph * ph, axis=-1, keepdims=True)
        parts.append(ph * lax.rsqrt(ms + EPS) * gain)
    return jnp.concatenate(parts, axis=1)


def project(normed, w, l, qkg, put, rows):
    def step(m, carry):
        row = pl.multiple_of(m * CLIP_TOK, CLIP_TOK)
        p = jnp.dot(
            normed[pl.ds(row, CLIP_TOK), :], w[l], preferred_element_type=F32
        )
        for c in range(3):
            pc = p[:, c * INNER : (c + 1) * INNER]
            if c < 2:
                pc = head_norm(pc, qkg[l, c : c + 1, :])
            put(m, c, pc.astype(BF16))
        return carry

    lax.fori_loop(0, rows // CLIP_TOK, step, 0)


def place():
    clip, head = lax.axis_index("clip"), lax.axis_index("head")
    return head & 1, head >> 1, clip & 3, (clip >> 2) & 3


def parity_of(which):
    zlo = place()[1]
    return zlo if which == 0 else 1 - zlo


def put_edges(which, rows, outer, inner):
    core, parity = place()[0], parity_of(which)
    for edge, last in ((outer, parity), (inner, 1 - parity)):
        start = pl.multiple_of((last ^ core) * BLK + last * (BLK - HALO), HALO)
        for kv in range(2):
            edge[kv] = rows(kv, pl.ds(start, HALO))


def rows_kernel(ci, x, out, low, high):
    low[...] = x[: BLK // 2, :]
    high[...] = x[BLK // 2 :, :]
    core, zlo = place()[:2]
    row = lax.broadcasted_iota(jnp.int32, (8, BLK), 0)
    col = lax.broadcasted_iota(jnp.int32, (8, BLK), 1)
    at = jnp.full((8, BLK), -1, jnp.int32)
    for r in range(4):
        at = jnp.where(row == r, ci[zlo, 4 * core + r] - core * BLK, at)
    hot = jnp.where(col == at, 1.0, 0.0).astype(BF16)
    got = jnp.dot(hot, x[...], preferred_element_type=F32)
    out[...] = got[:4].astype(BF16)


def context_rows(ci, x):
    return pl.pallas_call(
        rows_kernel,
        out_shape=(shape(4, D), shape(BLK // 2, D), shape(BLK // 2, D)),
        in_specs=[SM, VM],
        out_specs=(VM, VM, VM),
        compiler_params=params(4),
        name="context_rows",
    )(ci, x)


def context_kernel(c0, c1, c2, c3, gain, w, qkg, out, xs, normed):
    for j, c in enumerate((c0, c1, c2, c3)):
        xs[4 * j : 4 * j + 4, :] = c[...].astype(F32)
    v = xs[...]
    v = v * lax.rsqrt(jnp.mean(v * v, axis=-1, keepdims=True) + EPS)
    xs[...] = v

    def step(l, carry):
        normed[...] = (xs[...] * gain[pl.ds(l, 1), :]).astype(BF16)
        p = jnp.dot(normed[...], w[l, :, INNER:], preferred_element_type=F32)
        out[0, l, 0] = head_norm(p[:, :INNER], qkg[l, 1:2, :]).astype(BF16)
        out[0, l, 1] = p[:, INNER:].astype(BF16)
        return carry

    lax.fori_loop(0, 2, step, 0)


def context_kv(c, gain, w, qkg):
    return pl.pallas_call(
        context_kernel,
        out_shape=shape(1, 2, 2, 2 * CTX, INNER),
        in_specs=[VM] * 7,
        out_specs=VM,
        scratch_shapes=[
            pltpu.VMEM((2 * CTX, D), F32),
            pltpu.VMEM((2 * CTX, D), BF16),
        ],
        compiler_params=params(4),
        cost_estimate=pl.CostEstimate(
            flops=2 * 256 * D * 4 * INNER, transcendentals=0, bytes_accessed=8 * D * INNER
        ),
        name="context_kv",
    )(*c, gain, w, qkg)


def qkv_kernel(l, which, *refs):
    pieces, (gain, w, qkg, out, outer, inner, normed) = refs[:-7], refs[-7:]
    row = 0
    for src in pieces:
        norm_rows(src, gain.at[l : l + 1], normed, row, src.shape[0])
        row += src.shape[0]

    def put(m, c, p):
        out[c] = p

    project(normed, w, l, qkg, put, CLIP_TOK)
    put_edges(which, lambda kv, at: out[1 + kv, at, :], outer, inner)


def qkv(l, which, pieces, gain, w, qkg):
    return pl.pallas_call(
        functools.partial(qkv_kernel, l, which),
        out_shape=(
            shape(3, CLIP_TOK, INNER),
            shape(2, HALO, INNER),
            shape(2, HALO, INNER),
        ),
        in_specs=[VM] * (len(pieces) + 3),
        out_specs=(VM, VM, VM),
        scratch_shapes=[pltpu.VMEM((CLIP_TOK, D), BF16)],
        compiler_params=params(7),
        cost_estimate=pl.CostEstimate(
            flops=2 * CLIP_TOK * D * 3 * INNER,
            transcendentals=0,
            bytes_accessed=2 * (3 * D * INNER + CLIP_TOK * D),
        ),
        name="qkv",
    )(*pieces, gain, w, qkg)


def halo_mask(halo, which):
    parity = parity_of(which)
    seen = halo[parity]
    end = jnp.where(parity == 0, 0, lax.axis_size("clip") - 1)
    exists = jnp.where(lax.axis_index("clip") == end, 0, 1)
    lane = lax.broadcasted_iota(jnp.int32, (1, 2 * HALO), 1)
    mask = jnp.zeros((1, 2 * HALO), F32)
    for side, count in enumerate((seen, seen * exists)):
        prev = parity if side == 0 else 1 - parity
        low = side * HALO + prev * (HALO - 16 * count)
        mask = jnp.where(lane >= low, jnp.where(lane < low + 16 * count, 1.0, mask), mask)
    return mask


def attend_clip(cl, mask, mine, inner, outer, ctx, put, at=0):
    factor = math.log2(math.e) / math.sqrt(HD)
    tn = (((1,), (1,)), ((), ()))

    def step(h, carry):
        cols = pl.ds(pl.multiple_of(h * HD, HD), HD)
        q = mine[0, :, cols]
        rows = []
        for kv in range(2):
            parts = [mine[1 + kv, :, cols]]
            for ref in ctx:
                parts.append(ref[:, cl, kv, :, cols].reshape(-1, HD))
            rows.append(jnp.concatenate(parts, axis=0))
        k, v = rows
        kh = jnp.concatenate([inner[0, :, cols], outer[at, :, cols]], axis=0)
        vh = jnp.concatenate([inner[1, :, cols], outer[at + 1, :, cols]], axis=0)
        v = jnp.concatenate([v, jnp.ones_like(v)], axis=1)
        vh = jnp.concatenate([vh, jnp.ones_like(vh)], axis=1)
        s = lax.dot_general(q, k, tn, preferred_element_type=F32)
        sh = lax.dot_general(q, kh, tn, preferred_element_type=F32)
        p = jnp.exp2(s * factor).astype(BF16)
        ph = (jnp.exp2(sh * factor) * mask).astype(BF16)
        r = jnp.dot(p, v, preferred_element_type=F32)
        r = r + jnp.dot(ph, vh, preferred_element_type=F32)
        put(cols, (r[:, :HD] / r[:, HD:]).astype(BF16))
        return carry

    lax.fori_loop(0, HL, step, 0)


def attend_cost(clips, ctx):
    keys = CLIP_TOK + 2 * HALO + sum(c.shape[0] * c.shape[3] for c in ctx)
    return pl.CostEstimate(
        flops=clips * 6 * CLIP_TOK * keys * INNER,
        transcendentals=clips * HL * CLIP_TOK * keys,
        bytes_accessed=4 * keys * INNER + clips * 4 * CLIP_TOK * INNER,
    )


def attend_kernel(cl, which, halo, mine, inner, outer, c0, c1, c2, c3, out):
    def put(cols, a):
        out[0, :, cols] = a[:BLK]
        out[1, :, cols] = a[BLK:]

    ctx = (c0, c1, c2, c3)
    attend_clip(cl, halo_mask(halo, which), mine, inner, outer, ctx, put)


def attend(cl, which, halo, mine, inner, outer, ctx):
    return pl.pallas_call(
        functools.partial(attend_kernel, cl, which),
        out_shape=shape(2, BLK, INNER),
        in_specs=[SM] + [VM] * 7,
        out_specs=VM,
        compiler_params=params(7),
        cost_estimate=attend_cost(1, ctx),
        name="attend",
    )(halo, mine, inner, outer, *ctx)


def attend_pair_kernel(cl, at, *refs):
    (halo, qo, io, eo, qp, ip, ep) = refs[:7]
    ctx, (o0, o1, p0, p1) = refs[7:11], refs[11:]
    for which, args, (low, high) in (
        (0, (qo, ip, eo), (o0, o1)),
        (1, (qp, io, ep), (p0, p1)),
    ):

        def put(cols, a, low=low, high=high):
            low[:, cols] = a[:BLK]
            high[:, cols] = a[BLK:]

        attend_clip(cl, halo_mask(halo, which), *args, ctx, put, at)


def attend_pair(cl, at, halo, own, par, outer_own, outer_par, ctx):
    return pl.pallas_call(
        functools.partial(attend_pair_kernel, cl, at),
        out_shape=(shape(BLK, INNER),) * 4,
        in_specs=[SM] + [VM] * 10,
        out_specs=(VM,) * 4,
        compiler_params=params(7),
        cost_estimate=attend_cost(2, ctx),
        name="attend_pair",
    )(halo, own[0], own[2], outer_own, par[0], par[2], outer_par, *ctx)


def first_kernel(*refs):
    (o0, p0, o1, p1, o2, p2, o3, p3) = refs[:8]
    xs, refs = refs[8:-16], refs[-16:]
    (wslot, gain, w, qkg, ci) = refs[:5]
    (first, qo, eo, io, qp, ep, ip, ctx) = refs[5:13]
    (acat, xbuf, normed) = refs[13:]
    for j, (ao, ap) in enumerate(((o0, p0), (o1, p1), (p2, o2), (p3, o3))):
        for clip, piece in enumerate((ao, ap)):
            for b in range(2):
                row = (2 * clip + b) * BLK
                acat[row : row + BLK, j * INNER : (j + 1) * INNER] = piece[b ^ (j & 1)]
    rows = 2 * CLIP_TOK

    def block(k, carry):
        cols = pl.ds(quarter(place()[2], k), QUART)
        row = 0
        for x in xs:
            if row % CLIP_TOK == 0:
                left = acat[row : row + CLIP_TOK, :]
                t = jnp.dot(left, wslot[k], preferred_element_type=F32)
            end = row + x.shape[0]
            base = row - row % CLIP_TOK
            v = x[:, cols].astype(F32) + t[row - base : end - base]
            xbuf[row:end, cols] = v.astype(BF16)
            row = end
        return carry

    lax.fori_loop(0, 4, block, 0)
    first[...] = xbuf[:BLK, :]
    norm_rows(xbuf, gain.at[1:2], normed, 0, rows)

    def put(m, c, p):
        @pl.when(m == 0)
        def _():
            qo[c] = p

        @pl.when(m == 1)
        def _():
            qp[c] = p

    project(normed, w, 1, qkg, put, rows)
    col = lax.broadcasted_iota(jnp.int32, (CLIP_TOK, CTX), 0)
    found = []
    for which, (q, e, i) in enumerate(((qo, eo, io), (qp, ep, ip))):
        put_edges(which, lambda kv, at, q=q: q[1 + kv, at, :], e, i)
        idx = jnp.where(parity_of(which) == 0, ci[0:1, :], ci[1:2, :])
        rel = ((idx // BLK) ^ place()[0]) * BLK + idx % BLK
        hot = jnp.where(col == rel, 1.0, 0.0).astype(BF16)
        tt = (((0,), (0,)), ((), ()))
        found.append(
            [
                lax.dot_general(hot, q[1 + kv], tt, preferred_element_type=F32)
                for kv in range(2)
            ]
        )
    for kv in range(2):
        both = jnp.concatenate([found[0][kv], found[1][kv]], axis=0)
        ctx[0, 0, kv] = both.astype(BF16)


def first_qkv(atts, xs, wslot, gain, w, qkg, ci):
    one = (
        shape(3, CLIP_TOK, INNER),
        shape(2, HALO, INNER),
        shape(2, HALO, INNER),
    )
    rows = 2 * CLIP_TOK
    res = pl.pallas_call(
        first_kernel,
        out_shape=(shape(BLK, D),) + one + one + (shape(1, 1, 2, 2 * CTX, INNER),),
        in_specs=[VM] * (13 + len(xs)),
        out_specs=(VM,) * 8,
        scratch_shapes=[
            pltpu.VMEM((rows, 4 * INNER), BF16),
            pltpu.VMEM((rows, D), BF16),
            pltpu.VMEM((rows, D), BF16),
        ],
        compiler_params=params(14),
        cost_estimate=pl.CostEstimate(
            flops=2 * rows * D * 7 * INNER,
            transcendentals=0,
            bytes_accessed=2 * (7 * D * INNER + 2 * rows * D),
        ),
        name="first_qkv",
    )(*atts, *xs, wslot, gain, w, qkg, ci)
    return res[0], res[1:4], res[4:7], res[7]


def final_kernel(*refs):
    skip, atts, others = refs[0], refs[1:5], refs[5:9]
    (video, first, wslot, out, acat) = refs[9:]
    for j in range(4):
        for b, piece in enumerate((atts[j], others[j])):
            acat[b * BLK : (b + 1) * BLK, j * INNER : (j + 1) * INNER] = piece[...]
    skip_first = skip[place()[1]] == 0

    def block(k, carry):
        cols = pl.ds(quarter(place()[3], k), QUART)
        t = jnp.dot(acat[...], wslot[k], preferred_element_type=F32)
        f = first[:, cols].astype(F32)
        strong = (f + t[:BLK]).astype(BF16).astype(F32)
        other = (video[:, cols].astype(F32) + t[BLK:]).astype(BF16).astype(F32)
        weak = jnp.where(skip_first, other, f)
        out[:, cols] = (strong + GUIDE * (strong - weak)).astype(BF16)
        return carry

    lax.fori_loop(0, 4, block, 0)


def final(skip, atts, others, video, first, wslot):
    return pl.pallas_call(
        final_kernel,
        out_shape=shape(BLK, D),
        in_specs=[SM] + [VM] * 11,
        out_specs=VM,
        scratch_shapes=[pltpu.VMEM((2 * BLK, 4 * INNER), BF16)],
        compiler_params=params(7),
        cost_estimate=pl.CostEstimate(
            flops=4 * BLK * D * 4 * INNER,
            transcendentals=0,
            bytes_accessed=2 * (4 * D * INNER + 3 * BLK * D),
        ),
        name="final",
    )(skip, *atts, *others, video, first, wslot)


def after(value, *done):
    return lax.optimization_barrier((value,) + done)[0]


def columns_kernel(wo, *refs):
    outs, sems = refs[:2], refs[2]
    copies = []
    for l in range(2):
        cols = pl.ds(pl.multiple_of(place()[2 + l] * QUART, QUART), QUART)
        copies.append(
            pltpu.make_async_copy(wo.at[l, :, cols], outs[l], sems.at[l])
        )
    for copy in copies:
        copy.start()
    for copy in copies:
        copy.wait()


def columns(weight):
    return pl.pallas_call(
        columns_kernel,
        out_shape=(shape(INNER, QUART),) * 2,
        in_specs=[pl.BlockSpec(memory_space=pltpu.HBM)],
        out_specs=(VM, VM),
        scratch_shapes=[pltpu.SemaphoreType.DMA((2,))],
        compiler_params=params(3),
        name="columns",
    )(weight)


def edges(own, par):
    return send(par[1], edge_par), send(own[1], edge_own)


def body(video, norm_gain, w_qkv, qk_gain, w_out, skip_layer, halo_frames, context_index):
    x0 = video
    piece0, piece1 = columns(w_out)
    here0 = send(piece0, to_far_z)
    c0, xa, xb = context_rows(context_index, after(x0, piece0))
    c = [c0, send(c0, to_sib), send(c0, to_z), send(c0, to_diag)]
    x2a = send(xa, to_z)
    x1 = send(after(x0, c0), to_sib)
    w = stage(jnp.transpose(w_qkv, (0, 2, 1, 3)))
    kv = context_kv(c, norm_gain, w, qk_gain)
    kz = send(kv, to_far)
    x2b = send(after(xb, kv), to_z)
    own0 = qkv(0, 0, (after(x0, kv), x1), norm_gain, w, qk_gain)
    kx = pack(kv, after(kz, own0[0]))
    kxs = [send(kx, to_x(d)) for d in (1, 3, 2)]
    wz0 = [here0] + [send(after(here0, kx), to_x(d)) for d in (1, 3, 2)]
    x3a = send(after(x2a, kx), to_sib)
    own1 = qkv(1, 0, (after(x0, kx), x1), norm_gain, w, qk_gain)
    ky = pack(kx, *[after(k, own1[0]) for k in kxs])
    kys = [send(ky, to_y(d)) for d in (1, 3, 2)]
    x3b = send(after(x2b, own1[0]), to_sib)
    halves = (after(x2a, ky), x2b, x3a, x3b)
    par0 = qkv(0, 1, halves, norm_gain, w, qk_gain)
    eo, ep = edges(own0, par0)
    wsib = send(after(w_out, par0[0]), to_sib)
    here1 = send(after(piece1, par0[0]), to_far_z)
    ctx = [ky] + kys
    ao = attend(0, 0, halo_frames, own0[0], par0[2], eo, ctx)
    oz = send(ao, to_z)
    os = send(ao, to_sib)
    ap = attend(0, 1, halo_frames, after(par0[0], ao), own0[2], ep, ctx)
    pz = send(ap, to_z)
    ps = send(ap, to_sib)
    halves = (after(x2a, ap), x2b, x3a, x3b)
    par1 = qkv(1, 1, halves, norm_gain, w, qk_gain)
    wzs0 = [send(after(p, ap), to_sib) for p in wz0]
    wz1 = [here1] + [send(after(here1, par1[0]), to_y(d)) for d in (1, 3, 2)]
    ozs = send(after(oz, par1[0]), to_sib)
    wslot0 = assemble(0, after(w_out, par1[0]), wsib, wz0, wzs0)
    pzs = send(pz, to_sib)

    first, fo, fp, fkv = first_qkv(
        (ao, ap, os, ps, oz, pz, ozs, pzs),
        (x0, x1, x2a, x2b, x3a, x3b),
        wslot0,
        norm_gain,
        w,
        qk_gain,
        context_index,
    )
    fz = send(fkv, to_far)
    both_own = pack(own1[1], fo[1])
    both_par = pack(par1[1], fp[1])
    fx = pack(fkv, fz)
    fxs = [send(fx, to_x(d)) for d in (1, 3, 2)]
    so, sp = edges((None, after(both_own, fx)), (None, after(both_par, fx)))
    fy = pack(fx, *fxs)
    fys = [send(fy, to_y(d)) for d in (1, 3, 2)]
    mine = (after(own1[0], fy),) + own1[1:]
    b = attend_pair(1, 0, halo_frames, mine, par1, so, sp, ctx)
    others = [b[0], send(b[1], to_sib), send(b[2], to_z), send(b[3], to_diag)]
    mine = (after(fo[0], b[0]),) + fo[1:]
    g = attend_pair(0, 2, halo_frames, mine, fp, so, sp, [fy] + fys)
    atts = [g[0], send(g[1], to_sib), send(g[2], to_z), send(g[3], to_diag)]
    wzs1 = [send(after(p, b[0]), to_sib) for p in wz1]
    wslot1 = assemble(1, after(w_out, g[0]), wsib, wz1, wzs1)
    return final(skip_layer, atts, others, x0, first, wslot1)


def solution(mesh):
    in_specs = (
        P(("clip", "head"), None),
        P(),
        P(None, None, None, "head"),
        P(),
        P(None, "head", None),
        P("clip"),
        P("clip"),
        P("clip", None),
    )
    out_specs = P(("clip", "head"), None)

    return jax.shard_map(
        body, mesh=mesh, in_specs=in_specs, out_specs=out_specs, check_vma=False
    )
```

profile of v0, /device:TPU:64, one launch (start us, length us, event | category | flops | bytes accessed | tf_op | source)
XLA Modules:
  0.0 225.9 jit_solution(7810505959632051402)
XLA Ops:
  0.0 2.3 %copy-done = bf16[2,384,3072]{2,1,0:T(8,128)(2,1)S(1)} copy-done((bf16[2,384,3072]{2,1,0:T(8,128)(2,1)S(1)}, bf16[2,384,3072]{2,1,0:T(8,128)(2,1)}, u32[]{:S(2)}) %copy-start) | copy-done | bytes 4718616
  6.7 5.0 %copy-done.3 = bf16[2,3072,3,384]{3,1,2,0:T(8,128)(2,1)S(1)} copy-done((bf16[2,3072,3,384]{3,1,2,0:T(8,128)(2,1)S(1)}, bf16[2,3072,3,384]{3,1,2,0:T(8,128)(2,1)}, u32[]{:S(2)}) %copy-start.3) | copy-done | bytes 14155800
  17.1 5.5 %qkv.4 = (bf16[3,256,384]{2,1,0:T(8,128)(2,1)S(1)}, bf16[2,32,384]{2,1,0:T(8,128)(2,1)S(1)}, bf16[2,32,384]{2,1,0:T(8,128)(2,1)S(1)}) custom-call(bf16[128,3072]{1,0:T(8,128)(2,1)} %refs_9_.1, bf16[128,3072]{1,0:T(8,128)(2,1)S(1)} %collective-permute-done.3.refs_1_.refs_9_, f32[2,3072]{1,0:T(2,128)S(1)} %copy-done.4, ...), custom_call_target="tpu_custom_call" | custom-call | flops 1811939328 | bytes 8650752 | tf_op jit(solution)/shard_map/qkv/pallas_call | solution.py:300
  22.7 13.0 %collective-permute-done.5.refs_1_ = bf16[1,2,2,16,384]{4,3,2,1,0:T(8,128)(2,1)S(1)} collective-permute-done((bf16[1,2,2,16,384]{4,3,2,1,0:T(8,128)(2,1)S(1)}, bf16[1,2,2,16,384]{4,3,2,1,0:T(8,128)(2,1)S(1)}, u32[]{:S(2)}, u32[]{:S(2)}) %collective-permute-start.5) | collective-permute-done | bytes 49184 | tf_op jit(solution)/shard_map/ppermute | solution.py:42
  35.7 5.5 %qkv.5 = (bf16[3,256,384]{2,1,0:T(8,128)(2,1)S(1)}, bf16[2,32,384]{2,1,0:T(8,128)(2,1)S(1)}, bf16[2,32,384]{2,1,0:T(8,128)(2,1)S(1)}) custom-call(bf16[128,3072]{1,0:T(8,128)(2,1)} %refs_9_.1, bf16[128,3072]{1,0:T(8,128)(2,1)S(1)} %collective-permute-done.3.refs_1_.refs_9_, f32[2,3072]{1,0:T(2,128)S(1)} %copy-done.4, ...), custom_call_target="tpu_custom_call" | custom-call | flops 1811939328 | bytes 8650752 | tf_op jit(solution)/shard_map/qkv/pallas_call | solution.py:300
  41.8 3.0 %collective-permute-start.8 = (bf16[2,2,2,16,384]{4,3,2,1,0:T(8,128)(2,1)S(1)}, bf16[2,2,2,16,384]{4,3,2,1,0:T(8,128)(2,1)S(1)}, u32[]{:S(2)}, u32[]{:S(2)}) collective-permute-start(bf16[2,2,2,16,384]{4,3,2,1,0:T(8,128)(2,1)S(1)} %pack.6.refs_0_), channel_id=1, source_target_pairs={{0,8},{1,9},{2,10},{3,11},{4,12},{5,13},{6,14},{7,15},{8,0},{9,1},... | collective-permute-start | bytes 294920 | tf_op jit(solution)/shard_map/ppermute | solution.py:42
  51.9 4.4 %qkv.6 = (bf16[3,256,384]{2,1,0:T(8,128)(2,1)S(1)}, bf16[2,32,384]{2,1,0:T(8,128)(2,1)S(1)}, bf16[2,32,384]{2,1,0:T(8,128)(2,1)S(1)}) custom-call(bf16[64,3072]{1,0:T(8,128)(2,1)S(1)} %collective-permute-done.4.refs_0_.refs_10_, bf16[64,3072]{1,0:T(8,128)(2,1)S(1)} %collective-permute-done.9.refs_1_.refs_11_, ...), custom_call_target="tpu_custom_call" | custom-call | flops 1811939328 | bytes 8650752 | tf_op jit(solution)/shard_map/qkv/pallas_call | solution.py:300
  56.4 2.0 collective-permute-start.24
  61.6 2.0 collective-permute-start.15
  63.6 8.7 %collective-permute-done.24.refs_0_ = bf16[384,768]{1,0:T(8,128)(2,1)S(1)} collective-permute-done((bf16[384,768]{1,0:T(8,128)(2,1)S(1)}, bf16[384,768]{1,0:T(8,128)(2,1)S(1)}, u32[]{:S(2)}, u32[]{:S(2)}) %collective-permute-start.24) | collective-permute-done | bytes 589856 | tf_op jit(solution)/shard_map/ppermute | solution.py:42
  72.3 9.6 %collective-permute-start.16 = (bf16[2,32,384]{2,1,0:T(8,128)(2,1)S(1)}, bf16[2,32,384]{2,1,0:T(8,128)(2,1)S(1)}, u32[]{:S(2)}, u32[]{:S(2)}) collective-permute-start(bf16[2,32,384]{2,1,0:T(8,128)(2,1)S(1)} %get-tuple-element.94), channel_id=1, source_target_pairs={{2,6},{3,7},{4,0},{5,1},{6,10},{7,11},{8,4},{9,5},{10,14},{11,15},... | collective-permute-start | bytes 147464 | tf_op jit(solution)/shard_map/ppermute | solution.py:42
  85.5 11.8 %collective-permute-done.12.outer = bf16[2,32,384]{2,1,0:T(8,128)(2,1)S(1)} collective-permute-done((bf16[2,32,384]{2,1,0:T(8,128)(2,1)S(1)}, bf16[2,32,384]{2,1,0:T(8,128)(2,1)S(1)}, u32[]{:S(2)}, u32[]{:S(2)}) %collective-permute-start.12) | collective-permute-done | bytes 49184 | tf_op jit(solution)/shard_map/ppermute | solution.py:42
  97.4 2.0 collective-permute-start.25
  99.4 2.8 %attend.2.refs_0_ = bf16[2,128,384]{2,1,0:T(8,128)(2,1)S(1)} custom-call(s32[2]{0:T(128)S(1)} %copy-done.6, bf16[3,256,384]{2,1,0:T(8,128)(2,1)S(1)} %get-tuple-element.76.mine, bf16[2,32,384]{2,1,0:T(8,128)(2,1)S(1)} %get-tuple-element.89.inner, bf16[2,32,384]{2,1,0:T(8,128)(2,1)S(1)} %collective-permute-done.12.outer, ...), custom_call_target="tpu_custom_call" | custom-call | flops 490733568 | bytes 1671168 | tf_op jit(solution)/shard_map/attend/pallas_call | solution.py:383
  102.3 12.8 %collective-permute-done.27.refs_3_ = bf16[384,768]{1,0:T(8,128)(2,1)S(1)} collective-permute-done((bf16[384,768]{1,0:T(8,128)(2,1)S(1)}, bf16[384,768]{1,0:T(8,128)(2,1)S(1)}, u32[]{:S(2)}, u32[]{:S(2)}) %collective-permute-start.27) | collective-permute-done | bytes 589856 | tf_op jit(solution)/shard_map/ppermute | solution.py:42
  115.1 2.8 %attend.3.refs_1_ = bf16[2,128,384]{2,1,0:T(8,128)(2,1)S(1)} custom-call(s32[2]{0:T(128)S(1)} %copy-done.6, bf16[3,256,384]{2,1,0:T(8,128)(2,1)S(1)} %get-tuple-element.92.mine, bf16[2,32,384]{2,1,0:T(8,128)(2,1)S(1)} %get-tuple-element.93.inner, bf16[2,32,384]{2,1,0:T(8,128)(2,1)S(1)} %collective-permute-done.16.outer, ...), custom_call_target="tpu_custom_call" | custom-call | flops 490733568 | bytes 1671168 | tf_op jit(solution)/shard_map/attend/pallas_call | solution.py:383
  118.0 2.1 collective-permute-start.20
  120.1 2.5 %collective-permute-done.25.refs_1_ = bf16[384,768]{1,0:T(8,128)(2,1)S(1)} collective-permute-done((bf16[384,768]{1,0:T(8,128)(2,1)S(1)}, bf16[384,768]{1,0:T(8,128)(2,1)S(1)}, u32[]{:S(2)}, u32[]{:S(2)}) %collective-permute-start.25) | collective-permute-done | bytes 589856 | tf_op jit(solution)/shard_map/ppermute | solution.py:42
  124.2 4.4 %qkv.7 = (bf16[3,256,384]{2,1,0:T(8,128)(2,1)S(1)}, bf16[2,32,384]{2,1,0:T(8,128)(2,1)S(1)}, bf16[2,32,384]{2,1,0:T(8,128)(2,1)S(1)}) custom-call(bf16[64,3072]{1,0:T(8,128)(2,1)S(1)} %collective-permute-done.4.refs_0_.refs_10_, bf16[64,3072]{1,0:T(8,128)(2,1)S(1)} %collective-permute-done.9.refs_1_.refs_11_, ...), custom_call_target="tpu_custom_call" | custom-call | flops 1811939328 | bytes 8650752 | tf_op jit(solution)/shard_map/qkv/pallas_call | solution.py:300
  131.9 2.0 collective-permute-start.48
  134.0 16.4 %first_qkv.1 = (bf16[128,3072]{1,0:T(8,128)(2,1)S(1)}, bf16[3,256,384]{2,1,0:T(8,128)(2,1)S(1)}, bf16[2,32,384]{2,1,0:T(8,128)(2,1)S(1)}, bf16[2,32,384]{2,1,0:T...) custom-call(bf16[2,128,384]{2,1,0:T(8,128)(2,1)S(1)} %attend.2.refs_, ...), custom_call_target="tpu_custom_call" | custom-call | flops 8455716864 | bytes 22806528 | tf_op jit(solution)/shard_map/first_qkv/pallas_call | solution.py:488
  150.4 3.5 %collective-permute-start.32 = (bf16[1,1,2,16,384]{4,3,2,1,0:T(8,128)(2,1)S(1)}, bf16[1,1,2,16,384]{4,3,2,1,0:T(8,128)(2,1)S(1)}, u32[]{:S(2)}, u32[]{:S(2)}) collective-permute-start(bf16[1,1,2,16,384]{4,3,2,1,0:T(8,128)(2,1)S(1)} %get-tuple-element.106.refs_0_), channel_id=1, source_target_pairs={{0,64},{1,65},{2,66},{3,67},{4,68},{5,69},{6,70},{7,71},{8,72},{9,... | collective-permute-start | bytes 73736 | tf_op jit(solution)/shard_map/ppermute | solution.py:42
  157.1 2.0 collective-permute-start.34
  159.1 2.1 collective-permute-done.33.refs_1_
  162.1 9.0 %collective-permute-start.37 = (bf16[4,32,384]{2,1,0:T(8,128)(2,1)S(1)}, bf16[4,32,384]{2,1,0:T(8,128)(2,1)S(1)}, u32[]{:S(2)}, u32[]{:S(2)}) collective-permute-start(bf16[4,32,384]{2,1,0:T(8,128)(2,1)S(1)} %pack.11), channel_id=1, source_target_pairs={{2,6},{3,7},{4,0},{5,1},{6,10},{7,11},{8,4},{9,5},{10,14},{11,15},... | collective-permute-start | bytes 294920 | tf_op jit(solution)/shard_map/ppermute | solution.py:42
  173.4 10.1 %collective-permute-done.36.refs_3_ = bf16[4,32,384]{2,1,0:T(8,128)(2,1)S(1)} collective-permute-done((bf16[4,32,384]{2,1,0:T(8,128)(2,1)S(1)}, bf16[4,32,384]{2,1,0:T(8,128)(2,1)S(1)}, u32[]{:S(2)}, u32[]{:S(2)}) %collective-permute-start.36) | collective-permute-done | bytes 98336 | tf_op jit(solution)/shard_map/ppermute | solution.py:42
  183.4 5.1 %attend_pair.2 = (bf16[128,384]{1,0:T(8,128)(2,1)S(1)}, bf16[128,384]{1,0:T(8,128)(2,1)S(1)}, bf16[128,384]{1,0:T(8,128)(2,1)S(1)}, bf16[128,384]{1,0:T(8,128)(2,1)S(1)}) custom-call(s32[2]{0:T(128)S(1)} %copy-done.6, bf16[3,256,384]{2,1,0:T(8,128)(2,1)S(1)} %get-tuple-element.107.refs_1_, bf16[2,32,384]{2,1,0:T(8,128)(2,1)S(1)} %get-tuple-element.108.refs_2_, ...), custom_call_target="tpu_custom_call" | custom-call | flops 981467136 | bytes 2064384 | tf_op jit(solution)/shard_map/attend_pair/pallas_call | solution.py:410
  189.7 6.9 %collective-permute-done.39.refs_9_ = bf16[8,1,2,16,384]{4,3,2,1,0:T(8,128)(2,1)S(1)} collective-permute-done((bf16[8,1,2,16,384]{4,3,2,1,0:T(8,128)(2,1)S(1)}, bf16[8,1,2,16,384]{4,3,2,1,0:T(8,128)(2,1)S(1)}, u32[]{:S(2)}, u32[]{:S(2)}) %collective-permute-start.39) | collective-permute-done | bytes 196640 | tf_op jit(solution)/shard_map/ppermute | solution.py:42
  196.6 7.6 %collective-permute-done.40.refs_10_ = bf16[8,1,2,16,384]{4,3,2,1,0:T(8,128)(2,1)S(1)} collective-permute-done((bf16[8,1,2,16,384]{4,3,2,1,0:T(8,128)(2,1)S(1)}, bf16[8,1,2,16,384]{4,3,2,1,0:T(8,128)(2,1)S(1)}, u32[]{:S(2)}, u32[]{:S(2)}) %collective-permute-start.40) | collective-permute-done | bytes 196640 | tf_op jit(solution)/shard_map/ppermute | solution.py:42
  204.1 5.1 %attend_pair.3 = (bf16[128,384]{1,0:T(8,128)(2,1)S(1)}, bf16[128,384]{1,0:T(8,128)(2,1)S(1)}, bf16[128,384]{1,0:T(8,128)(2,1)S(1)}, bf16[128,384]{1,0:T(8,128)(2,1)S(1)}) custom-call(s32[2]{0:T(128)S(1)} %copy-done.6, bf16[3,256,384]{2,1,0:T(8,128)(2,1)S(1)} %get-tuple-element.117.refs_1_, bf16[2,32,384]{2,1,0:T(8,128)(2,1)S(1)} %get-tuple-element.118.refs_2_, ...), custom_call_target="tpu_custom_call" | custom-call | flops 981467136 | bytes 2064384 | tf_op jit(solution)/shard_map/attend_pair/pallas_call | solution.py:410
  216.2 3.0 %collective-permute-done.42.refs_3_ = bf16[128,384]{1,0:T(8,128)(2,1)S(1)} collective-permute-done((bf16[128,384]{1,0:T(8,128)(2,1)S(1)}, bf16[128,384]{1,0:T(8,128)(2,1)S(1)}, u32[]{:S(2)}, u32[]{:S(2)}) %collective-permute-start.42) | collective-permute-done | bytes 98336 | tf_op jit(solution)/shard_map/ppermute | solution.py:42
  220.4 5.5 %final.1 = bf16[128,3072]{1,0:T(8,128)(2,1)} custom-call(s32[2]{0:T(128)S(1)} %copy-done.9, bf16[128,384]{1,0:T(8,128)(2,1)S(1)} %get-tuple-element.121.refs_1_, bf16[128,384]{1,0:T(8,128)(2,1)S(1)} %collective-permute-done.41.refs_2_, bf16[128,384]{1,0:T(8,128)(2,1)S(1)} %collective-permute-done.42.refs_3_, ...), custom_call_target="tpu_custom_call" | custom-call | flops 2415919104 | bytes 11796480 | tf_op jit(solution)/shard_map/final/pallas_call | solution.py:531
  (125 shorter events, 44.8 us)
Async XLA Ops:
  4.5 12.6 %collective-permute-start.3 = (bf16[128,3072]{1,0:T(8,128)(2,1)}, bf16[128,3072]{1,0:T(8,128)(2,1)S(1)}, u32[]{:S(2)}, u32[]{:S(2)}) collective-permute-start(bf16[128,3072]{1,0:T(8,128)(2,1)} %refs_9_.1), channel_id=1, source_target_pairs={{0,1},{1,0},{2,3},{3,2},{4,5},{5,4},{6,7},{7,6},{8,9},{9,8},{10,11... | collective-permute-start | bytes 2359304 | tf_op jit(solution)/shard_map/ppermute | solution.py:42
  4.6 8.6 %collective-permute-start = (bf16[4,3072]{1,0:T(4,128)(2,1)S(1)}, bf16[4,3072]{1,0:T(4,128)(2,1)S(1)}, u32[]{:S(2)}, u32[]{:S(2)}) collective-permute-start(bf16[4,3072]{1,0:T(4,128)(2,1)S(1)} %get-tuple-element.73.c0), channel_id=1, source_target_pairs={{0,1},{1,0},{2,3},{3,2},{4,5},{5,4},{6,7},{7,6},{8,9},{9,8},{10,11... | collective-permute-start | bytes 73736 | tf_op jit(solution)/shard_map/ppermute | solution.py:42
  5.1 8.2 %collective-permute-start.1 = (bf16[4,3072]{1,0:T(4,128)(2,1)S(1)}, bf16[4,3072]{1,0:T(4,128)(2,1)S(1)}, u32[]{:S(2)}, u32[]{:S(2)}) collective-permute-start(bf16[4,3072]{1,0:T(4,128)(2,1)S(1)} %get-tuple-element.73.c0), channel_id=1, source_target_pairs={{0,2},{1,3},{2,0},{3,1},{4,6},{5,7},{6,4},{7,5},{8,10},{9,11},{10,... | collective-permute-start | bytes 73736 | tf_op jit(solution)/shard_map/ppermute | solution.py:42
  15.1 26.1 %collective-permute-start.9 = (bf16[64,3072]{1,0:T(8,128)(2,1)S(1)}, bf16[64,3072]{1,0:T(8,128)(2,1)S(1)}, u32[]{:S(2)}, u32[]{:S(2)}) collective-permute-start(bf16[64,3072]{1,0:T(8,128)(2,1)S(1)} %get-tuple-element.86), channel_id=1, source_target_pairs={{0,2},{1,3},{2,0},{3,1},{4,6},{5,7},{6,4},{7,5},{8,10},{9,11},{10,... | collective-permute-start | bytes 1179656 | tf_op jit(solution)/shard_map/ppermute | solution.py:42
  16.6 24.8 %collective-permute-start.4 = (bf16[64,3072]{1,0:T(8,128)(2,1)S(1)}, bf16[64,3072]{1,0:T(8,128)(2,1)S(1)}, u32[]{:S(2)}, u32[]{:S(2)}) collective-permute-start(bf16[64,3072]{1,0:T(8,128)(2,1)S(1)} %get-tuple-element.77), channel_id=1, source_target_pairs={{0,2},{1,3},{2,0},{3,1},{4,6},{5,7},{6,4},{7,5},{8,10},{9,11},{10,... | collective-permute-start | bytes 1179656 | tf_op jit(solution)/shard_map/ppermute | solution.py:42
  17.1 18.5 %collective-permute-start.5 = (bf16[1,2,2,16,384]{4,3,2,1,0:T(8,128)(2,1)S(1)}, bf16[1,2,2,16,384]{4,3,2,1,0:T(8,128)(2,1)S(1)}, u32[]{:S(2)}, u32[]{:S(2)}) collective-permute-start(bf16[1,2,2,16,384]{4,3,2,1,0:T(8,128)(2,1)S(1)} %context_kv.1.refs_0_), channel_id=1, source_target_pairs={{0,64},{1,65},{2,66},{3,67},{4,68},{5,69},{6,70},{7,71},{8,72},{9,... | collective-permute-start | bytes 147464 | tf_op jit(solution)/shard_map/ppermute | solution.py:42
  41.2 10.6 %collective-permute-start.11 = (bf16[64,3072]{1,0:T(8,128)(2,1)S(1)}, bf16[64,3072]{1,0:T(8,128)(2,1)S(1)}, u32[]{:S(2)}, u32[]{:S(2)}) collective-permute-start(bf16[64,3072]{1,0:T(8,128)(2,1)S(1)} %collective-permute-done.9.refs_1_.refs_11_), channel_id=1, source_target_pairs={{0,1},{1,0},{2,3},{3,2},{4,5},{5,4},{6,7},{7,6},{8,9},{9,8},{10,11... | collective-permute-start | bytes 1179656 | tf_op jit(solution)/shard_map/ppermute | solution.py:42
  41.3 10.5 %collective-permute-start.10 = (bf16[64,3072]{1,0:T(8,128)(2,1)S(1)}, bf16[64,3072]{1,0:T(8,128)(2,1)S(1)}, u32[]{:S(2)}, u32[]{:S(2)}) collective-permute-start(bf16[64,3072]{1,0:T(8,128)(2,1)S(1)} %collective-permute-done.4.refs_0_.refs_10_), channel_id=1, source_target_pairs={{0,1},{1,0},{2,3},{3,2},{4,5},{5,4},{6,7},{7,6},{8,9},{9,8},{10,11... | collective-permute-start | bytes 1179656 | tf_op jit(solution)/shard_map/ppermute | solution.py:42
  56.3 73.4 %collective-permute-start.23 = (bf16[2,384,3072]{2,1,0:T(8,128)(2,1)S(1)}, bf16[2,384,3072]{2,1,0:T(8,128)(2,1)S(1)}, u32[]{:S(2)}, u32[]{:S(2)}) collective-permute-start(bf16[2,384,3072]{2,1,0:T(8,128)(2,1)S(1)} %bitcast.2), channel_id=1, source_target_pairs={{0,1},{1,0},{2,3},{3,2},{4,5},{5,4},{6,7},{7,6},{8,9},{9,8},{10,11... | collective-permute-start | bytes 14155784 | tf_op jit(solution)/shard_map/ppermute | solution.py:42
  56.4 15.9 %collective-permute-start.24 = (bf16[384,768]{1,0:T(8,128)(2,1)S(1)}, bf16[384,768]{1,0:T(8,128)(2,1)S(1)}, u32[]{:S(2)}, u32[]{:S(2)}) collective-permute-start(bf16[384,768]{1,0:T(8,128)(2,1)S(1)} %get-tuple-element.71), channel_id=1, source_target_pairs={{0,66},{1,67},{2,64},{3,65},{4,70},{5,71},{6,68},{7,69},{8,74},{9,... | collective-permute-start | bytes 1769480 | tf_op jit(solution)/shard_map/ppermute | solution.py:42
  58.4 39.0 %collective-permute-start.13 = (bf16[8,2,2,16,384]{4,3,2,1,0:T(8,128)(2,1)S(1)}, bf16[8,2,2,16,384]{4,3,2,1,0:T(8,128)(2,1)S(1)}, u32[]{:S(2)}, u32[]{:S(2)}) collective-permute-start(bf16[8,2,2,16,384]{4,3,2,1,0:T(8,128)(2,1)S(1)} %pack.7.c0.refs_7_), channel_id=1, source_target_pairs={{0,16},{1,17},{2,18},{3,19},{4,20},{5,21},{6,22},{7,23},{8,24},{9,... | collective-permute-start | bytes 1179656 | tf_op jit(solution)/shard_map/ppermute | solution.py:42
  60.0 37.4 %collective-permute-start.14 = (bf16[8,2,2,16,384]{4,3,2,1,0:T(8,128)(2,1)S(1)}, bf16[8,2,2,16,384]{4,3,2,1,0:T(8,128)(2,1)S(1)}, u32[]{:S(2)}, u32[]{:S(2)}) collective-permute-start(bf16[8,2,2,16,384]{4,3,2,1,0:T(8,128)(2,1)S(1)} %pack.7.c0.refs_7_), channel_id=1, source_target_pairs={{0,48},{1,49},{2,50},{3,51},{4,52},{5,53},{6,54},{7,55},{8,56},{9,... | collective-permute-start | bytes 1179656 | tf_op jit(solution)/shard_map/ppermute | solution.py:42
  61.6 37.8 %collective-permute-start.15 = (bf16[8,2,2,16,384]{4,3,2,1,0:T(8,128)(2,1)S(1)}, bf16[8,2,2,16,384]{4,3,2,1,0:T(8,128)(2,1)S(1)}, u32[]{:S(2)}, u32[]{:S(2)}) collective-permute-start(bf16[8,2,2,16,384]{4,3,2,1,0:T(8,128)(2,1)S(1)} %pack.7.c0.refs_7_), channel_id=1, source_target_pairs={{0,32},{1,33},{2,34},{3,35},{4,36},{5,37},{6,38},{7,39},{8,40},{9,... | collective-permute-start | bytes 1179656 | tf_op jit(solution)/shard_map/ppermute | solution.py:42
  72.3 11.3 %collective-permute-start.16 = (bf16[2,32,384]{2,1,0:T(8,128)(2,1)S(1)}, bf16[2,32,384]{2,1,0:T(8,128)(2,1)S(1)}, u32[]{:S(2)}, u32[]{:S(2)}) collective-permute-start(bf16[2,32,384]{2,1,0:T(8,128)(2,1)S(1)} %get-tuple-element.94), channel_id=1, source_target_pairs={{2,6},{3,7},{4,0},{5,1},{6,10},{7,11},{8,4},{9,5},{10,14},{11,15},... | collective-permute-start | bytes 147464 | tf_op jit(solution)/shard_map/ppermute | solution.py:42
  83.6 13.8 %collective-permute-start.12 = (bf16[2,32,384]{2,1,0:T(8,128)(2,1)S(1)}, bf16[2,32,384]{2,1,0:T(8,128)(2,1)S(1)}, u32[]{:S(2)}, u32[]{:S(2)}) collective-permute-start(bf16[2,32,384]{2,1,0:T(8,128)(2,1)S(1)} %get-tuple-element.90), channel_id=1, source_target_pairs={{0,4},{1,5},{4,8},{5,9},{6,2},{7,3},{8,12},{9,13},{10,6},{11,7},{1... | collective-permute-start | bytes 147464 | tf_op jit(solution)/shard_map/ppermute | solution.py:42
  97.4 17.7 %collective-permute-start.27 = (bf16[384,768]{1,0:T(8,128)(2,1)S(1)}, bf16[384,768]{1,0:T(8,128)(2,1)S(1)}, u32[]{:S(2)}, u32[]{:S(2)}) collective-permute-start(bf16[384,768]{1,0:T(8,128)(2,1)S(1)} %collective-permute-done.24.refs_0_), channel_id=1, source_target_pairs={{0,8},{1,9},{2,10},{3,11},{4,12},{5,13},{6,14},{7,15},{8,0},{9,1},... | collective-permute-start | bytes 1769480 | tf_op jit(solution)/shard_map/ppermute | solution.py:42
  97.4 20.6 %collective-permute-start.26 = (bf16[384,768]{1,0:T(8,128)(2,1)S(1)}, bf16[384,768]{1,0:T(8,128)(2,1)S(1)}, u32[]{:S(2)}, u32[]{:S(2)}) collective-permute-start(bf16[384,768]{1,0:T(8,128)(2,1)S(1)} %collective-permute-done.24.refs_0_), channel_id=1, source_target_pairs={{0,12},{1,13},{2,14},{3,15},{4,0},{5,1},{6,2},{7,3},{8,4},{9,5},{1... | collective-permute-start | bytes 1769480 | tf_op jit(solution)/shard_map/ppermute | solution.py:42
  97.4 25.2 %collective-permute-start.25 = (bf16[384,768]{1,0:T(8,128)(2,1)S(1)}, bf16[384,768]{1,0:T(8,128)(2,1)S(1)}, u32[]{:S(2)}, u32[]{:S(2)}) collective-permute-start(bf16[384,768]{1,0:T(8,128)(2,1)S(1)} %collective-permute-done.24.refs_0_), channel_id=1, source_target_pairs={{0,4},{1,5},{2,6},{3,7},{4,8},{5,9},{6,10},{7,11},{8,12},{9,13},{1... | collective-permute-start | bytes 1769480 | tf_op jit(solution)/shard_map/ppermute | solution.py:42
  99.4 24.3 %collective-permute-start.47 = (bf16[384,768]{1,0:T(8,128)(2,1)S(1)}, bf16[384,768]{1,0:T(8,128)(2,1)S(1)}, u32[]{:S(2)}, u32[]{:S(2)}) collective-permute-start(bf16[384,768]{1,0:T(8,128)(2,1)S(1)} %get-tuple-element.131), channel_id=1, source_target_pairs={{0,66},{1,67},{2,64},{3,65},{4,70},{5,71},{6,68},{7,69},{8,74},{9,... | collective-permute-start | bytes 1769480 | tf_op jit(solution)/shard_map/ppermute | solution.py:42
  129.7 58.8 %collective-permute-start.50 = (bf16[384,768]{1,0:T(8,128)(2,1)S(1)}, bf16[384,768]{1,0:T(8,128)(2,1)S(1)}, u32[]{:S(2)}, u32[]{:S(2)}) collective-permute-start(bf16[384,768]{1,0:T(8,128)(2,1)S(1)} %collective-permute-done.47.refs_0_), channel_id=1, source_target_pairs={{0,32},{1,33},{2,34},{3,35},{4,36},{5,37},{6,38},{7,39},{8,40},{9,... | collective-permute-start | bytes 1769480 | tf_op jit(solution)/shard_map/ppermute | solution.py:42
  131.9 56.7 %collective-permute-start.49 = (bf16[384,768]{1,0:T(8,128)(2,1)S(1)}, bf16[384,768]{1,0:T(8,128)(2,1)S(1)}, u32[]{:S(2)}, u32[]{:S(2)}) collective-permute-start(bf16[384,768]{1,0:T(8,128)(2,1)S(1)} %collective-permute-done.47.refs_0_), channel_id=1, source_target_pairs={{0,48},{1,49},{2,50},{3,51},{4,52},{5,53},{6,54},{7,55},{8,56},{9,... | collective-permute-start | bytes 1769480 | tf_op jit(solution)/shard_map/ppermute | solution.py:42
  131.9 57.2 %collective-permute-start.48 = (bf16[384,768]{1,0:T(8,128)(2,1)S(1)}, bf16[384,768]{1,0:T(8,128)(2,1)S(1)}, u32[]{:S(2)}, u32[]{:S(2)}) collective-permute-start(bf16[384,768]{1,0:T(8,128)(2,1)S(1)} %collective-permute-done.47.refs_0_), channel_id=1, source_target_pairs={{0,16},{1,17},{2,18},{3,19},{4,20},{5,21},{6,22},{7,23},{8,24},{9,... | collective-permute-start | bytes 1769480 | tf_op jit(solution)/shard_map/ppermute | solution.py:42
  161.1 10.1 %collective-permute-start.35 = (bf16[2,1,2,16,384]{4,3,2,1,0:T(8,128)(2,1)S(1)}, bf16[2,1,2,16,384]{4,3,2,1,0:T(8,128)(2,1)S(1)}, u32[]{:S(2)}, u32[]{:S(2)}) collective-permute-start(bf16[2,1,2,16,384]{4,3,2,1,0:T(8,128)(2,1)S(1)} %pack.8.refs_0_), channel_id=1, source_target_pairs={{0,8},{1,9},{2,10},{3,11},{4,12},{5,13},{6,14},{7,15},{8,0},{9,1},... | collective-permute-start | bytes 147464 | tf_op jit(solution)/shard_map/ppermute | solution.py:42
  162.1 11.2 %collective-permute-start.37 = (bf16[4,32,384]{2,1,0:T(8,128)(2,1)S(1)}, bf16[4,32,384]{2,1,0:T(8,128)(2,1)S(1)}, u32[]{:S(2)}, u32[]{:S(2)}) collective-permute-start(bf16[4,32,384]{2,1,0:T(8,128)(2,1)S(1)} %pack.11), channel_id=1, source_target_pairs={{2,6},{3,7},{4,0},{5,1},{6,10},{7,11},{8,4},{9,5},{10,14},{11,15},... | collective-permute-start | bytes 294920 | tf_op jit(solution)/shard_map/ppermute | solution.py:42
  171.2 12.2 %collective-permute-start.36 = (bf16[4,32,384]{2,1,0:T(8,128)(2,1)S(1)}, bf16[4,32,384]{2,1,0:T(8,128)(2,1)S(1)}, u32[]{:S(2)}, u32[]{:S(2)}) collective-permute-start(bf16[4,32,384]{2,1,0:T(8,128)(2,1)S(1)} %pack.10), channel_id=1, source_target_pairs={{0,4},{1,5},{4,8},{5,9},{6,2},{7,3},{8,12},{9,13},{10,6},{11,7},{1... | collective-permute-start | bytes 294920 | tf_op jit(solution)/shard_map/ppermute | solution.py:42
  173.4 16.3 %collective-permute-start.38 = (bf16[8,1,2,16,384]{4,3,2,1,0:T(8,128)(2,1)S(1)}, bf16[8,1,2,16,384]{4,3,2,1,0:T(8,128)(2,1)S(1)}, u32[]{:S(2)}, u32[]{:S(2)}) collective-permute-start(bf16[8,1,2,16,384]{4,3,2,1,0:T(8,128)(2,1)S(1)} %pack.9.refs_7_), channel_id=1, source_target_pairs={{0,16},{1,17},{2,18},{3,19},{4,20},{5,21},{6,22},{7,23},{8,24},{9,... | collective-permute-start | bytes 589832 | tf_op jit(solution)/shard_map/ppermute | solution.py:42
  188.5 20.8 %collective-permute-start.54 = (bf16[384,768]{1,0:T(8,128)(2,1)S(1)}, bf16[384,768]{1,0:T(8,128)(2,1)S(1)}, u32[]{:S(2)}, u32[]{:S(2)}) collective-permute-start(bf16[384,768]{1,0:T(8,128)(2,1)S(1)} %collective-permute-done.50.refs_3_), channel_id=1, source_target_pairs={{0,1},{1,0},{2,3},{3,2},{4,5},{5,4},{6,7},{7,6},{8,9},{9,8},{10,11... | collective-permute-start | bytes 1769480 | tf_op jit(solution)/shard_map/ppermute | solution.py:42
  188.7 22.5 %collective-permute-start.53 = (bf16[384,768]{1,0:T(8,128)(2,1)S(1)}, bf16[384,768]{1,0:T(8,128)(2,1)S(1)}, u32[]{:S(2)}, u32[]{:S(2)}) collective-permute-start(bf16[384,768]{1,0:T(8,128)(2,1)S(1)} %collective-permute-done.49.refs_2_), channel_id=1, source_target_pairs={{0,1},{1,0},{2,3},{3,2},{4,5},{5,4},{6,7},{7,6},{8,9},{9,8},{10,11... | collective-permute-start | bytes 1769480 | tf_op jit(solution)/shard_map/ppermute | solution.py:42
  189.1 22.3 %collective-permute-start.52 = (bf16[384,768]{1,0:T(8,128)(2,1)S(1)}, bf16[384,768]{1,0:T(8,128)(2,1)S(1)}, u32[]{:S(2)}, u32[]{:S(2)}) collective-permute-start(bf16[384,768]{1,0:T(8,128)(2,1)S(1)} %collective-permute-done.48.refs_1_), channel_id=1, source_target_pairs={{0,1},{1,0},{2,3},{3,2},{4,5},{5,4},{6,7},{7,6},{8,9},{9,8},{10,11... | collective-permute-start | bytes 1769480 | tf_op jit(solution)/shard_map/ppermute | solution.py:42
  189.2 22.4 %collective-permute-start.51 = (bf16[384,768]{1,0:T(8,128)(2,1)S(1)}, bf16[384,768]{1,0:T(8,128)(2,1)S(1)}, u32[]{:S(2)}, u32[]{:S(2)}) collective-permute-start(bf16[384,768]{1,0:T(8,128)(2,1)S(1)} %collective-permute-done.47.refs_0_), channel_id=1, source_target_pairs={{0,1},{1,0},{2,3},{3,2},{4,5},{5,4},{6,7},{7,6},{8,9},{9,8},{10,11... | collective-permute-start | bytes 1769480 | tf_op jit(solution)/shard_map/ppermute | solution.py:42
  211.5 7.7 %collective-permute-start.42 = (bf16[128,384]{1,0:T(8,128)(2,1)S(1)}, bf16[128,384]{1,0:T(8,128)(2,1)S(1)}, u32[]{:S(2)}, u32[]{:S(2)}) collective-permute-start(bf16[128,384]{1,0:T(8,128)(2,1)S(1)} %get-tuple-element.123), channel_id=1, source_target_pairs={{0,2},{1,3},{2,0},{3,1},{4,6},{5,7},{6,4},{7,5},{8,10},{9,11},{10,... | collective-permute-start | bytes 294920 | tf_op jit(solution)/shard_map/ppermute | solution.py:42
  211.7 8.7 %collective-permute-start.43 = (bf16[128,384]{1,0:T(8,128)(2,1)S(1)}, bf16[128,384]{1,0:T(8,128)(2,1)S(1)}, u32[]{:S(2)}, u32[]{:S(2)}) collective-permute-start(bf16[128,384]{1,0:T(8,128)(2,1)S(1)} %get-tuple-element.124), channel_id=1, source_target_pairs={{0,3},{1,2},{2,1},{3,0},{4,7},{5,6},{6,5},{7,4},{8,11},{9,10},{10,... | collective-permute-start | bytes 294920 | tf_op jit(solution)/shard_map/ppermute | solution.py:42
  (35 other events, 296.0 us)
where the time goes:
time: 227 us; the launch traced here: 226 us
  waiting for transfers between devices  90.7 us (40%)
  Pallas kernels  65.6 us (29%)
  starting transfers between devices  60.5 us (27%)
  local copies, waits for them, and re-layouts  8.65 us (4%)
    ppermute x55, waiting for transfers between devices, send(): return lax.ppermute(value, AXES, pairs)  90.7 us
    ppermute x55, starting transfers between devices, send(): return lax.ppermute(value, AXES, pairs)  60.5 us
    pallas_call x4, Pallas kernels, qkv(): pl.pallas_call(functools.partial(qkv_kernel, l, which), out_shape=(shape(...  19.8 us
    pallas_call x1, Pallas kernels, first_qkv(): pl.pallas_call(first_kernel, out_shape=(shape(BLK, D),) + one + one + (sh...  16.4 us
    pallas_call x2, Pallas kernels, attend_pair(): pl.pallas_call(functools.partial(attend_pair_kernel, cl, at), out_shape=(...  10.2 us
    unnamed x24, local copies, waits for them, and re-layouts  8.65 us
    pallas_call x2, Pallas kernels, attend(): pl.pallas_call(functools.partial(attend_kernel, cl, which), out_shape=sha...  5.69 us
    pallas_call x1, Pallas kernels, final(): pl.pallas_call(final_kernel, out_shape=shape(BLK, D), in_specs=[SM] + [VM...  5.5 us
  transfers between devices with their start and end apart: 55, of which 20 were waited for; matrix products, arithmetic and copies ran while one was open for 0% of the time, Pallas kernels for 24%

commit v1 on v0

--- a/solution.py
+++ b/solution.py
@@ -142,7 +142,7 @@
     wz, wzs, out, sems = refs[:4], refs[4:8], refs[8], refs[9]
     copies = []
     for k in range(4):
-        cols = pl.ds(quarter(place()[2 + layer], k), QUART)
+        cols = pl.ds(quarter(place()[3 - layer], k), QUART)
         for j, src in enumerate(
             (wo.at[layer, :, cols], wsib.at[layer, :, cols], wz[k], wzs[k])
         ):
@@ -167,16 +167,19 @@
     )(wo, wsib, *wz, *wzs)
 
 
-def norm_rows(src, gain, dst, row0, rows):
+def norm_rows(pieces, gain, dst, unroll=1):
+    rows = pieces[0].shape[0]
+
     def step(i, carry):
         at = pl.ds(pl.multiple_of(i * 16, 16), 16)
-        to = pl.ds(pl.multiple_of(row0 + i * 16, 16), 16)
-        v = src[at, :].astype(F32)
-        ms = jnp.mean(v * v, axis=-1, keepdims=True)
-        dst[to, :] = (v * lax.rsqrt(ms + EPS) * gain[...]).astype(BF16)
+        for k, src in enumerate(pieces):
+            to = pl.ds(pl.multiple_of(k * rows + i * 16, 16), 16)
+            v = src[at, :].astype(F32)
+            ms = jnp.mean(v * v, axis=-1, keepdims=True)
+            dst[to, :] = (v * lax.rsqrt(ms + EPS) * gain[...]).astype(BF16)
         return carry
 
-    lax.fori_loop(0, rows // 16, step, 0)
+    lax.fori_loop(0, rows // 16, step, 0, unroll=unroll)
 
 
 def head_norm(p, gain):
@@ -284,10 +287,7 @@
 
 def qkv_kernel(l, which, *refs):
     pieces, (gain, w, qkg, out, outer, inner, normed) = refs[:-7], refs[-7:]
-    row = 0
-    for src in pieces:
-        norm_rows(src, gain.at[l : l + 1], normed, row, src.shape[0])
-        row += src.shape[0]
+    norm_rows(pieces, gain.at[l : l + 1], normed, 4 // len(pieces))
 
     def put(m, c, p):
         out[c] = p
@@ -432,7 +432,7 @@
     rows = 2 * CLIP_TOK
 
     def block(k, carry):
-        cols = pl.ds(quarter(place()[2], k), QUART)
+        cols = pl.ds(quarter(place()[3], k), QUART)
         row = 0
         for x in xs:
             if row % CLIP_TOK == 0:
@@ -447,7 +447,7 @@
 
     lax.fori_loop(0, 4, block, 0)
     first[...] = xbuf[:BLK, :]
-    norm_rows(xbuf, gain.at[1:2], normed, 0, rows)
+    norm_rows([xbuf], gain.at[1:2], normed, 2)
 
     def put(m, c, p):
         @pl.when(m == 0)
@@ -515,7 +515,7 @@
     skip_first = skip[place()[1]] == 0
 
     def block(k, carry):
-        cols = pl.ds(quarter(place()[3], k), QUART)
+        cols = pl.ds(quarter(place()[2], k), QUART)
         t = jnp.dot(acat[...], wslot[k], preferred_element_type=F32)
         f = first[:, cols].astype(F32)
         strong = (f + t[:BLK]).astype(BF16).astype(F32)
@@ -552,7 +552,7 @@
     outs, sems = refs[:2], refs[2]
     copies = []
     for l in range(2):
-        cols = pl.ds(pl.multiple_of(place()[2 + l] * QUART, QUART), QUART)
+        cols = pl.ds(pl.multiple_of(place()[3 - l] * QUART, QUART), QUART)
         copies.append(
             pltpu.make_async_copy(wo.at[l, :, cols], outs[l], sems.at[l])
         )
@@ -580,21 +580,22 @@
 
 def body(video, norm_gain, w_qkv, qk_gain, w_out, skip_layer, halo_frames, context_index):
     x0 = video
-    piece0, piece1 = columns(w_out)
+    piece0, piece1 = columns(pltpu.with_memory_space_constraint(w_out, pltpu.HBM))
     here0 = send(piece0, to_far_z)
     c0, xa, xb = context_rows(context_index, after(x0, piece0))
     c = [c0, send(c0, to_sib), send(c0, to_z), send(c0, to_diag)]
     x2a = send(xa, to_z)
     x1 = send(after(x0, c0), to_sib)
-    w = stage(jnp.transpose(w_qkv, (0, 2, 1, 3)))
+    w = stage(pltpu.with_memory_space_constraint(jnp.transpose(w_qkv, (0, 2, 1, 3)), pltpu.HBM))
     kv = context_kv(c, norm_gain, w, qk_gain)
     kz = send(kv, to_far)
     x2b = send(after(xb, kv), to_z)
+    wz0 = [here0] + [send(after(here0, kv), to_y(d)) for d in (1, 3)]
     own0 = qkv(0, 0, (after(x0, kv), x1), norm_gain, w, qk_gain)
     kx = pack(kv, after(kz, own0[0]))
     kxs = [send(kx, to_x(d)) for d in (1, 3, 2)]
-    wz0 = [here0] + [send(after(here0, kx), to_x(d)) for d in (1, 3, 2)]
     x3a = send(after(x2a, kx), to_sib)
+    here1 = send(after(piece1, kx), to_far_z)
     own1 = qkv(1, 0, (after(x0, kx), x1), norm_gain, w, qk_gain)
     ky = pack(kx, *[after(k, own1[0]) for k in kxs])
     kys = [send(ky, to_y(d)) for d in (1, 3, 2)]
@@ -603,7 +604,8 @@
     par0 = qkv(0, 1, halves, norm_gain, w, qk_gain)
     eo, ep = edges(own0, par0)
     wsib = send(after(w_out, par0[0]), to_sib)
-    here1 = send(after(piece1, par0[0]), to_far_z)
+    wz0.append(send(after(here0, par0[0]), to_y(2)))
+    wz1 = [here1] + [send(after(here1, eo, ep), to_x(d)) for d in (1, 3, 2)]
     ctx = [ky] + kys
     ao = attend(0, 0, halo_frames, own0[0], par0[2], eo, ctx)
     oz = send(ao, to_z)
@@ -614,7 +616,6 @@
     halves = (after(x2a, ap), x2b, x3a, x3b)
     par1 = qkv(1, 1, halves, norm_gain, w, qk_gain)
     wzs0 = [send(after(p, ap), to_sib) for p in wz0]
-    wz1 = [here1] + [send(after(here1, par1[0]), to_y(d)) for d in (1, 3, 2)]
     ozs = send(after(oz, par1[0]), to_sib)
     wslot0 = assemble(0, after(w_out, par1[0]), wsib, wz0, wzs0)
     pzs = send(pz, to_sib)

time: 227 us -> 220 us (0.969)
  waiting for transfers between devices: 90.7 us -> 103 us
  starting transfers between devices: 60.5 us -> 53.8 us
  Pallas kernels: 65.6 us -> 59 us
  local copies, waits for them, and re-layouts: 8.65 us -> 2.43 us
    ppermute x55, waiting for transfers between devices: 90.7 us -> 103 us  [send(): return lax.ppermute(value, AXES, pairs)]
    pallas_call x4, Pallas kernels: 19.8 us -> 12.4 us  [qkv(): pl.pallas_call(functools.partial(qkv_kernel, l, which), out_shape=(shape(...]
    ppermute x55, starting transfers between devices: 60.5 us -> 53.8 us  [send(): return lax.ppermute(value, AXES, pairs)]
    unnamed x24, local copies, waits for them, and re-layouts: 8.65 us -> 2.43 us
    pallas_call x1, Pallas kernels: 1.48 us -> 5.17 us  [stage(): pl.pallas_call(stage_kernel, out_shape=pltpu.VMEM((2, D, 3 * INNER), BF16...]
    pallas_call x1, Pallas kernels: 16.4 us -> 13.5 us  [first_qkv(): pl.pallas_call(first_kernel, out_shape=(shape(BLK, D),) + one + one + (sh...]
  transfers between devices with their start and end apart: 55 -> 55, of which waited for: 20 -> 20; matrix products, arithmetic and copies ran while one was open for 0% -> 0% of each run, Pallas kernels for 24% -> 22%
where the time goes in v1:
time: 220 us; the launch traced here: 219 us
  waiting for transfers between devices  103 us (47%)
  Pallas kernels  59 us (27%)
  starting transfers between devices  53.8 us (24%)
  local copies, waits for them, and re-layouts  2.43 us (1%)
    ppermute x55, waiting for transfers between devices, send(): return lax.ppermute(value, AXES, pairs)  103 us
    ppermute x55, starting transfers between devices, send(): return lax.ppermute(value, AXES, pairs)  53.8 us
    pallas_call x1, Pallas kernels, first_qkv(): pl.pallas_call(first_kernel, out_shape=(shape(BLK, D),) + one + one + (sh...  13.5 us
    pallas_call x4, Pallas kernels, qkv(): pl.pallas_call(functools.partial(qkv_kernel, l, which), out_shape=(shape(...  12.4 us
    pallas_call x2, Pallas kernels, attend_pair(): pl.pallas_call(functools.partial(attend_pair_kernel, cl, at), out_shape=(...  10.2 us
    pallas_call x2, Pallas kernels, attend(): pl.pallas_call(functools.partial(attend_kernel, cl, which), out_shape=sha...  5.68 us
    pallas_call x1, Pallas kernels, stage(): pl.pallas_call(stage_kernel, out_shape=pltpu.VMEM((2, D, 3 * INNER), BF16...  5.17 us
    pallas_call x1, Pallas kernels, final(): pl.pallas_call(final_kernel, out_shape=shape(BLK, D), in_specs=[SM] + [VM...  4.9 us
  transfers between devices with their start and end apart: 55, of which 20 were waited for; matrix products, arithmetic and copies ran while one was open for 0% of the time, Pallas kernels for 22%

profile of v1, /device:TPU:64, one launch (start us, length us, event | category | flops | bytes accessed | tf_op | source)
XLA Modules:
  0.0 219.1 jit_solution(17085357184016159698)
XLA Ops:
  6.1 5.2 %stage.1.w.refs_3_.refs_5_.refs_16_ = bf16[2,3072,1152]{2,1,0:T(8,128)(2,1)S(1)} custom-call(bf16[2,3,3072,384]{3,2,1,0:T(8,128)(2,1)} %bitcast.3), custom_call_target="tpu_custom_call" | custom-call | tf_op jit(solution)/shard_map/stage/pallas_call | solution.py:130
  15.2 3.1 %qkv.4 = (bf16[3,256,384]{2,1,0:T(8,128)(2,1)S(1)}, bf16[2,32,384]{2,1,0:T(8,128)(2,1)S(1)}, bf16[2,32,384]{2,1,0:T(8,128)(2,1)S(1)}) custom-call(bf16[128,3072]{1,0:T(8,128)(2,1)S(1)} %copy-done.3, bf16[128,3072]{1,0:T(8,128)(2,1)S(1)} %collective-permute-done.3.refs_1_.refs_9_, f32[2,3072]{1,0:T(2,128)S(1)} %copy-done.4, ...), custom_call_target="tpu_custom_call" | custom-call | flops 1811939328 | bytes 8650752 | tf_op jit(solution)/shard_map/qkv/pallas_call | solution.py:300
  18.3 15.4 %collective-permute-done.5.refs_1_ = bf16[1,2,2,16,384]{4,3,2,1,0:T(8,128)(2,1)S(1)} collective-permute-done((bf16[1,2,2,16,384]{4,3,2,1,0:T(8,128)(2,1)S(1)}, bf16[1,2,2,16,384]{4,3,2,1,0:T(8,128)(2,1)S(1)}, u32[]{:S(2)}, u32[]{:S(2)}) %collective-permute-start.5) | collective-permute-done | bytes 49184 | tf_op jit(solution)/shard_map/ppermute | solution.py:42
  33.7 3.1 %qkv.5 = (bf16[3,256,384]{2,1,0:T(8,128)(2,1)S(1)}, bf16[2,32,384]{2,1,0:T(8,128)(2,1)S(1)}, bf16[2,32,384]{2,1,0:T(8,128)(2,1)S(1)}) custom-call(bf16[128,3072]{1,0:T(8,128)(2,1)S(1)} %copy-done.3, bf16[128,3072]{1,0:T(8,128)(2,1)S(1)} %collective-permute-done.3.refs_1_.refs_9_, f32[2,3072]{1,0:T(2,128)S(1)} %copy-done.4, ...), custom_call_target="tpu_custom_call" | custom-call | flops 1811939328 | bytes 8650752 | tf_op jit(solution)/shard_map/qkv/pallas_call | solution.py:300
  37.4 3.0 %collective-permute-start.8 = (bf16[2,2,2,16,384]{4,3,2,1,0:T(8,128)(2,1)S(1)}, bf16[2,2,2,16,384]{4,3,2,1,0:T(8,128)(2,1)S(1)}, u32[]{:S(2)}, u32[]{:S(2)}) collective-permute-start(bf16[2,2,2,16,384]{4,3,2,1,0:T(8,128)(2,1)S(1)} %pack.6.refs_0_), channel_id=1, source_target_pairs={{0,8},{1,9},{2,10},{3,11},{4,12},{5,13},{6,14},{7,15},{8,0},{9,1},... | collective-permute-start | bytes 294920 | tf_op jit(solution)/shard_map/ppermute | solution.py:42
  44.0 2.0 collective-permute-done.7.refs_2_
  47.5 3.1 %qkv.6 = (bf16[3,256,384]{2,1,0:T(8,128)(2,1)S(1)}, bf16[2,32,384]{2,1,0:T(8,128)(2,1)S(1)}, bf16[2,32,384]{2,1,0:T(8,128)(2,1)S(1)}) custom-call(bf16[64,3072]{1,0:T(8,128)(2,1)S(1)} %collective-permute-done.4.refs_0_.refs_10_, bf16[64,3072]{1,0:T(8,128)(2,1)S(1)} %collective-permute-done.9.refs_1_.refs_11_, ...), custom_call_target="tpu_custom_call" | custom-call | flops 1811939328 | bytes 8650752 | tf_op jit(solution)/shard_map/qkv/pallas_call | solution.py:300
  50.7 2.0 collective-permute-start.24
  56.0 2.0 collective-permute-start.15
  58.0 8.7 %collective-permute-done.24.refs_0_ = bf16[384,768]{1,0:T(8,128)(2,1)S(1)} collective-permute-done((bf16[384,768]{1,0:T(8,128)(2,1)S(1)}, bf16[384,768]{1,0:T(8,128)(2,1)S(1)}, u32[]{:S(2)}, u32[]{:S(2)}) %collective-permute-start.24) | collective-permute-done | bytes 589856 | tf_op jit(solution)/shard_map/ppermute | solution.py:42
  66.6 9.6 %collective-permute-start.16 = (bf16[2,32,384]{2,1,0:T(8,128)(2,1)S(1)}, bf16[2,32,384]{2,1,0:T(8,128)(2,1)S(1)}, u32[]{:S(2)}, u32[]{:S(2)}) collective-permute-start(bf16[2,32,384]{2,1,0:T(8,128)(2,1)S(1)} %get-tuple-element.95), channel_id=1, source_target_pairs={{2,6},{3,7},{4,0},{5,1},{6,10},{7,11},{8,4},{9,5},{10,14},{11,15},... | collective-permute-start | bytes 147464 | tf_op jit(solution)/shard_map/ppermute | solution.py:42
  79.9 10.3 %collective-permute-done.12.outer = bf16[2,32,384]{2,1,0:T(8,128)(2,1)S(1)} collective-permute-done((bf16[2,32,384]{2,1,0:T(8,128)(2,1)S(1)}, bf16[2,32,384]{2,1,0:T(8,128)(2,1)S(1)}, u32[]{:S(2)}, u32[]{:S(2)}) %collective-permute-start.12) | collective-permute-done | bytes 49184 | tf_op jit(solution)/shard_map/ppermute | solution.py:42
  90.1 2.0 collective-permute-start.25
  92.3 2.8 %attend.2.refs_0_ = bf16[2,128,384]{2,1,0:T(8,128)(2,1)S(1)} custom-call(s32[2]{0:T(128)S(1)} %copy-done.6, bf16[3,256,384]{2,1,0:T(8,128)(2,1)S(1)} %get-tuple-element.77.mine, bf16[2,32,384]{2,1,0:T(8,128)(2,1)S(1)} %get-tuple-element.90.inner, bf16[2,32,384]{2,1,0:T(8,128)(2,1)S(1)} %collective-permute-done.12.outer, ...), custom_call_target="tpu_custom_call" | custom-call | flops 490733568 | bytes 1671168 | tf_op jit(solution)/shard_map/attend/pallas_call | solution.py:383
  95.1 11.2 %collective-permute-done.26.refs_2_ = bf16[384,768]{1,0:T(8,128)(2,1)S(1)} collective-permute-done((bf16[384,768]{1,0:T(8,128)(2,1)S(1)}, bf16[384,768]{1,0:T(8,128)(2,1)S(1)}, u32[]{:S(2)}, u32[]{:S(2)}) %collective-permute-start.26) | collective-permute-done | bytes 589856 | tf_op jit(solution)/shard_map/ppermute | solution.py:42
  106.3 2.8 %attend.3.refs_1_ = bf16[2,128,384]{2,1,0:T(8,128)(2,1)S(1)} custom-call(s32[2]{0:T(128)S(1)} %copy-done.6, bf16[3,256,384]{2,1,0:T(8,128)(2,1)S(1)} %get-tuple-element.93.mine, bf16[2,32,384]{2,1,0:T(8,128)(2,1)S(1)} %get-tuple-element.94.inner, bf16[2,32,384]{2,1,0:T(8,128)(2,1)S(1)} %collective-permute-done.16.outer, ...), custom_call_target="tpu_custom_call" | custom-call | flops 490733568 | bytes 1671168 | tf_op jit(solution)/shard_map/attend/pallas_call | solution.py:383
  109.2 7.4 %collective-permute-done.25.refs_1_ = bf16[384,768]{1,0:T(8,128)(2,1)S(1)} collective-permute-done((bf16[384,768]{1,0:T(8,128)(2,1)S(1)}, bf16[384,768]{1,0:T(8,128)(2,1)S(1)}, u32[]{:S(2)}, u32[]{:S(2)}) %collective-permute-start.25) | collective-permute-done | bytes 589856 | tf_op jit(solution)/shard_map/ppermute | solution.py:42
  117.2 5.0 %collective-permute-done.20.refs_5_ = bf16[2,128,384]{2,1,0:T(8,128)(2,1)S(1)} collective-permute-done((bf16[2,128,384]{2,1,0:T(8,128)(2,1)S(1)}, bf16[2,128,384]{2,1,0:T(8,128)(2,1)S(1)}, u32[]{:S(2)}, u32[]{:S(2)}) %collective-permute-start.20) | collective-permute-done | bytes 196640 | tf_op jit(solution)/shard_map/ppermute | solution.py:42
  122.3 3.1 %qkv.7 = (bf16[3,256,384]{2,1,0:T(8,128)(2,1)S(1)}, bf16[2,32,384]{2,1,0:T(8,128)(2,1)S(1)}, bf16[2,32,384]{2,1,0:T(8,128)(2,1)S(1)}) custom-call(bf16[64,3072]{1,0:T(8,128)(2,1)S(1)} %collective-permute-done.4.refs_0_.refs_10_, bf16[64,3072]{1,0:T(8,128)(2,1)S(1)} %collective-permute-done.9.refs_1_.refs_11_, ...), custom_call_target="tpu_custom_call" | custom-call | flops 1811939328 | bytes 8650752 | tf_op jit(solution)/shard_map/qkv/pallas_call | solution.py:300
  128.8 2.0 collective-permute-start.48
  130.9 13.5 %first_qkv.1 = (bf16[128,3072]{1,0:T(8,128)(2,1)S(1)}, bf16[3,256,384]{2,1,0:T(8,128)(2,1)S(1)}, bf16[2,32,384]{2,1,0:T(8,128)(2,1)S(1)}, bf16[2,32,384]{2,1,0:T...) custom-call(bf16[2,128,384]{2,1,0:T(8,128)(2,1)S(1)} %attend.2.refs_, ...), custom_call_target="tpu_custom_call" | custom-call | flops 8455716864 | bytes 22806528 | tf_op jit(solution)/shard_map/first_qkv/pallas_call | solution.py:488
  146.1 3.7 %collective-permute-done.32.refs_1_ = bf16[1,1,2,16,384]{4,3,2,1,0:T(8,128)(2,1)S(1)} collective-permute-done((bf16[1,1,2,16,384]{4,3,2,1,0:T(8,128)(2,1)S(1)}, bf16[1,1,2,16,384]{4,3,2,1,0:T(8,128)(2,1)S(1)}, u32[]{:S(2)}, u32[]{:S(2)}) %collective-permute-start.32) | collective-permute-done | bytes 24608 | tf_op jit(solution)/shard_map/ppermute | solution.py:42
  151.1 2.0 collective-permute-start.34
  153.1 4.4 %collective-permute-done.33.refs_1_ = bf16[2,1,2,16,384]{4,3,2,1,0:T(8,128)(2,1)S(1)} collective-permute-done((bf16[2,1,2,16,384]{4,3,2,1,0:T(8,128)(2,1)S(1)}, bf16[2,1,2,16,384]{4,3,2,1,0:T(8,128)(2,1)S(1)}, u32[]{:S(2)}, u32[]{:S(2)}) %collective-permute-start.33) | collective-permute-done | bytes 49184 | tf_op jit(solution)/shard_map/ppermute | solution.py:42
  157.8 7.2 %collective-permute-start.37 = (bf16[4,32,384]{2,1,0:T(8,128)(2,1)S(1)}, bf16[4,32,384]{2,1,0:T(8,128)(2,1)S(1)}, u32[]{:S(2)}, u32[]{:S(2)}) collective-permute-start(bf16[4,32,384]{2,1,0:T(8,128)(2,1)S(1)} %pack.11), channel_id=1, source_target_pairs={{2,6},{3,7},{4,0},{5,1},{6,10},{7,11},{8,4},{9,5},{10,14},{11,15},... | collective-permute-start | bytes 294920 | tf_op jit(solution)/shard_map/ppermute | solution.py:42
  167.2 10.0 %collective-permute-done.36.refs_3_ = bf16[4,32,384]{2,1,0:T(8,128)(2,1)S(1)} collective-permute-done((bf16[4,32,384]{2,1,0:T(8,128)(2,1)S(1)}, bf16[4,32,384]{2,1,0:T(8,128)(2,1)S(1)}, u32[]{:S(2)}, u32[]{:S(2)}) %collective-permute-start.36) | collective-permute-done | bytes 98336 | tf_op jit(solution)/shard_map/ppermute | solution.py:42
  177.2 5.1 %attend_pair.2 = (bf16[128,384]{1,0:T(8,128)(2,1)S(1)}, bf16[128,384]{1,0:T(8,128)(2,1)S(1)}, bf16[128,384]{1,0:T(8,128)(2,1)S(1)}, bf16[128,384]{1,0:T(8,128)(2,1)S(1)}) custom-call(s32[2]{0:T(128)S(1)} %copy-done.6, bf16[3,256,384]{2,1,0:T(8,128)(2,1)S(1)} %get-tuple-element.109.refs_1_, bf16[2,32,384]{2,1,0:T(8,128)(2,1)S(1)} %get-tuple-element.110.refs_2_, ...), custom_call_target="tpu_custom_call" | custom-call | flops 981467136 | bytes 2064384 | tf_op jit(solution)/shard_map/attend_pair/pallas_call | solution.py:410
  183.5 6.9 %collective-permute-done.39.refs_9_ = bf16[8,1,2,16,384]{4,3,2,1,0:T(8,128)(2,1)S(1)} collective-permute-done((bf16[8,1,2,16,384]{4,3,2,1,0:T(8,128)(2,1)S(1)}, bf16[8,1,2,16,384]{4,3,2,1,0:T(8,128)(2,1)S(1)}, u32[]{:S(2)}, u32[]{:S(2)}) %collective-permute-start.39) | collective-permute-done | bytes 196640 | tf_op jit(solution)/shard_map/ppermute | solution.py:42
  190.4 7.6 %collective-permute-done.40.refs_10_ = bf16[8,1,2,16,384]{4,3,2,1,0:T(8,128)(2,1)S(1)} collective-permute-done((bf16[8,1,2,16,384]{4,3,2,1,0:T(8,128)(2,1)S(1)}, bf16[8,1,2,16,384]{4,3,2,1,0:T(8,128)(2,1)S(1)}, u32[]{:S(2)}, u32[]{:S(2)}) %collective-permute-start.40) | collective-permute-done | bytes 196640 | tf_op jit(solution)/shard_map/ppermute | solution.py:42
  198.0 5.1 %attend_pair.3 = (bf16[128,384]{1,0:T(8,128)(2,1)S(1)}, bf16[128,384]{1,0:T(8,128)(2,1)S(1)}, bf16[128,384]{1,0:T(8,128)(2,1)S(1)}, bf16[128,384]{1,0:T(8,128)(2,1)S(1)}) custom-call(s32[2]{0:T(128)S(1)} %copy-done.6, bf16[3,256,384]{2,1,0:T(8,128)(2,1)S(1)} %get-tuple-element.119.refs_1_, bf16[2,32,384]{2,1,0:T(8,128)(2,1)S(1)} %get-tuple-element.120.refs_2_, ...), custom_call_target="tpu_custom_call" | custom-call | flops 981467136 | bytes 2064384 | tf_op jit(solution)/shard_map/attend_pair/pallas_call | solution.py:410
  210.0 3.0 %collective-permute-done.42.refs_3_ = bf16[128,384]{1,0:T(8,128)(2,1)S(1)} collective-permute-done((bf16[128,384]{1,0:T(8,128)(2,1)S(1)}, bf16[128,384]{1,0:T(8,128)(2,1)S(1)}, u32[]{:S(2)}, u32[]{:S(2)}) %collective-permute-start.42) | collective-permute-done | bytes 98336 | tf_op jit(solution)/shard_map/ppermute | solution.py:42
  214.2 4.9 %final.1 = bf16[128,3072]{1,0:T(8,128)(2,1)} custom-call(s32[2]{0:T(128)S(1)} %copy-done.9, bf16[128,384]{1,0:T(8,128)(2,1)S(1)} %get-tuple-element.123.refs_1_, bf16[128,384]{1,0:T(8,128)(2,1)S(1)} %collective-permute-done.41.refs_2_, bf16[128,384]{1,0:T(8,128)(2,1)S(1)} %collective-permute-done.42.refs_3_, ...), custom_call_target="tpu_custom_call" | custom-call | flops 2415919104 | bytes 11796480 | tf_op jit(solution)/shard_map/final/pallas_call | solution.py:531
  (125 shorter events, 41.3 us)
Async XLA Ops:
  3.9 11.3 %collective-permute-start.3 = (bf16[128,3072]{1,0:T(8,128)(2,1)S(1)}, bf16[128,3072]{1,0:T(8,128)(2,1)S(1)}, u32[]{:S(2)}, u32[]{:S(2)}) collective-permute-start(bf16[128,3072]{1,0:T(8,128)(2,1)S(1)} %copy-done.2), channel_id=1, source_target_pairs={{0,1},{1,0},{2,3},{3,2},{4,5},{5,4},{6,7},{7,6},{8,9},{9,8},{10,11... | collective-permute-start | bytes 2359304 | tf_op jit(solution)/shard_map/ppermute | solution.py:42
  13.1 23.7 %collective-permute-start.9 = (bf16[64,3072]{1,0:T(8,128)(2,1)S(1)}, bf16[64,3072]{1,0:T(8,128)(2,1)S(1)}, u32[]{:S(2)}, u32[]{:S(2)}) collective-permute-start(bf16[64,3072]{1,0:T(8,128)(2,1)S(1)} %get-tuple-element.87), channel_id=1, source_target_pairs={{0,2},{1,3},{2,0},{3,1},{4,6},{5,7},{6,4},{7,5},{8,10},{9,11},{10,... | collective-permute-start | bytes 1179656 | tf_op jit(solution)/shard_map/ppermute | solution.py:42
  14.6 22.4 %collective-permute-start.4 = (bf16[64,3072]{1,0:T(8,128)(2,1)S(1)}, bf16[64,3072]{1,0:T(8,128)(2,1)S(1)}, u32[]{:S(2)}, u32[]{:S(2)}) collective-permute-start(bf16[64,3072]{1,0:T(8,128)(2,1)S(1)} %get-tuple-element.78), channel_id=1, source_target_pairs={{0,2},{1,3},{2,0},{3,1},{4,6},{5,7},{6,4},{7,5},{8,10},{9,11},{10,... | collective-permute-start | bytes 1179656 | tf_op jit(solution)/shard_map/ppermute | solution.py:42
  15.1 18.5 %collective-permute-start.5 = (bf16[1,2,2,16,384]{4,3,2,1,0:T(8,128)(2,1)S(1)}, bf16[1,2,2,16,384]{4,3,2,1,0:T(8,128)(2,1)S(1)}, u32[]{:S(2)}, u32[]{:S(2)}) collective-permute-start(bf16[1,2,2,16,384]{4,3,2,1,0:T(8,128)(2,1)S(1)} %context_kv.1.refs_0_), channel_id=1, source_target_pairs={{0,64},{1,65},{2,66},{3,67},{4,68},{5,69},{6,70},{7,71},{8,72},{9,... | collective-permute-start | bytes 147464 | tf_op jit(solution)/shard_map/ppermute | solution.py:42
  36.8 10.6 %collective-permute-start.11 = (bf16[64,3072]{1,0:T(8,128)(2,1)S(1)}, bf16[64,3072]{1,0:T(8,128)(2,1)S(1)}, u32[]{:S(2)}, u32[]{:S(2)}) collective-permute-start(bf16[64,3072]{1,0:T(8,128)(2,1)S(1)} %collective-permute-done.9.refs_1_.refs_11_), channel_id=1, source_target_pairs={{0,1},{1,0},{2,3},{3,2},{4,5},{5,4},{6,7},{7,6},{8,9},{9,8},{10,11... | collective-permute-start | bytes 1179656 | tf_op jit(solution)/shard_map/ppermute | solution.py:42
  36.9 10.5 %collective-permute-start.10 = (bf16[64,3072]{1,0:T(8,128)(2,1)S(1)}, bf16[64,3072]{1,0:T(8,128)(2,1)S(1)}, u32[]{:S(2)}, u32[]{:S(2)}) collective-permute-start(bf16[64,3072]{1,0:T(8,128)(2,1)S(1)} %collective-permute-done.4.refs_0_.refs_10_), channel_id=1, source_target_pairs={{0,1},{1,0},{2,3},{3,2},{4,5},{5,4},{6,7},{7,6},{8,9},{9,8},{10,11... | collective-permute-start | bytes 1179656 | tf_op jit(solution)/shard_map/ppermute | solution.py:42
  50.6 76.0 %collective-permute-start.23 = (bf16[2,384,3072]{2,1,0:T(8,128)(2,1)S(1)}, bf16[2,384,3072]{2,1,0:T(8,128)(2,1)S(1)}, u32[]{:S(2)}, u32[]{:S(2)}) collective-permute-start(bf16[2,384,3072]{2,1,0:T(8,128)(2,1)S(1)} %bitcast.2), channel_id=1, source_target_pairs={{0,1},{1,0},{2,3},{3,2},{4,5},{5,4},{6,7},{7,6},{8,9},{9,8},{10,11... | collective-permute-start | bytes 14155784 | tf_op jit(solution)/shard_map/ppermute | solution.py:42
  50.7 15.9 %collective-permute-start.24 = (bf16[384,768]{1,0:T(8,128)(2,1)S(1)}, bf16[384,768]{1,0:T(8,128)(2,1)S(1)}, u32[]{:S(2)}, u32[]{:S(2)}) collective-permute-start(bf16[384,768]{1,0:T(8,128)(2,1)S(1)} %get-tuple-element.72), channel_id=1, source_target_pairs={{0,66},{1,67},{2,64},{3,65},{4,70},{5,71},{6,68},{7,69},{8,74},{9,... | collective-permute-start | bytes 1769480 | tf_op jit(solution)/shard_map/ppermute | solution.py:42
  52.7 37.4 %collective-permute-start.13 = (bf16[8,2,2,16,384]{4,3,2,1,0:T(8,128)(2,1)S(1)}, bf16[8,2,2,16,384]{4,3,2,1,0:T(8,128)(2,1)S(1)}, u32[]{:S(2)}, u32[]{:S(2)}) collective-permute-start(bf16[8,2,2,16,384]{4,3,2,1,0:T(8,128)(2,1)S(1)} %pack.7.c0.refs_7_), channel_id=1, source_target_pairs={{0,16},{1,17},{2,18},{3,19},{4,20},{5,21},{6,22},{7,23},{8,24},{9,... | collective-permute-start | bytes 1179656 | tf_op jit(solution)/shard_map/ppermute | solution.py:42
  54.3 37.9 %collective-permute-start.14 = (bf16[8,2,2,16,384]{4,3,2,1,0:T(8,128)(2,1)S(1)}, bf16[8,2,2,16,384]{4,3,2,1,0:T(8,128)(2,1)S(1)}, u32[]{:S(2)}, u32[]{:S(2)}) collective-permute-start(bf16[8,2,2,16,384]{4,3,2,1,0:T(8,128)(2,1)S(1)} %pack.7.c0.refs_7_), channel_id=1, source_target_pairs={{0,48},{1,49},{2,50},{3,51},{4,52},{5,53},{6,54},{7,55},{8,56},{9,... | collective-permute-start | bytes 1179656 | tf_op jit(solution)/shard_map/ppermute | solution.py:42
  56.0 36.2 %collective-permute-start.15 = (bf16[8,2,2,16,384]{4,3,2,1,0:T(8,128)(2,1)S(1)}, bf16[8,2,2,16,384]{4,3,2,1,0:T(8,128)(2,1)S(1)}, u32[]{:S(2)}, u32[]{:S(2)}) collective-permute-start(bf16[8,2,2,16,384]{4,3,2,1,0:T(8,128)(2,1)S(1)} %pack.7.c0.refs_7_), channel_id=1, source_target_pairs={{0,32},{1,33},{2,34},{3,35},{4,36},{5,37},{6,38},{7,39},{8,40},{9,... | collective-permute-start | bytes 1179656 | tf_op jit(solution)/shard_map/ppermute | solution.py:42
  66.6 11.3 %collective-permute-start.16 = (bf16[2,32,384]{2,1,0:T(8,128)(2,1)S(1)}, bf16[2,32,384]{2,1,0:T(8,128)(2,1)S(1)}, u32[]{:S(2)}, u32[]{:S(2)}) collective-permute-start(bf16[2,32,384]{2,1,0:T(8,128)(2,1)S(1)} %get-tuple-element.95), channel_id=1, source_target_pairs={{2,6},{3,7},{4,0},{5,1},{6,10},{7,11},{8,4},{9,5},{10,14},{11,15},... | collective-permute-start | bytes 147464 | tf_op jit(solution)/shard_map/ppermute | solution.py:42
  78.0 12.2 %collective-permute-start.12 = (bf16[2,32,384]{2,1,0:T(8,128)(2,1)S(1)}, bf16[2,32,384]{2,1,0:T(8,128)(2,1)S(1)}, u32[]{:S(2)}, u32[]{:S(2)}) collective-permute-start(bf16[2,32,384]{2,1,0:T(8,128)(2,1)S(1)} %get-tuple-element.91), channel_id=1, source_target_pairs={{0,4},{1,5},{4,8},{5,9},{6,2},{7,3},{8,12},{9,13},{10,6},{11,7},{1... | collective-permute-start | bytes 147464 | tf_op jit(solution)/shard_map/ppermute | solution.py:42
  90.1 16.2 %collective-permute-start.26 = (bf16[384,768]{1,0:T(8,128)(2,1)S(1)}, bf16[384,768]{1,0:T(8,128)(2,1)S(1)}, u32[]{:S(2)}, u32[]{:S(2)}) collective-permute-start(bf16[384,768]{1,0:T(8,128)(2,1)S(1)} %collective-permute-done.24.refs_0_), channel_id=1, source_target_pairs={{0,48},{1,49},{2,50},{3,51},{4,52},{5,53},{6,54},{7,55},{8,56},{9,... | collective-permute-start | bytes 1769480 | tf_op jit(solution)/shard_map/ppermute | solution.py:42
  90.1 26.5 %collective-permute-start.25 = (bf16[384,768]{1,0:T(8,128)(2,1)S(1)}, bf16[384,768]{1,0:T(8,128)(2,1)S(1)}, u32[]{:S(2)}, u32[]{:S(2)}) collective-permute-start(bf16[384,768]{1,0:T(8,128)(2,1)S(1)} %collective-permute-done.24.refs_0_), channel_id=1, source_target_pairs={{0,16},{1,17},{2,18},{3,19},{4,20},{5,21},{6,22},{7,23},{8,24},{9,... | collective-permute-start | bytes 1769480 | tf_op jit(solution)/shard_map/ppermute | solution.py:42
  92.2 24.5 %collective-permute-start.27 = (bf16[384,768]{1,0:T(8,128)(2,1)S(1)}, bf16[384,768]{1,0:T(8,128)(2,1)S(1)}, u32[]{:S(2)}, u32[]{:S(2)}) collective-permute-start(bf16[384,768]{1,0:T(8,128)(2,1)S(1)} %collective-permute-done.24.refs_0_), channel_id=1, source_target_pairs={{0,32},{1,33},{2,34},{3,35},{4,36},{5,37},{6,38},{7,39},{8,40},{9,... | collective-permute-start | bytes 1769480 | tf_op jit(solution)/shard_map/ppermute | solution.py:42
  92.2 24.5 %collective-permute-start.47 = (bf16[384,768]{1,0:T(8,128)(2,1)S(1)}, bf16[384,768]{1,0:T(8,128)(2,1)S(1)}, u32[]{:S(2)}, u32[]{:S(2)}) collective-permute-start(bf16[384,768]{1,0:T(8,128)(2,1)S(1)} %get-tuple-element.133), channel_id=1, source_target_pairs={{0,66},{1,67},{2,64},{3,65},{4,70},{5,71},{6,68},{7,69},{8,74},{9,... | collective-permute-start | bytes 1769480 | tf_op jit(solution)/shard_map/ppermute | solution.py:42
  106.3 10.8 %collective-permute-start.19 = (bf16[2,128,384]{2,1,0:T(8,128)(2,1)S(1)}, bf16[2,128,384]{2,1,0:T(8,128)(2,1)S(1)}, u32[]{:S(2)}, u32[]{:S(2)}) collective-permute-start(bf16[2,128,384]{2,1,0:T(8,128)(2,1)S(1)} %attend.2.refs_0_), channel_id=1, source_target_pairs={{0,2},{1,3},{2,0},{3,1},{4,6},{5,7},{6,4},{7,5},{8,10},{9,11},{10,... | collective-permute-start | bytes 589832 | tf_op jit(solution)/shard_map/ppermute | solution.py:42
  116.6 8.8 %collective-permute-start.30 = (bf16[384,768]{1,0:T(8,128)(2,1)S(1)}, bf16[384,768]{1,0:T(8,128)(2,1)S(1)}, u32[]{:S(2)}, u32[]{:S(2)}) collective-permute-start(bf16[384,768]{1,0:T(8,128)(2,1)S(1)} %collective-permute-done.26.refs_2_), channel_id=1, source_target_pairs={{0,1},{1,0},{2,3},{3,2},{4,5},{5,4},{6,7},{7,6},{8,9},{9,8},{10,11... | collective-permute-start | bytes 1769480 | tf_op jit(solution)/shard_map/ppermute | solution.py:42
  116.6 9.4 %collective-permute-start.29 = (bf16[384,768]{1,0:T(8,128)(2,1)S(1)}, bf16[384,768]{1,0:T(8,128)(2,1)S(1)}, u32[]{:S(2)}, u32[]{:S(2)}) collective-permute-start(bf16[384,768]{1,0:T(8,128)(2,1)S(1)} %collective-permute-done.25.refs_1_), channel_id=1, source_target_pairs={{0,1},{1,0},{2,3},{3,2},{4,5},{5,4},{6,7},{7,6},{8,9},{9,8},{10,11... | collective-permute-start | bytes 1769480 | tf_op jit(solution)/shard_map/ppermute | solution.py:42
  117.1 9.0 %collective-permute-start.28 = (bf16[384,768]{1,0:T(8,128)(2,1)S(1)}, bf16[384,768]{1,0:T(8,128)(2,1)S(1)}, u32[]{:S(2)}, u32[]{:S(2)}) collective-permute-start(bf16[384,768]{1,0:T(8,128)(2,1)S(1)} %collective-permute-done.24.refs_0_), channel_id=1, source_target_pairs={{0,1},{1,0},{2,3},{3,2},{4,5},{5,4},{6,7},{7,6},{8,9},{9,8},{10,11... | collective-permute-start | bytes 1769480 | tf_op jit(solution)/shard_map/ppermute | solution.py:42
  126.6 55.7 %collective-permute-start.50 = (bf16[384,768]{1,0:T(8,128)(2,1)S(1)}, bf16[384,768]{1,0:T(8,128)(2,1)S(1)}, u32[]{:S(2)}, u32[]{:S(2)}) collective-permute-start(bf16[384,768]{1,0:T(8,128)(2,1)S(1)} %collective-permute-done.47.refs_0_), channel_id=1, source_target_pairs={{0,8},{1,9},{2,10},{3,11},{4,12},{5,13},{6,14},{7,15},{8,0},{9,1},... | collective-permute-start | bytes 1769480 | tf_op jit(solution)/shard_map/ppermute | solution.py:42
  128.8 53.7 %collective-permute-start.49 = (bf16[384,768]{1,0:T(8,128)(2,1)S(1)}, bf16[384,768]{1,0:T(8,128)(2,1)S(1)}, u32[]{:S(2)}, u32[]{:S(2)}) collective-permute-start(bf16[384,768]{1,0:T(8,128)(2,1)S(1)} %collective-permute-done.47.refs_0_), channel_id=1, source_target_pairs={{0,12},{1,13},{2,14},{3,15},{4,0},{5,1},{6,2},{7,3},{8,4},{9,5},{1... | collective-permute-start | bytes 1769480 | tf_op jit(solution)/shard_map/ppermute | solution.py:42
  128.8 54.2 %collective-permute-start.48 = (bf16[384,768]{1,0:T(8,128)(2,1)S(1)}, bf16[384,768]{1,0:T(8,128)(2,1)S(1)}, u32[]{:S(2)}, u32[]{:S(2)}) collective-permute-start(bf16[384,768]{1,0:T(8,128)(2,1)S(1)} %collective-permute-done.47.refs_0_), channel_id=1, source_target_pairs={{0,4},{1,5},{2,6},{3,7},{4,8},{5,9},{6,10},{7,11},{8,12},{9,13},{1... | collective-permute-start | bytes 1769480 | tf_op jit(solution)/shard_map/ppermute | solution.py:42
  157.8 9.5 %collective-permute-start.37 = (bf16[4,32,384]{2,1,0:T(8,128)(2,1)S(1)}, bf16[4,32,384]{2,1,0:T(8,128)(2,1)S(1)}, u32[]{:S(2)}, u32[]{:S(2)}) collective-permute-start(bf16[4,32,384]{2,1,0:T(8,128)(2,1)S(1)} %pack.11), channel_id=1, source_target_pairs={{2,6},{3,7},{4,0},{5,1},{6,10},{7,11},{8,4},{9,5},{10,14},{11,15},... | collective-permute-start | bytes 294920 | tf_op jit(solution)/shard_map/ppermute | solution.py:42
  165.0 12.2 %collective-permute-start.36 = (bf16[4,32,384]{2,1,0:T(8,128)(2,1)S(1)}, bf16[4,32,384]{2,1,0:T(8,128)(2,1)S(1)}, u32[]{:S(2)}, u32[]{:S(2)}) collective-permute-start(bf16[4,32,384]{2,1,0:T(8,128)(2,1)S(1)} %pack.10), channel_id=1, source_target_pairs={{0,4},{1,5},{4,8},{5,9},{6,2},{7,3},{8,12},{9,13},{10,6},{11,7},{1... | collective-permute-start | bytes 294920 | tf_op jit(solution)/shard_map/ppermute | solution.py:42
  167.2 16.2 %collective-permute-start.38 = (bf16[8,1,2,16,384]{4,3,2,1,0:T(8,128)(2,1)S(1)}, bf16[8,1,2,16,384]{4,3,2,1,0:T(8,128)(2,1)S(1)}, u32[]{:S(2)}, u32[]{:S(2)}) collective-permute-start(bf16[8,1,2,16,384]{4,3,2,1,0:T(8,128)(2,1)S(1)} %pack.9.refs_7_), channel_id=1, source_target_pairs={{0,16},{1,17},{2,18},{3,19},{4,20},{5,21},{6,22},{7,23},{8,24},{9,... | collective-permute-start | bytes 589832 | tf_op jit(solution)/shard_map/ppermute | solution.py:42
  182.4 20.8 %collective-permute-start.54 = (bf16[384,768]{1,0:T(8,128)(2,1)S(1)}, bf16[384,768]{1,0:T(8,128)(2,1)S(1)}, u32[]{:S(2)}, u32[]{:S(2)}) collective-permute-start(bf16[384,768]{1,0:T(8,128)(2,1)S(1)} %collective-permute-done.50.refs_3_), channel_id=1, source_target_pairs={{0,1},{1,0},{2,3},{3,2},{4,5},{5,4},{6,7},{7,6},{8,9},{9,8},{10,11... | collective-permute-start | bytes 1769480 | tf_op jit(solution)/shard_map/ppermute | solution.py:42
  182.5 22.5 %collective-permute-start.53 = (bf16[384,768]{1,0:T(8,128)(2,1)S(1)}, bf16[384,768]{1,0:T(8,128)(2,1)S(1)}, u32[]{:S(2)}, u32[]{:S(2)}) collective-permute-start(bf16[384,768]{1,0:T(8,128)(2,1)S(1)} %collective-permute-done.49.refs_2_), channel_id=1, source_target_pairs={{0,1},{1,0},{2,3},{3,2},{4,5},{5,4},{6,7},{7,6},{8,9},{9,8},{10,11... | collective-permute-start | bytes 1769480 | tf_op jit(solution)/shard_map/ppermute | solution.py:42
  183.0 22.3 %collective-permute-start.52 = (bf16[384,768]{1,0:T(8,128)(2,1)S(1)}, bf16[384,768]{1,0:T(8,128)(2,1)S(1)}, u32[]{:S(2)}, u32[]{:S(2)}) collective-permute-start(bf16[384,768]{1,0:T(8,128)(2,1)S(1)} %collective-permute-done.48.refs_1_), channel_id=1, source_target_pairs={{0,1},{1,0},{2,3},{3,2},{4,5},{5,4},{6,7},{7,6},{8,9},{9,8},{10,11... | collective-permute-start | bytes 1769480 | tf_op jit(solution)/shard_map/ppermute | solution.py:42
  183.1 22.4 %collective-permute-start.51 = (bf16[384,768]{1,0:T(8,128)(2,1)S(1)}, bf16[384,768]{1,0:T(8,128)(2,1)S(1)}, u32[]{:S(2)}, u32[]{:S(2)}) collective-permute-start(bf16[384,768]{1,0:T(8,128)(2,1)S(1)} %collective-permute-done.47.refs_0_), channel_id=1, source_target_pairs={{0,1},{1,0},{2,3},{3,2},{4,5},{5,4},{6,7},{7,6},{8,9},{9,8},{10,11... | collective-permute-start | bytes 1769480 | tf_op jit(solution)/shard_map/ppermute | solution.py:42
  205.5 8.7 %collective-permute-start.43 = (bf16[128,384]{1,0:T(8,128)(2,1)S(1)}, bf16[128,384]{1,0:T(8,128)(2,1)S(1)}, u32[]{:S(2)}, u32[]{:S(2)}) collective-permute-start(bf16[128,384]{1,0:T(8,128)(2,1)S(1)} %get-tuple-element.126), channel_id=1, source_target_pairs={{0,3},{1,2},{2,1},{3,0},{4,7},{5,6},{6,5},{7,4},{8,11},{9,10},{10,... | collective-permute-start | bytes 294920 | tf_op jit(solution)/shard_map/ppermute | solution.py:42
  (35 other events, 300.5 us)

commit v2 on v1

--- a/solution.py
+++ b/solution.py
@@ -287,7 +287,9 @@
 
 def qkv_kernel(l, which, *refs):
     pieces, (gain, w, qkg, out, outer, inner, normed) = refs[:-7], refs[-7:]
-    norm_rows(pieces, gain.at[l : l + 1], normed, 4 // len(pieces))
+    half = BLK // 2
+    views = [p.at[pl.ds(r, half)] for p in pieces for r in range(0, p.shape[0], half)]
+    norm_rows(views, gain.at[l : l + 1], normed)
 
     def put(m, c, p):
         out[c] = p
@@ -508,7 +510,7 @@
 
 def final_kernel(*refs):
     skip, atts, others = refs[0], refs[1:5], refs[5:9]
-    (video, first, wslot, out, acat) = refs[9:]
+    (xa, xb, first, wslot, out, acat) = refs[9:]
     for j in range(4):
         for b, piece in enumerate((atts[j], others[j])):
             acat[b * BLK : (b + 1) * BLK, j * INNER : (j + 1) * INNER] = piece[...]
@@ -519,7 +521,8 @@
         t = jnp.dot(acat[...], wslot[k], preferred_element_type=F32)
         f = first[:, cols].astype(F32)
         strong = (f + t[:BLK]).astype(BF16).astype(F32)
-        other = (video[:, cols].astype(F32) + t[BLK:]).astype(BF16).astype(F32)
+        video = jnp.concatenate([xa[:, cols], xb[:, cols]], axis=0).astype(F32)
+        other = (video + t[BLK:]).astype(BF16).astype(F32)
         weak = jnp.where(skip_first, other, f)
         out[:, cols] = (strong + GUIDE * (strong - weak)).astype(BF16)
         return carry
@@ -527,11 +530,11 @@
     lax.fori_loop(0, 4, block, 0)
 
 
-def final(skip, atts, others, video, first, wslot):
+def final(skip, atts, others, xa, xb, first, wslot):
     return pl.pallas_call(
         final_kernel,
         out_shape=shape(BLK, D),
-        in_specs=[SM] + [VM] * 11,
+        in_specs=[SM] + [VM] * 12,
         out_specs=VM,
         scratch_shapes=[pltpu.VMEM((2 * BLK, 4 * INNER), BF16)],
         compiler_params=params(7),
@@ -541,7 +544,7 @@
             bytes_accessed=2 * (4 * D * INNER + 3 * BLK * D),
         ),
         name="final",
-    )(skip, *atts, *others, video, first, wslot)
+    )(skip, *atts, *others, xa, xb, first, wslot)
 
 
 def after(value, *done):
@@ -591,23 +594,22 @@
     kz = send(kv, to_far)
     x2b = send(after(xb, kv), to_z)
     wz0 = [here0] + [send(after(here0, kv), to_y(d)) for d in (1, 3)]
-    own0 = qkv(0, 0, (after(x0, kv), x1), norm_gain, w, qk_gain)
+    own0 = qkv(0, 0, (after(xa, kv), xb, x1), norm_gain, w, qk_gain)
     kx = pack(kv, after(kz, own0[0]))
     kxs = [send(kx, to_x(d)) for d in (1, 3, 2)]
     x3a = send(after(x2a, kx), to_sib)
-    here1 = send(after(piece1, kx), to_far_z)
-    own1 = qkv(1, 0, (after(x0, kx), x1), norm_gain, w, qk_gain)
+    own1 = qkv(1, 0, (after(xa, kx), xb, x1), norm_gain, w, qk_gain)
     ky = pack(kx, *[after(k, own1[0]) for k in kxs])
     kys = [send(ky, to_y(d)) for d in (1, 3, 2)]
+    here1 = send(after(piece1, ky), to_far_z)
     x3b = send(after(x2b, own1[0]), to_sib)
     halves = (after(x2a, ky), x2b, x3a, x3b)
     par0 = qkv(0, 1, halves, norm_gain, w, qk_gain)
     eo, ep = edges(own0, par0)
     wsib = send(after(w_out, par0[0]), to_sib)
-    wz0.append(send(after(here0, par0[0]), to_y(2)))
-    wz1 = [here1] + [send(after(here1, eo, ep), to_x(d)) for d in (1, 3, 2)]
     ctx = [ky] + kys
     ao = attend(0, 0, halo_frames, own0[0], par0[2], eo, ctx)
+    wz0.append(send(after(here0, ao), to_y(2)))
     oz = send(ao, to_z)
     os = send(ao, to_sib)
     ap = attend(0, 1, halo_frames, after(par0[0], ao), own0[2], ep, ctx)
@@ -615,14 +617,16 @@
     ps = send(ap, to_sib)
     halves = (after(x2a, ap), x2b, x3a, x3b)
     par1 = qkv(1, 1, halves, norm_gain, w, qk_gain)
-    wzs0 = [send(after(p, ap), to_sib) for p in wz0]
+    wzs0 = [send(after(p, ap), to_sib) for p in wz0[:3]]
+    wzs0.append(send(after(wz0[3], par1[0]), to_sib))
+    wz1 = [here1] + [send(after(here1, par1[0]), to_x(d)) for d in (1, 3, 2)]
     ozs = send(after(oz, par1[0]), to_sib)
     wslot0 = assemble(0, after(w_out, par1[0]), wsib, wz0, wzs0)
     pzs = send(pz, to_sib)
 
     first, fo, fp, fkv = first_qkv(
         (ao, ap, os, ps, oz, pz, ozs, pzs),
-        (x0, x1, x2a, x2b, x3a, x3b),
+        (xa, xb, x1, x2a, x2b, x3a, x3b),
         wslot0,
         norm_gain,
         w,
@@ -645,7 +649,7 @@
     atts = [g[0], send(g[1], to_sib), send(g[2], to_z), send(g[3], to_diag)]
     wzs1 = [send(after(p, b[0]), to_sib) for p in wz1]
     wslot1 = assemble(1, after(w_out, g[0]), wsib, wz1, wzs1)
-    return final(skip_layer, atts, others, x0, first, wslot1)
+    return final(skip_layer, atts, others, xa, xb, first, wslot1)
 
 
 def solution(mesh):

time: 220 us -> 211 us (0.959)
  waiting for transfers between devices: 103 us -> 92.4 us
  starting transfers between devices: 53.8 us -> 56.8 us
    ppermute x55, waiting for transfers between devices: 103 us -> 92.4 us  [send(): return lax.ppermute(value, AXES, pairs)]
    ppermute x55, starting transfers between devices: 53.8 us -> 56.8 us  [send(): return lax.ppermute(value, AXES, pairs)]
  transfers between devices with their start and end apart: 55 -> 55, of which waited for: 20 -> 21; matrix products, arithmetic and copies ran while one was open for 0% -> 0% of each run, Pallas kernels for 22% -> 23%
where the time goes in v2:
time: 211 us; the launch traced here: 210 us
  waiting for transfers between devices  92.4 us (44%)
  Pallas kernels  59.5 us (28%)
  starting transfers between devices  56.8 us (27%)
    ppermute x55, waiting for transfers between devices, send(): return lax.ppermute(value, AXES, pairs)  92.4 us
    ppermute x55, starting transfers between devices, send(): return lax.ppermute(value, AXES, pairs)  56.8 us
    pallas_call x1, Pallas kernels, first_qkv(): pl.pallas_call(first_kernel, out_shape=(shape(BLK, D),) + one + one + (sh...  13.5 us
    pallas_call x4, Pallas kernels, qkv(): pl.pallas_call(functools.partial(qkv_kernel, l, which), out_shape=(shape(...  12.4 us
    pallas_call x2, Pallas kernels, attend_pair(): pl.pallas_call(functools.partial(attend_pair_kernel, cl, at), out_shape=(...  10.2 us
    pallas_call x2, Pallas kernels, attend(): pl.pallas_call(functools.partial(attend_kernel, cl, which), out_shape=sha...  5.67 us
    pallas_call x1, Pallas kernels, stage(): pl.pallas_call(stage_kernel, out_shape=pltpu.VMEM((2, D, 3 * INNER), BF16...  5.17 us
    pallas_call x1, Pallas kernels, final(): pl.pallas_call(final_kernel, out_shape=shape(BLK, D), in_specs=[SM] + [VM...  4.89 us
  transfers between devices with their start and end apart: 55, of which 21 were waited for; matrix products, arithmetic and copies ran while one was open for 0% of the time, Pallas kernels for 23%

profile of v2, /device:TPU:64, one launch (start us, length us, event | category | flops | bytes accessed | tf_op | source)
XLA Modules:
  0.0 210.0 jit_solution(16544572487449341042)
XLA Ops:
  5.5 5.2 %stage.1.w.refs_4_.refs_5_.refs_17_ = bf16[2,3072,1152]{2,1,0:T(8,128)(2,1)S(1)} custom-call(bf16[2,3,3072,384]{3,2,1,0:T(8,128)(2,1)} %bitcast.3), custom_call_target="tpu_custom_call" | custom-call | tf_op jit(solution)/shard_map/stage/pallas_call | solution.py:130
  14.6 3.1 %qkv.4 = (bf16[3,256,384]{2,1,0:T(8,128)(2,1)S(1)}, bf16[2,32,384]{2,1,0:T(8,128)(2,1)S(1)}, bf16[2,32,384]{2,1,0:T(8,128)(2,1)S(1)}) custom-call(bf16[64,3072]{1,0:T(8,128)(2,1)S(1)} %get-tuple-element.81.refs_0_.refs_8_.refs_9_, bf16[64,3072]{1,0:T(8,128)(2,1)S(1)} %get-tuple-element.87.refs_1_.refs_9_.refs_10_, ...), custom_call_target="tpu_custom_call" | custom-call | flops 1811939328 | bytes 8650752 | tf_op jit(solution)/shard_map/qkv/pallas_call | solution.py:302
  17.7 15.4 %collective-permute-done.5.refs_1_ = bf16[1,2,2,16,384]{4,3,2,1,0:T(8,128)(2,1)S(1)} collective-permute-done((bf16[1,2,2,16,384]{4,3,2,1,0:T(8,128)(2,1)S(1)}, bf16[1,2,2,16,384]{4,3,2,1,0:T(8,128)(2,1)S(1)}, u32[]{:S(2)}, u32[]{:S(2)}) %collective-permute-start.5) | collective-permute-done | bytes 49184 | tf_op jit(solution)/shard_map/ppermute | solution.py:42
  33.1 3.1 %qkv.5 = (bf16[3,256,384]{2,1,0:T(8,128)(2,1)S(1)}, bf16[2,32,384]{2,1,0:T(8,128)(2,1)S(1)}, bf16[2,32,384]{2,1,0:T(8,128)(2,1)S(1)}) custom-call(bf16[64,3072]{1,0:T(8,128)(2,1)S(1)} %get-tuple-element.81.refs_0_.refs_8_.refs_9_, bf16[64,3072]{1,0:T(8,128)(2,1)S(1)} %get-tuple-element.87.refs_1_.refs_9_.refs_10_, ...), custom_call_target="tpu_custom_call" | custom-call | flops 1811939328 | bytes 8650752 | tf_op jit(solution)/shard_map/qkv/pallas_call | solution.py:302
  36.9 3.0 %collective-permute-start.8 = (bf16[2,2,2,16,384]{4,3,2,1,0:T(8,128)(2,1)S(1)}, bf16[2,2,2,16,384]{4,3,2,1,0:T(8,128)(2,1)S(1)}, u32[]{:S(2)}, u32[]{:S(2)}) collective-permute-start(bf16[2,2,2,16,384]{4,3,2,1,0:T(8,128)(2,1)S(1)} %pack.6.refs_0_), channel_id=1, source_target_pairs={{0,8},{1,9},{2,10},{3,11},{4,12},{5,13},{6,14},{7,15},{8,0},{9,1},... | collective-permute-start | bytes 294920 | tf_op jit(solution)/shard_map/ppermute | solution.py:42
  43.4 2.0 collective-permute-done.7.refs_2_
  46.9 3.1 %qkv.6 = (bf16[3,256,384]{2,1,0:T(8,128)(2,1)S(1)}, bf16[2,32,384]{2,1,0:T(8,128)(2,1)S(1)}, bf16[2,32,384]{2,1,0:T(8,128)(2,1)S(1)}) custom-call(bf16[64,3072]{1,0:T(8,128)(2,1)S(1)} %collective-permute-done.4.refs_0_.refs_11_, bf16[64,3072]{1,0:T(8,128)(2,1)S(1)} %collective-permute-done.9.refs_1_.refs_12_, ...), custom_call_target="tpu_custom_call" | custom-call | flops 1811939328 | bytes 8650752 | tf_op jit(solution)/shard_map/qkv/pallas_call | solution.py:302
  50.2 2.0 collective-permute-start.24
  55.4 2.0 collective-permute-start.15
  57.4 8.7 %collective-permute-done.24.refs_0_ = bf16[384,768]{1,0:T(8,128)(2,1)S(1)} collective-permute-done((bf16[384,768]{1,0:T(8,128)(2,1)S(1)}, bf16[384,768]{1,0:T(8,128)(2,1)S(1)}, u32[]{:S(2)}, u32[]{:S(2)}) %collective-permute-start.24) | collective-permute-done | bytes 589856 | tf_op jit(solution)/shard_map/ppermute | solution.py:42
  66.1 1.9 collective-permute-start.12
  68.0 9.8 %collective-permute-done.12.outer = bf16[2,32,384]{2,1,0:T(8,128)(2,1)S(1)} collective-permute-done((bf16[2,32,384]{2,1,0:T(8,128)(2,1)S(1)}, bf16[2,32,384]{2,1,0:T(8,128)(2,1)S(1)}, u32[]{:S(2)}, u32[]{:S(2)}) %collective-permute-start.12) | collective-permute-done | bytes 49184 | tf_op jit(solution)/shard_map/ppermute | solution.py:42
  77.8 2.0 collective-permute-start.25
  79.8 5.1 %collective-permute-start.16 = (bf16[2,32,384]{2,1,0:T(8,128)(2,1)S(1)}, bf16[2,32,384]{2,1,0:T(8,128)(2,1)S(1)}, u32[]{:S(2)}, u32[]{:S(2)}) collective-permute-start(bf16[2,32,384]{2,1,0:T(8,128)(2,1)S(1)} %get-tuple-element.95), channel_id=1, source_target_pairs={{2,6},{3,7},{4,0},{5,1},{6,10},{7,11},{8,4},{9,5},{10,14},{11,15},... | collective-permute-start | bytes 147464 | tf_op jit(solution)/shard_map/ppermute | solution.py:42
  84.9 2.8 %attend.2.refs_0_ = bf16[2,128,384]{2,1,0:T(8,128)(2,1)S(1)} custom-call(s32[2]{0:T(128)S(1)} %copy-done.4, bf16[3,256,384]{2,1,0:T(8,128)(2,1)S(1)} %get-tuple-element.79.mine, bf16[2,32,384]{2,1,0:T(8,128)(2,1)S(1)} %get-tuple-element.90.inner, bf16[2,32,384]{2,1,0:T(8,128)(2,1)S(1)} %collective-permute-done.12.outer, ...), custom_call_target="tpu_custom_call" | custom-call | flops 490733568 | bytes 1671168 | tf_op jit(solution)/shard_map/attend/pallas_call | solution.py:385
  88.0 6.0 %collective-permute-done.26.refs_2_ = bf16[384,768]{1,0:T(8,128)(2,1)S(1)} collective-permute-done((bf16[384,768]{1,0:T(8,128)(2,1)S(1)}, bf16[384,768]{1,0:T(8,128)(2,1)S(1)}, u32[]{:S(2)}, u32[]{:S(2)}) %collective-permute-start.26) | collective-permute-done | bytes 589856 | tf_op jit(solution)/shard_map/ppermute | solution.py:42
  94.0 2.8 %attend.3.refs_1_ = bf16[2,128,384]{2,1,0:T(8,128)(2,1)S(1)} custom-call(s32[2]{0:T(128)S(1)} %copy-done.4, bf16[3,256,384]{2,1,0:T(8,128)(2,1)S(1)} %get-tuple-element.93.mine, bf16[2,32,384]{2,1,0:T(8,128)(2,1)S(1)} %get-tuple-element.94.inner, bf16[2,32,384]{2,1,0:T(8,128)(2,1)S(1)} %collective-permute-done.16.outer, ...), custom_call_target="tpu_custom_call" | custom-call | flops 490733568 | bytes 1671168 | tf_op jit(solution)/shard_map/attend/pallas_call | solution.py:385
  96.8 8.7 %collective-permute-done.25.refs_1_ = bf16[384,768]{1,0:T(8,128)(2,1)S(1)} collective-permute-done((bf16[384,768]{1,0:T(8,128)(2,1)S(1)}, bf16[384,768]{1,0:T(8,128)(2,1)S(1)}, u32[]{:S(2)}, u32[]{:S(2)}) %collective-permute-start.25) | collective-permute-done | bytes 589856 | tf_op jit(solution)/shard_map/ppermute | solution.py:42
  105.5 3.1 %qkv.7 = (bf16[3,256,384]{2,1,0:T(8,128)(2,1)S(1)}, bf16[2,32,384]{2,1,0:T(8,128)(2,1)S(1)}, bf16[2,32,384]{2,1,0:T(8,128)(2,1)S(1)}) custom-call(bf16[64,3072]{1,0:T(8,128)(2,1)S(1)} %collective-permute-done.4.refs_0_.refs_11_, bf16[64,3072]{1,0:T(8,128)(2,1)S(1)} %collective-permute-done.9.refs_1_.refs_12_, ...), custom_call_target="tpu_custom_call" | custom-call | flops 1811939328 | bytes 8650752 | tf_op jit(solution)/shard_map/qkv/pallas_call | solution.py:302
  109.2 1.9 collective-permute-done.20.refs_5_
  119.0 13.5 %first_qkv.1 = (bf16[128,3072]{1,0:T(8,128)(2,1)S(1)}, bf16[3,256,384]{2,1,0:T(8,128)(2,1)S(1)}, bf16[2,32,384]{2,1,0:T(8,128)(2,1)S(1)}, bf16[2,32,384]{2,1,0:T...) custom-call(bf16[2,128,384]{2,1,0:T(8,128)(2,1)S(1)} %attend.2.refs_, ...), custom_call_target="tpu_custom_call" | custom-call | flops 8455716864 | bytes 22806528 | tf_op jit(solution)/shard_map/first_qkv/pallas_call | solution.py:490
  132.6 4.5 %collective-permute-start.32 = (bf16[1,1,2,16,384]{4,3,2,1,0:T(8,128)(2,1)S(1)}, bf16[1,1,2,16,384]{4,3,2,1,0:T(8,128)(2,1)S(1)}, u32[]{:S(2)}, u32[]{:S(2)}) collective-permute-start(bf16[1,1,2,16,384]{4,3,2,1,0:T(8,128)(2,1)S(1)} %get-tuple-element.108.refs_0_), channel_id=1, source_target_pairs={{0,64},{1,65},{2,66},{3,67},{4,68},{5,69},{6,70},{7,71},{8,72},{9,... | collective-permute-start | bytes 73736 | tf_op jit(solution)/shard_map/ppermute | solution.py:42
  142.1 2.9 %collective-permute-done.33.refs_1_ = bf16[2,1,2,16,384]{4,3,2,1,0:T(8,128)(2,1)S(1)} collective-permute-done((bf16[2,1,2,16,384]{4,3,2,1,0:T(8,128)(2,1)S(1)}, bf16[2,1,2,16,384]{4,3,2,1,0:T(8,128)(2,1)S(1)}, u32[]{:S(2)}, u32[]{:S(2)}) %collective-permute-start.33) | collective-permute-done | bytes 49184 | tf_op jit(solution)/shard_map/ppermute | solution.py:42
  146.1 9.7 %collective-permute-start.37 = (bf16[4,32,384]{2,1,0:T(8,128)(2,1)S(1)}, bf16[4,32,384]{2,1,0:T(8,128)(2,1)S(1)}, u32[]{:S(2)}, u32[]{:S(2)}) collective-permute-start(bf16[4,32,384]{2,1,0:T(8,128)(2,1)S(1)} %pack.11), channel_id=1, source_target_pairs={{2,6},{3,7},{4,0},{5,1},{6,10},{7,11},{8,4},{9,5},{10,14},{11,15},... | collective-permute-start | bytes 294920 | tf_op jit(solution)/shard_map/ppermute | solution.py:42
  155.9 1.9 collective-permute-start.36
  158.1 10.0 %collective-permute-done.36.refs_3_ = bf16[4,32,384]{2,1,0:T(8,128)(2,1)S(1)} collective-permute-done((bf16[4,32,384]{2,1,0:T(8,128)(2,1)S(1)}, bf16[4,32,384]{2,1,0:T(8,128)(2,1)S(1)}, u32[]{:S(2)}, u32[]{:S(2)}) %collective-permute-start.36) | collective-permute-done | bytes 98336 | tf_op jit(solution)/shard_map/ppermute | solution.py:42
  168.1 5.1 %attend_pair.2 = (bf16[128,384]{1,0:T(8,128)(2,1)S(1)}, bf16[128,384]{1,0:T(8,128)(2,1)S(1)}, bf16[128,384]{1,0:T(8,128)(2,1)S(1)}, bf16[128,384]{1,0:T(8,128)(2,1)S(1)}) custom-call(s32[2]{0:T(128)S(1)} %copy-done.4, bf16[3,256,384]{2,1,0:T(8,128)(2,1)S(1)} %get-tuple-element.109.refs_1_, bf16[2,32,384]{2,1,0:T(8,128)(2,1)S(1)} %get-tuple-element.110.refs_2_, ...), custom_call_target="tpu_custom_call" | custom-call | flops 981467136 | bytes 2064384 | tf_op jit(solution)/shard_map/attend_pair/pallas_call | solution.py:412
  174.4 6.9 %collective-permute-done.39.refs_9_ = bf16[8,1,2,16,384]{4,3,2,1,0:T(8,128)(2,1)S(1)} collective-permute-done((bf16[8,1,2,16,384]{4,3,2,1,0:T(8,128)(2,1)S(1)}, bf16[8,1,2,16,384]{4,3,2,1,0:T(8,128)(2,1)S(1)}, u32[]{:S(2)}, u32[]{:S(2)}) %collective-permute-start.39) | collective-permute-done | bytes 196640 | tf_op jit(solution)/shard_map/ppermute | solution.py:42
  181.3 7.6 %collective-permute-done.40.refs_10_ = bf16[8,1,2,16,384]{4,3,2,1,0:T(8,128)(2,1)S(1)} collective-permute-done((bf16[8,1,2,16,384]{4,3,2,1,0:T(8,128)(2,1)S(1)}, bf16[8,1,2,16,384]{4,3,2,1,0:T(8,128)(2,1)S(1)}, u32[]{:S(2)}, u32[]{:S(2)}) %collective-permute-start.40) | collective-permute-done | bytes 196640 | tf_op jit(solution)/shard_map/ppermute | solution.py:42
  188.8 5.1 %attend_pair.3 = (bf16[128,384]{1,0:T(8,128)(2,1)S(1)}, bf16[128,384]{1,0:T(8,128)(2,1)S(1)}, bf16[128,384]{1,0:T(8,128)(2,1)S(1)}, bf16[128,384]{1,0:T(8,128)(2,1)S(1)}) custom-call(s32[2]{0:T(128)S(1)} %copy-done.4, bf16[3,256,384]{2,1,0:T(8,128)(2,1)S(1)} %get-tuple-element.119.refs_1_, bf16[2,32,384]{2,1,0:T(8,128)(2,1)S(1)} %get-tuple-element.120.refs_2_, ...), custom_call_target="tpu_custom_call" | custom-call | flops 981467136 | bytes 2064384 | tf_op jit(solution)/shard_map/attend_pair/pallas_call | solution.py:412
  200.9 3.0 %collective-permute-done.42.refs_3_ = bf16[128,384]{1,0:T(8,128)(2,1)S(1)} collective-permute-done((bf16[128,384]{1,0:T(8,128)(2,1)S(1)}, bf16[128,384]{1,0:T(8,128)(2,1)S(1)}, u32[]{:S(2)}, u32[]{:S(2)}) %collective-permute-start.42) | collective-permute-done | bytes 98336 | tf_op jit(solution)/shard_map/ppermute | solution.py:42
  205.1 4.9 %final.1 = bf16[128,3072]{1,0:T(8,128)(2,1)} custom-call(s32[2]{0:T(128)S(1)} %copy-done.7, bf16[128,384]{1,0:T(8,128)(2,1)S(1)} %get-tuple-element.123.refs_1_, bf16[128,384]{1,0:T(8,128)(2,1)S(1)} %collective-permute-done.41.refs_2_, bf16[128,384]{1,0:T(8,128)(2,1)S(1)} %collective-permute-done.42.refs_3_, ...), custom_call_target="tpu_custom_call" | custom-call | flops 2415919104 | bytes 11796480 | tf_op jit(solution)/shard_map/final/pallas_call | solution.py:534
  (121 shorter events, 42.6 us)
Async XLA Ops:
  3.3 11.3 %collective-permute-start.3 = (bf16[128,3072]{1,0:T(8,128)(2,1)}, bf16[128,3072]{1,0:T(8,128)(2,1)S(1)}, u32[]{:S(2)}, u32[]{:S(2)}) collective-permute-start(bf16[128,3072]{1,0:T(8,128)(2,1)} %x), channel_id=1, source_target_pairs={{0,1},{1,0},{2,3},{3,2},{4,5},{5,4},{6,7},{7,6},{8,9},{9,8},{10,11... | collective-permute-start | bytes 2359304 | tf_op jit(solution)/shard_map/ppermute | solution.py:42
  12.5 23.7 %collective-permute-start.9 = (bf16[64,3072]{1,0:T(8,128)(2,1)S(1)}, bf16[64,3072]{1,0:T(8,128)(2,1)S(1)}, u32[]{:S(2)}, u32[]{:S(2)}) collective-permute-start(bf16[64,3072]{1,0:T(8,128)(2,1)S(1)} %get-tuple-element.87.refs_1_.refs_9_.refs_10_), channel_id=1, source_target_pairs={{0,2},{1,3},{2,0},{3,1},{4,6},{5,7},{6,4},{7,5},{8,10},{9,11},{10,... | collective-permute-start | bytes 1179656 | tf_op jit(solution)/shard_map/ppermute | solution.py:42
  14.0 22.4 %collective-permute-start.4 = (bf16[64,3072]{1,0:T(8,128)(2,1)S(1)}, bf16[64,3072]{1,0:T(8,128)(2,1)S(1)}, u32[]{:S(2)}, u32[]{:S(2)}) collective-permute-start(bf16[64,3072]{1,0:T(8,128)(2,1)S(1)} %get-tuple-element.81.refs_0_.refs_8_.refs_9_), channel_id=1, source_target_pairs={{0,2},{1,3},{2,0},{3,1},{4,6},{5,7},{6,4},{7,5},{8,10},{9,11},{10,... | collective-permute-start | bytes 1179656 | tf_op jit(solution)/shard_map/ppermute | solution.py:42
  14.6 18.5 %collective-permute-start.5 = (bf16[1,2,2,16,384]{4,3,2,1,0:T(8,128)(2,1)S(1)}, bf16[1,2,2,16,384]{4,3,2,1,0:T(8,128)(2,1)S(1)}, u32[]{:S(2)}, u32[]{:S(2)}) collective-permute-start(bf16[1,2,2,16,384]{4,3,2,1,0:T(8,128)(2,1)S(1)} %context_kv.1.refs_0_), channel_id=1, source_target_pairs={{0,64},{1,65},{2,66},{3,67},{4,68},{5,69},{6,70},{7,71},{8,72},{9,... | collective-permute-start | bytes 147464 | tf_op jit(solution)/shard_map/ppermute | solution.py:42
  36.3 10.6 %collective-permute-start.11 = (bf16[64,3072]{1,0:T(8,128)(2,1)S(1)}, bf16[64,3072]{1,0:T(8,128)(2,1)S(1)}, u32[]{:S(2)}, u32[]{:S(2)}) collective-permute-start(bf16[64,3072]{1,0:T(8,128)(2,1)S(1)} %collective-permute-done.9.refs_1_.refs_12_), channel_id=1, source_target_pairs={{0,1},{1,0},{2,3},{3,2},{4,5},{5,4},{6,7},{7,6},{8,9},{9,8},{10,11... | collective-permute-start | bytes 1179656 | tf_op jit(solution)/shard_map/ppermute | solution.py:42
  36.4 10.5 %collective-permute-start.10 = (bf16[64,3072]{1,0:T(8,128)(2,1)S(1)}, bf16[64,3072]{1,0:T(8,128)(2,1)S(1)}, u32[]{:S(2)}, u32[]{:S(2)}) collective-permute-start(bf16[64,3072]{1,0:T(8,128)(2,1)S(1)} %collective-permute-done.4.refs_0_.refs_11_), channel_id=1, source_target_pairs={{0,1},{1,0},{2,3},{3,2},{4,5},{5,4},{6,7},{7,6},{8,9},{9,8},{10,11... | collective-permute-start | bytes 1179656 | tf_op jit(solution)/shard_map/ppermute | solution.py:42
  50.1 64.1 %collective-permute-start.23 = (bf16[2,384,3072]{2,1,0:T(8,128)(2,1)S(1)}, bf16[2,384,3072]{2,1,0:T(8,128)(2,1)S(1)}, u32[]{:S(2)}, u32[]{:S(2)}) collective-permute-start(bf16[2,384,3072]{2,1,0:T(8,128)(2,1)S(1)} %bitcast.2), channel_id=1, source_target_pairs={{0,1},{1,0},{2,3},{3,2},{4,5},{5,4},{6,7},{7,6},{8,9},{9,8},{10,11... | collective-permute-start | bytes 14155784 | tf_op jit(solution)/shard_map/ppermute | solution.py:42
  50.2 15.9 %collective-permute-start.24 = (bf16[384,768]{1,0:T(8,128)(2,1)S(1)}, bf16[384,768]{1,0:T(8,128)(2,1)S(1)}, u32[]{:S(2)}, u32[]{:S(2)}) collective-permute-start(bf16[384,768]{1,0:T(8,128)(2,1)S(1)} %get-tuple-element.72), channel_id=1, source_target_pairs={{0,66},{1,67},{2,64},{3,65},{4,70},{5,71},{6,68},{7,69},{8,74},{9,... | collective-permute-start | bytes 1769480 | tf_op jit(solution)/shard_map/ppermute | solution.py:42
  52.2 25.6 %collective-permute-start.13 = (bf16[8,2,2,16,384]{4,3,2,1,0:T(8,128)(2,1)S(1)}, bf16[8,2,2,16,384]{4,3,2,1,0:T(8,128)(2,1)S(1)}, u32[]{:S(2)}, u32[]{:S(2)}) collective-permute-start(bf16[8,2,2,16,384]{4,3,2,1,0:T(8,128)(2,1)S(1)} %pack.7.c0.refs_7_), channel_id=1, source_target_pairs={{0,16},{1,17},{2,18},{3,19},{4,20},{5,21},{6,22},{7,23},{8,24},{9,... | collective-permute-start | bytes 1179656 | tf_op jit(solution)/shard_map/ppermute | solution.py:42
  53.8 26.1 %collective-permute-start.14 = (bf16[8,2,2,16,384]{4,3,2,1,0:T(8,128)(2,1)S(1)}, bf16[8,2,2,16,384]{4,3,2,1,0:T(8,128)(2,1)S(1)}, u32[]{:S(2)}, u32[]{:S(2)}) collective-permute-start(bf16[8,2,2,16,384]{4,3,2,1,0:T(8,128)(2,1)S(1)} %pack.7.c0.refs_7_), channel_id=1, source_target_pairs={{0,48},{1,49},{2,50},{3,51},{4,52},{5,53},{6,54},{7,55},{8,56},{9,... | collective-permute-start | bytes 1179656 | tf_op jit(solution)/shard_map/ppermute | solution.py:42
  55.4 29.5 %collective-permute-start.15 = (bf16[8,2,2,16,384]{4,3,2,1,0:T(8,128)(2,1)S(1)}, bf16[8,2,2,16,384]{4,3,2,1,0:T(8,128)(2,1)S(1)}, u32[]{:S(2)}, u32[]{:S(2)}) collective-permute-start(bf16[8,2,2,16,384]{4,3,2,1,0:T(8,128)(2,1)S(1)} %pack.7.c0.refs_7_), channel_id=1, source_target_pairs={{0,32},{1,33},{2,34},{3,35},{4,36},{5,37},{6,38},{7,39},{8,40},{9,... | collective-permute-start | bytes 1179656 | tf_op jit(solution)/shard_map/ppermute | solution.py:42
  66.1 11.7 %collective-permute-start.12 = (bf16[2,32,384]{2,1,0:T(8,128)(2,1)S(1)}, bf16[2,32,384]{2,1,0:T(8,128)(2,1)S(1)}, u32[]{:S(2)}, u32[]{:S(2)}) collective-permute-start(bf16[2,32,384]{2,1,0:T(8,128)(2,1)S(1)} %get-tuple-element.91), channel_id=1, source_target_pairs={{0,4},{1,5},{4,8},{5,9},{6,2},{7,3},{8,12},{9,13},{10,6},{11,7},{1... | collective-permute-start | bytes 147464 | tf_op jit(solution)/shard_map/ppermute | solution.py:42
  77.8 16.2 %collective-permute-start.26 = (bf16[384,768]{1,0:T(8,128)(2,1)S(1)}, bf16[384,768]{1,0:T(8,128)(2,1)S(1)}, u32[]{:S(2)}, u32[]{:S(2)}) collective-permute-start(bf16[384,768]{1,0:T(8,128)(2,1)S(1)} %collective-permute-done.24.refs_0_), channel_id=1, source_target_pairs={{0,48},{1,49},{2,50},{3,51},{4,52},{5,53},{6,54},{7,55},{8,56},{9,... | collective-permute-start | bytes 1769480 | tf_op jit(solution)/shard_map/ppermute | solution.py:42
  77.8 27.7 %collective-permute-start.25 = (bf16[384,768]{1,0:T(8,128)(2,1)S(1)}, bf16[384,768]{1,0:T(8,128)(2,1)S(1)}, u32[]{:S(2)}, u32[]{:S(2)}) collective-permute-start(bf16[384,768]{1,0:T(8,128)(2,1)S(1)} %collective-permute-done.24.refs_0_), channel_id=1, source_target_pairs={{0,16},{1,17},{2,18},{3,19},{4,20},{5,21},{6,22},{7,23},{8,24},{9,... | collective-permute-start | bytes 1769480 | tf_op jit(solution)/shard_map/ppermute | solution.py:42
  79.8 8.1 %collective-permute-start.16 = (bf16[2,32,384]{2,1,0:T(8,128)(2,1)S(1)}, bf16[2,32,384]{2,1,0:T(8,128)(2,1)S(1)}, u32[]{:S(2)}, u32[]{:S(2)}) collective-permute-start(bf16[2,32,384]{2,1,0:T(8,128)(2,1)S(1)} %get-tuple-element.95), channel_id=1, source_target_pairs={{2,6},{3,7},{4,0},{5,1},{6,10},{7,11},{8,4},{9,5},{10,14},{11,15},... | collective-permute-start | bytes 147464 | tf_op jit(solution)/shard_map/ppermute | solution.py:42
  87.8 20.9 %collective-permute-start.27 = (bf16[384,768]{1,0:T(8,128)(2,1)S(1)}, bf16[384,768]{1,0:T(8,128)(2,1)S(1)}, u32[]{:S(2)}, u32[]{:S(2)}) collective-permute-start(bf16[384,768]{1,0:T(8,128)(2,1)S(1)} %collective-permute-done.24.refs_0_), channel_id=1, source_target_pairs={{0,32},{1,33},{2,34},{3,35},{4,36},{5,37},{6,38},{7,39},{8,40},{9,... | collective-permute-start | bytes 1769480 | tf_op jit(solution)/shard_map/ppermute | solution.py:42
  87.9 23.3 %collective-permute-start.47 = (bf16[384,768]{1,0:T(8,128)(2,1)S(1)}, bf16[384,768]{1,0:T(8,128)(2,1)S(1)}, u32[]{:S(2)}, u32[]{:S(2)}) collective-permute-start(bf16[384,768]{1,0:T(8,128)(2,1)S(1)} %get-tuple-element.133), channel_id=1, source_target_pairs={{0,66},{1,67},{2,64},{3,65},{4,70},{5,71},{6,68},{7,69},{8,74},{9,... | collective-permute-start | bytes 1769480 | tf_op jit(solution)/shard_map/ppermute | solution.py:42
  94.0 14.8 %collective-permute-start.19 = (bf16[2,128,384]{2,1,0:T(8,128)(2,1)S(1)}, bf16[2,128,384]{2,1,0:T(8,128)(2,1)S(1)}, u32[]{:S(2)}, u32[]{:S(2)}) collective-permute-start(bf16[2,128,384]{2,1,0:T(8,128)(2,1)S(1)} %attend.2.refs_0_), channel_id=1, source_target_pairs={{0,2},{1,3},{2,0},{3,1},{4,6},{5,7},{6,4},{7,5},{8,10},{9,11},{10,... | collective-permute-start | bytes 589832 | tf_op jit(solution)/shard_map/ppermute | solution.py:42
  114.2 59.1 %collective-permute-start.50 = (bf16[384,768]{1,0:T(8,128)(2,1)S(1)}, bf16[384,768]{1,0:T(8,128)(2,1)S(1)}, u32[]{:S(2)}, u32[]{:S(2)}) collective-permute-start(bf16[384,768]{1,0:T(8,128)(2,1)S(1)} %collective-permute-done.47.refs_0_), channel_id=1, source_target_pairs={{0,8},{1,9},{2,10},{3,11},{4,12},{5,13},{6,14},{7,15},{8,0},{9,1},... | collective-permute-start | bytes 1769480 | tf_op jit(solution)/shard_map/ppermute | solution.py:42
  116.9 56.4 %collective-permute-start.49 = (bf16[384,768]{1,0:T(8,128)(2,1)S(1)}, bf16[384,768]{1,0:T(8,128)(2,1)S(1)}, u32[]{:S(2)}, u32[]{:S(2)}) collective-permute-start(bf16[384,768]{1,0:T(8,128)(2,1)S(1)} %collective-permute-done.47.refs_0_), channel_id=1, source_target_pairs={{0,12},{1,13},{2,14},{3,15},{4,0},{5,1},{6,2},{7,3},{8,4},{9,5},{1... | collective-permute-start | bytes 1769480 | tf_op jit(solution)/shard_map/ppermute | solution.py:42
  118.1 55.7 %collective-permute-start.48 = (bf16[384,768]{1,0:T(8,128)(2,1)S(1)}, bf16[384,768]{1,0:T(8,128)(2,1)S(1)}, u32[]{:S(2)}, u32[]{:S(2)}) collective-permute-start(bf16[384,768]{1,0:T(8,128)(2,1)S(1)} %collective-permute-done.47.refs_0_), channel_id=1, source_target_pairs={{0,4},{1,5},{2,6},{3,7},{4,8},{5,9},{6,10},{7,11},{8,12},{9,13},{1... | collective-permute-start | bytes 1769480 | tf_op jit(solution)/shard_map/ppermute | solution.py:42
  145.0 10.9 %collective-permute-start.35 = (bf16[2,1,2,16,384]{4,3,2,1,0:T(8,128)(2,1)S(1)}, bf16[2,1,2,16,384]{4,3,2,1,0:T(8,128)(2,1)S(1)}, u32[]{:S(2)}, u32[]{:S(2)}) collective-permute-start(bf16[2,1,2,16,384]{4,3,2,1,0:T(8,128)(2,1)S(1)} %pack.8.refs_0_), channel_id=1, source_target_pairs={{0,8},{1,9},{2,10},{3,11},{4,12},{5,13},{6,14},{7,15},{8,0},{9,1},... | collective-permute-start | bytes 147464 | tf_op jit(solution)/shard_map/ppermute | solution.py:42
  146.1 11.9 %collective-permute-start.37 = (bf16[4,32,384]{2,1,0:T(8,128)(2,1)S(1)}, bf16[4,32,384]{2,1,0:T(8,128)(2,1)S(1)}, u32[]{:S(2)}, u32[]{:S(2)}) collective-permute-start(bf16[4,32,384]{2,1,0:T(8,128)(2,1)S(1)} %pack.11), channel_id=1, source_target_pairs={{2,6},{3,7},{4,0},{5,1},{6,10},{7,11},{8,4},{9,5},{10,14},{11,15},... | collective-permute-start | bytes 294920 | tf_op jit(solution)/shard_map/ppermute | solution.py:42
  155.9 12.2 %collective-permute-start.36 = (bf16[4,32,384]{2,1,0:T(8,128)(2,1)S(1)}, bf16[4,32,384]{2,1,0:T(8,128)(2,1)S(1)}, u32[]{:S(2)}, u32[]{:S(2)}) collective-permute-start(bf16[4,32,384]{2,1,0:T(8,128)(2,1)S(1)} %pack.10), channel_id=1, source_target_pairs={{0,4},{1,5},{4,8},{5,9},{6,2},{7,3},{8,12},{9,13},{10,6},{11,7},{1... | collective-permute-start | bytes 294920 | tf_op jit(solution)/shard_map/ppermute | solution.py:42
  158.1 16.3 %collective-permute-start.38 = (bf16[8,1,2,16,384]{4,3,2,1,0:T(8,128)(2,1)S(1)}, bf16[8,1,2,16,384]{4,3,2,1,0:T(8,128)(2,1)S(1)}, u32[]{:S(2)}, u32[]{:S(2)}) collective-permute-start(bf16[8,1,2,16,384]{4,3,2,1,0:T(8,128)(2,1)S(1)} %pack.9.refs_7_), channel_id=1, source_target_pairs={{0,16},{1,17},{2,18},{3,19},{4,20},{5,21},{6,22},{7,23},{8,24},{9,... | collective-permute-start | bytes 589832 | tf_op jit(solution)/shard_map/ppermute | solution.py:42
  173.3 20.8 %collective-permute-start.54 = (bf16[384,768]{1,0:T(8,128)(2,1)S(1)}, bf16[384,768]{1,0:T(8,128)(2,1)S(1)}, u32[]{:S(2)}, u32[]{:S(2)}) collective-permute-start(bf16[384,768]{1,0:T(8,128)(2,1)S(1)} %collective-permute-done.50.refs_3_), channel_id=1, source_target_pairs={{0,1},{1,0},{2,3},{3,2},{4,5},{5,4},{6,7},{7,6},{8,9},{9,8},{10,11... | collective-permute-start | bytes 1769480 | tf_op jit(solution)/shard_map/ppermute | solution.py:42
  173.4 22.5 %collective-permute-start.53 = (bf16[384,768]{1,0:T(8,128)(2,1)S(1)}, bf16[384,768]{1,0:T(8,128)(2,1)S(1)}, u32[]{:S(2)}, u32[]{:S(2)}) collective-permute-start(bf16[384,768]{1,0:T(8,128)(2,1)S(1)} %collective-permute-done.49.refs_2_), channel_id=1, source_target_pairs={{0,1},{1,0},{2,3},{3,2},{4,5},{5,4},{6,7},{7,6},{8,9},{9,8},{10,11... | collective-permute-start | bytes 1769480 | tf_op jit(solution)/shard_map/ppermute | solution.py:42
  173.8 22.3 %collective-permute-start.52 = (bf16[384,768]{1,0:T(8,128)(2,1)S(1)}, bf16[384,768]{1,0:T(8,128)(2,1)S(1)}, u32[]{:S(2)}, u32[]{:S(2)}) collective-permute-start(bf16[384,768]{1,0:T(8,128)(2,1)S(1)} %collective-permute-done.48.refs_1_), channel_id=1, source_target_pairs={{0,1},{1,0},{2,3},{3,2},{4,5},{5,4},{6,7},{7,6},{8,9},{9,8},{10,11... | collective-permute-start | bytes 1769480 | tf_op jit(solution)/shard_map/ppermute | solution.py:42
  173.9 22.4 %collective-permute-start.51 = (bf16[384,768]{1,0:T(8,128)(2,1)S(1)}, bf16[384,768]{1,0:T(8,128)(2,1)S(1)}, u32[]{:S(2)}, u32[]{:S(2)}) collective-permute-start(bf16[384,768]{1,0:T(8,128)(2,1)S(1)} %collective-permute-done.47.refs_0_), channel_id=1, source_target_pairs={{0,1},{1,0},{2,3},{3,2},{4,5},{5,4},{6,7},{7,6},{8,9},{9,8},{10,11... | collective-permute-start | bytes 1769480 | tf_op jit(solution)/shard_map/ppermute | solution.py:42
  181.3 7.6 %collective-permute-start.40 = (bf16[8,1,2,16,384]{4,3,2,1,0:T(8,128)(2,1)S(1)}, bf16[8,1,2,16,384]{4,3,2,1,0:T(8,128)(2,1)S(1)}, u32[]{:S(2)}, u32[]{:S(2)}) collective-permute-start(bf16[8,1,2,16,384]{4,3,2,1,0:T(8,128)(2,1)S(1)} %pack.9.refs_7_), channel_id=1, source_target_pairs={{0,32},{1,33},{2,34},{3,35},{4,36},{5,37},{6,38},{7,39},{8,40},{9,... | collective-permute-start | bytes 589832 | tf_op jit(solution)/shard_map/ppermute | solution.py:42
  196.2 7.7 %collective-permute-start.42 = (bf16[128,384]{1,0:T(8,128)(2,1)S(1)}, bf16[128,384]{1,0:T(8,128)(2,1)S(1)}, u32[]{:S(2)}, u32[]{:S(2)}) collective-permute-start(bf16[128,384]{1,0:T(8,128)(2,1)S(1)} %get-tuple-element.125), channel_id=1, source_target_pairs={{0,2},{1,3},{2,0},{3,1},{4,6},{5,7},{6,4},{7,5},{8,10},{9,11},{10,... | collective-permute-start | bytes 294920 | tf_op jit(solution)/shard_map/ppermute | solution.py:42
  196.4 8.7 %collective-permute-start.43 = (bf16[128,384]{1,0:T(8,128)(2,1)S(1)}, bf16[128,384]{1,0:T(8,128)(2,1)S(1)}, u32[]{:S(2)}, u32[]{:S(2)}) collective-permute-start(bf16[128,384]{1,0:T(8,128)(2,1)S(1)} %get-tuple-element.126), channel_id=1, source_target_pairs={{0,3},{1,2},{2,1},{3,0},{4,7},{5,6},{6,5},{7,4},{8,11},{9,10},{10,... | collective-permute-start | bytes 294920 | tf_op jit(solution)/shard_map/ppermute | solution.py:42
  (33 other events, 285.9 us)

commit v3 on v2

--- a/solution.py
+++ b/solution.py
@@ -605,7 +605,7 @@
     x3b = send(after(x2b, own1[0]), to_sib)
     halves = (after(x2a, ky), x2b, x3a, x3b)
     par0 = qkv(0, 1, halves, norm_gain, w, qk_gain)
-    eo, ep = edges(own0, par0)
+    eo, ep = edges((None, after(own0[1], par0[0])), par0)
     wsib = send(after(w_out, par0[0]), to_sib)
     ctx = [ky] + kys
     ao = attend(0, 0, halo_frames, own0[0], par0[2], eo, ctx)
@@ -618,8 +618,8 @@
     halves = (after(x2a, ap), x2b, x3a, x3b)
     par1 = qkv(1, 1, halves, norm_gain, w, qk_gain)
     wzs0 = [send(after(p, ap), to_sib) for p in wz0[:3]]
+    wz1 = [here1] + [send(after(here1, par1[0]), to_x(d)) for d in (1, 3, 2)]
     wzs0.append(send(after(wz0[3], par1[0]), to_sib))
-    wz1 = [here1] + [send(after(here1, par1[0]), to_x(d)) for d in (1, 3, 2)]
     ozs = send(after(oz, par1[0]), to_sib)
     wslot0 = assemble(0, after(w_out, par1[0]), wsib, wz0, wzs0)
     pzs = send(pz, to_sib)
@@ -638,7 +638,8 @@
     both_par = pack(par1[1], fp[1])
     fx = pack(fkv, fz)
     fxs = [send(fx, to_x(d)) for d in (1, 3, 2)]
-    so, sp = edges((None, after(both_own, fx)), (None, after(both_par, fx)))
+    sp = send(both_own, edge_own)
+    so = send(after(both_par, fx), edge_par)
     fy = pack(fx, *fxs)
     fys = [send(fy, to_y(d)) for d in (1, 3, 2)]
     mine = (after(own1[0], fy),) + own1[1:]

time: 211 us -> 219 us (1.038)
  waiting for transfers between devices: 92.4 us -> 98.2 us
    ppermute x55, waiting for transfers between devices: 92.4 us -> 98.2 us  [send(): return lax.ppermute(value, AXES, pairs)]
  transfers between devices with their start and end apart: 55 -> 55, of which waited for: 21 -> 21; matrix products, arithmetic and copies ran while one was open for 0% -> 0% of each run, Pallas kernels for 23% -> 22%
where the time goes in v3:
time: 219 us; the launch traced here: 218 us
  waiting for transfers between devices  98.2 us (45%)
  Pallas kernels  59.6 us (27%)
  starting transfers between devices  58.6 us (27%)
    ppermute x55, waiting for transfers between devices, send(): return lax.ppermute(value, AXES, pairs)  98.2 us
    ppermute x55, starting transfers between devices, send(): return lax.ppermute(value, AXES, pairs)  58.6 us
    pallas_call x1, Pallas kernels, first_qkv(): pl.pallas_call(first_kernel, out_shape=(shape(BLK, D),) + one + one + (sh...  13.5 us
    pallas_call x4, Pallas kernels, qkv(): pl.pallas_call(functools.partial(qkv_kernel, l, which), out_shape=(shape(...  12.4 us
    pallas_call x2, Pallas kernels, attend_pair(): pl.pallas_call(functools.partial(attend_pair_kernel, cl, at), out_shape=(...  10.2 us
    pallas_call x2, Pallas kernels, attend(): pl.pallas_call(functools.partial(attend_kernel, cl, which), out_shape=sha...  5.68 us
    pallas_call x1, Pallas kernels, stage(): pl.pallas_call(stage_kernel, out_shape=pltpu.VMEM((2, D, 3 * INNER), BF16...  5.17 us
    pallas_call x1, Pallas kernels, final(): pl.pallas_call(final_kernel, out_shape=shape(BLK, D), in_specs=[SM] + [VM...  4.89 us
  transfers between devices with their start and end apart: 55, of which 21 were waited for; matrix products, arithmetic and copies ran while one was open for 0% of the time, Pallas kernels for 22%

profile of v3, /device:TPU:64, one launch (start us, length us, event | category | flops | bytes accessed | tf_op | source)
XLA Modules:
  0.0 218.2 jit_solution(3784427303712605589)
XLA Ops:
  5.5 5.2 %stage.1.w.refs_4_.refs_5_.refs_17_ = bf16[2,3072,1152]{2,1,0:T(8,128)(2,1)S(1)} custom-call(bf16[2,3,3072,384]{3,2,1,0:T(8,128)(2,1)} %bitcast.3), custom_call_target="tpu_custom_call" | custom-call | tf_op jit(solution)/shard_map/stage/pallas_call | solution.py:130
  14.6 3.1 %qkv.4 = (bf16[3,256,384]{2,1,0:T(8,128)(2,1)S(1)}, bf16[2,32,384]{2,1,0:T(8,128)(2,1)S(1)}, bf16[2,32,384]{2,1,0:T(8,128)(2,1)S(1)}) custom-call(bf16[64,3072]{1,0:T(8,128)(2,1)S(1)} %get-tuple-element.81.refs_0_.refs_8_.refs_9_, bf16[64,3072]{1,0:T(8,128)(2,1)S(1)} %get-tuple-element.87.refs_1_.refs_9_.refs_10_, ...), custom_call_target="tpu_custom_call" | custom-call | flops 1811939328 | bytes 8650752 | tf_op jit(solution)/shard_map/qkv/pallas_call | solution.py:302
  17.7 15.4 %collective-permute-done.5.refs_1_ = bf16[1,2,2,16,384]{4,3,2,1,0:T(8,128)(2,1)S(1)} collective-permute-done((bf16[1,2,2,16,384]{4,3,2,1,0:T(8,128)(2,1)S(1)}, bf16[1,2,2,16,384]{4,3,2,1,0:T(8,128)(2,1)S(1)}, u32[]{:S(2)}, u32[]{:S(2)}) %collective-permute-start.5) | collective-permute-done | bytes 49184 | tf_op jit(solution)/shard_map/ppermute | solution.py:42
  33.1 3.1 %qkv.5 = (bf16[3,256,384]{2,1,0:T(8,128)(2,1)S(1)}, bf16[2,32,384]{2,1,0:T(8,128)(2,1)S(1)}, bf16[2,32,384]{2,1,0:T(8,128)(2,1)S(1)}) custom-call(bf16[64,3072]{1,0:T(8,128)(2,1)S(1)} %get-tuple-element.81.refs_0_.refs_8_.refs_9_, bf16[64,3072]{1,0:T(8,128)(2,1)S(1)} %get-tuple-element.87.refs_1_.refs_9_.refs_10_, ...), custom_call_target="tpu_custom_call" | custom-call | flops 1811939328 | bytes 8650752 | tf_op jit(solution)/shard_map/qkv/pallas_call | solution.py:302
  36.9 3.0 %collective-permute-start.8 = (bf16[2,2,2,16,384]{4,3,2,1,0:T(8,128)(2,1)S(1)}, bf16[2,2,2,16,384]{4,3,2,1,0:T(8,128)(2,1)S(1)}, u32[]{:S(2)}, u32[]{:S(2)}) collective-permute-start(bf16[2,2,2,16,384]{4,3,2,1,0:T(8,128)(2,1)S(1)} %pack.6.refs_0_), channel_id=1, source_target_pairs={{0,8},{1,9},{2,10},{3,11},{4,12},{5,13},{6,14},{7,15},{8,0},{9,1},... | collective-permute-start | bytes 294920 | tf_op jit(solution)/shard_map/ppermute | solution.py:42
  43.4 2.0 collective-permute-done.7.refs_2_
  46.9 3.1 %qkv.6 = (bf16[3,256,384]{2,1,0:T(8,128)(2,1)S(1)}, bf16[2,32,384]{2,1,0:T(8,128)(2,1)S(1)}, bf16[2,32,384]{2,1,0:T(8,128)(2,1)S(1)}) custom-call(bf16[64,3072]{1,0:T(8,128)(2,1)S(1)} %collective-permute-done.4.refs_0_.refs_11_, bf16[64,3072]{1,0:T(8,128)(2,1)S(1)} %collective-permute-done.9.refs_1_.refs_12_, ...), custom_call_target="tpu_custom_call" | custom-call | flops 1811939328 | bytes 8650752 | tf_op jit(solution)/shard_map/qkv/pallas_call | solution.py:302
  50.2 2.0 collective-permute-start.24
  55.4 2.0 collective-permute-start.15
  57.4 8.7 %collective-permute-done.24.refs_0_ = bf16[384,768]{1,0:T(8,128)(2,1)S(1)} collective-permute-done((bf16[384,768]{1,0:T(8,128)(2,1)S(1)}, bf16[384,768]{1,0:T(8,128)(2,1)S(1)}, u32[]{:S(2)}, u32[]{:S(2)}) %collective-permute-start.24) | collective-permute-done | bytes 589856 | tf_op jit(solution)/shard_map/ppermute | solution.py:42
  68.0 9.8 %collective-permute-done.12.outer = bf16[2,32,384]{2,1,0:T(8,128)(2,1)S(1)} collective-permute-done((bf16[2,32,384]{2,1,0:T(8,128)(2,1)S(1)}, bf16[2,32,384]{2,1,0:T(8,128)(2,1)S(1)}, u32[]{:S(2)}, u32[]{:S(2)}) %collective-permute-start.12) | collective-permute-done | bytes 49184 | tf_op jit(solution)/shard_map/ppermute | solution.py:42
  77.8 2.0 collective-permute-start.25
  79.8 2.8 %attend.2.refs_0_ = bf16[2,128,384]{2,1,0:T(8,128)(2,1)S(1)} custom-call(s32[2]{0:T(128)S(1)} %copy-done.4, bf16[3,256,384]{2,1,0:T(8,128)(2,1)S(1)} %get-tuple-element.79.mine, bf16[2,32,384]{2,1,0:T(8,128)(2,1)S(1)} %get-tuple-element.90.inner, bf16[2,32,384]{2,1,0:T(8,128)(2,1)S(1)} %collective-permute-done.12.outer, ...), custom_call_target="tpu_custom_call" | custom-call | flops 490733568 | bytes 1671168 | tf_op jit(solution)/shard_map/attend/pallas_call | solution.py:385
  82.9 11.1 %collective-permute-done.26.refs_2_ = bf16[384,768]{1,0:T(8,128)(2,1)S(1)} collective-permute-done((bf16[384,768]{1,0:T(8,128)(2,1)S(1)}, bf16[384,768]{1,0:T(8,128)(2,1)S(1)}, u32[]{:S(2)}, u32[]{:S(2)}) %collective-permute-start.26) | collective-permute-done | bytes 589856 | tf_op jit(solution)/shard_map/ppermute | solution.py:42
  94.0 7.0 %collective-permute-start.16 = (bf16[2,32,384]{2,1,0:T(8,128)(2,1)S(1)}, bf16[2,32,384]{2,1,0:T(8,128)(2,1)S(1)}, u32[]{:S(2)}, u32[]{:S(2)}) collective-permute-start(bf16[2,32,384]{2,1,0:T(8,128)(2,1)S(1)} %get-tuple-element.96), channel_id=1, source_target_pairs={{2,6},{3,7},{4,0},{5,1},{6,10},{7,11},{8,4},{9,5},{10,14},{11,15},... | collective-permute-start | bytes 147464 | tf_op jit(solution)/shard_map/ppermute | solution.py:42
  101.0 2.6 %collective-permute-done.16.outer = bf16[2,32,384]{2,1,0:T(8,128)(2,1)S(1)} collective-permute-done((bf16[2,32,384]{2,1,0:T(8,128)(2,1)S(1)}, bf16[2,32,384]{2,1,0:T(8,128)(2,1)S(1)}, u32[]{:S(2)}, u32[]{:S(2)}) %collective-permute-start.16) | collective-permute-done | bytes 49184 | tf_op jit(solution)/shard_map/ppermute | solution.py:42
  103.6 12.6 %collective-permute-start.19 = (bf16[2,128,384]{2,1,0:T(8,128)(2,1)S(1)}, bf16[2,128,384]{2,1,0:T(8,128)(2,1)S(1)}, u32[]{:S(2)}, u32[]{:S(2)}) collective-permute-start(bf16[2,128,384]{2,1,0:T(8,128)(2,1)S(1)} %attend.2.refs_0_), channel_id=1, source_target_pairs={{0,2},{1,3},{2,0},{3,1},{4,6},{5,7},{6,4},{7,5},{8,10},{9,11},{10,... | collective-permute-start | bytes 589832 | tf_op jit(solution)/shard_map/ppermute | solution.py:42
  116.2 2.8 %attend.3.refs_1_ = bf16[2,128,384]{2,1,0:T(8,128)(2,1)S(1)} custom-call(s32[2]{0:T(128)S(1)} %copy-done.4, bf16[3,256,384]{2,1,0:T(8,128)(2,1)S(1)} %get-tuple-element.93.mine, bf16[2,32,384]{2,1,0:T(8,128)(2,1)S(1)} %get-tuple-element.94.inner, bf16[2,32,384]{2,1,0:T(8,128)(2,1)S(1)} %collective-permute-done.16.outer, ...), custom_call_target="tpu_custom_call" | custom-call | flops 490733568 | bytes 1671168 | tf_op jit(solution)/shard_map/attend/pallas_call | solution.py:385
  119.1 3.1 %qkv.7 = (bf16[3,256,384]{2,1,0:T(8,128)(2,1)S(1)}, bf16[2,32,384]{2,1,0:T(8,128)(2,1)S(1)}, bf16[2,32,384]{2,1,0:T(8,128)(2,1)S(1)}) custom-call(bf16[64,3072]{1,0:T(8,128)(2,1)S(1)} %collective-permute-done.4.refs_0_.refs_11_, bf16[64,3072]{1,0:T(8,128)(2,1)S(1)} %collective-permute-done.9.refs_1_.refs_12_, ...), custom_call_target="tpu_custom_call" | custom-call | flops 1811939328 | bytes 8650752 | tf_op jit(solution)/shard_map/qkv/pallas_call | solution.py:302
  129.9 2.0 collective-permute-start.48
  132.0 13.5 %first_qkv.1 = (bf16[128,3072]{1,0:T(8,128)(2,1)S(1)}, bf16[3,256,384]{2,1,0:T(8,128)(2,1)S(1)}, bf16[2,32,384]{2,1,0:T(8,128)(2,1)S(1)}, bf16[2,32,384]{2,1,0:T...) custom-call(bf16[2,128,384]{2,1,0:T(8,128)(2,1)S(1)} %attend.2.refs_, ...), custom_call_target="tpu_custom_call" | custom-call | flops 8455716864 | bytes 22806528 | tf_op jit(solution)/shard_map/first_qkv/pallas_call | solution.py:490
  145.6 5.3 %collective-permute-done.32.refs_1_ = bf16[1,1,2,16,384]{4,3,2,1,0:T(8,128)(2,1)S(1)} collective-permute-done((bf16[1,1,2,16,384]{4,3,2,1,0:T(8,128)(2,1)S(1)}, bf16[1,1,2,16,384]{4,3,2,1,0:T(8,128)(2,1)S(1)}, u32[]{:S(2)}, u32[]{:S(2)}) %collective-permute-start.32) | collective-permute-done | bytes 24608 | tf_op jit(solution)/shard_map/ppermute | solution.py:42
  152.2 2.0 collective-permute-start.34
  154.2 4.4 %collective-permute-done.33.refs_1_ = bf16[2,1,2,16,384]{4,3,2,1,0:T(8,128)(2,1)S(1)} collective-permute-done((bf16[2,1,2,16,384]{4,3,2,1,0:T(8,128)(2,1)S(1)}, bf16[2,1,2,16,384]{4,3,2,1,0:T(8,128)(2,1)S(1)}, u32[]{:S(2)}, u32[]{:S(2)}) %collective-permute-start.33) | collective-permute-done | bytes 49184 | tf_op jit(solution)/shard_map/ppermute | solution.py:42
  158.9 3.3 %collective-permute-start.37 = (bf16[4,32,384]{2,1,0:T(8,128)(2,1)S(1)}, bf16[4,32,384]{2,1,0:T(8,128)(2,1)S(1)}, u32[]{:S(2)}, u32[]{:S(2)}) collective-permute-start(bf16[4,32,384]{2,1,0:T(8,128)(2,1)S(1)} %pack.11), channel_id=1, source_target_pairs={{2,6},{3,7},{4,0},{5,1},{6,10},{7,11},{8,4},{9,5},{10,14},{11,15},... | collective-permute-start | bytes 294920 | tf_op jit(solution)/shard_map/ppermute | solution.py:42
  166.2 10.2 %collective-permute-done.36.refs_3_ = bf16[4,32,384]{2,1,0:T(8,128)(2,1)S(1)} collective-permute-done((bf16[4,32,384]{2,1,0:T(8,128)(2,1)S(1)}, bf16[4,32,384]{2,1,0:T(8,128)(2,1)S(1)}, u32[]{:S(2)}, u32[]{:S(2)}) %collective-permute-start.36) | collective-permute-done | bytes 98336 | tf_op jit(solution)/shard_map/ppermute | solution.py:42
  176.4 5.1 %attend_pair.2 = (bf16[128,384]{1,0:T(8,128)(2,1)S(1)}, bf16[128,384]{1,0:T(8,128)(2,1)S(1)}, bf16[128,384]{1,0:T(8,128)(2,1)S(1)}, bf16[128,384]{1,0:T(8,128)(2,1)S(1)}) custom-call(s32[2]{0:T(128)S(1)} %copy-done.4, bf16[3,256,384]{2,1,0:T(8,128)(2,1)S(1)} %get-tuple-element.110.refs_1_, bf16[2,32,384]{2,1,0:T(8,128)(2,1)S(1)} %get-tuple-element.111.refs_2_, ...), custom_call_target="tpu_custom_call" | custom-call | flops 981467136 | bytes 2064384 | tf_op jit(solution)/shard_map/attend_pair/pallas_call | solution.py:412
  182.6 6.9 %collective-permute-done.39.refs_9_ = bf16[8,1,2,16,384]{4,3,2,1,0:T(8,128)(2,1)S(1)} collective-permute-done((bf16[8,1,2,16,384]{4,3,2,1,0:T(8,128)(2,1)S(1)}, bf16[8,1,2,16,384]{4,3,2,1,0:T(8,128)(2,1)S(1)}, u32[]{:S(2)}, u32[]{:S(2)}) %collective-permute-start.39) | collective-permute-done | bytes 196640 | tf_op jit(solution)/shard_map/ppermute | solution.py:42
  189.5 7.6 %collective-permute-done.40.refs_10_ = bf16[8,1,2,16,384]{4,3,2,1,0:T(8,128)(2,1)S(1)} collective-permute-done((bf16[8,1,2,16,384]{4,3,2,1,0:T(8,128)(2,1)S(1)}, bf16[8,1,2,16,384]{4,3,2,1,0:T(8,128)(2,1)S(1)}, u32[]{:S(2)}, u32[]{:S(2)}) %collective-permute-start.40) | collective-permute-done | bytes 196640 | tf_op jit(solution)/shard_map/ppermute | solution.py:42
  197.1 5.1 %attend_pair.3 = (bf16[128,384]{1,0:T(8,128)(2,1)S(1)}, bf16[128,384]{1,0:T(8,128)(2,1)S(1)}, bf16[128,384]{1,0:T(8,128)(2,1)S(1)}, bf16[128,384]{1,0:T(8,128)(2,1)S(1)}) custom-call(s32[2]{0:T(128)S(1)} %copy-done.4, bf16[3,256,384]{2,1,0:T(8,128)(2,1)S(1)} %get-tuple-element.119.refs_1_, bf16[2,32,384]{2,1,0:T(8,128)(2,1)S(1)} %get-tuple-element.120.refs_2_, ...), custom_call_target="tpu_custom_call" | custom-call | flops 981467136 | bytes 2064384 | tf_op jit(solution)/shard_map/attend_pair/pallas_call | solution.py:412
  209.1 3.0 %collective-permute-done.42.refs_3_ = bf16[128,384]{1,0:T(8,128)(2,1)S(1)} collective-permute-done((bf16[128,384]{1,0:T(8,128)(2,1)S(1)}, bf16[128,384]{1,0:T(8,128)(2,1)S(1)}, u32[]{:S(2)}, u32[]{:S(2)}) %collective-permute-start.42) | collective-permute-done | bytes 98336 | tf_op jit(solution)/shard_map/ppermute | solution.py:42
  213.4 4.9 %final.1 = bf16[128,3072]{1,0:T(8,128)(2,1)} custom-call(s32[2]{0:T(128)S(1)} %copy-done.7, bf16[128,384]{1,0:T(8,128)(2,1)S(1)} %get-tuple-element.123.refs_1_, bf16[128,384]{1,0:T(8,128)(2,1)S(1)} %collective-permute-done.41.refs_2_, bf16[128,384]{1,0:T(8,128)(2,1)S(1)} %collective-permute-done.42.refs_3_, ...), custom_call_target="tpu_custom_call" | custom-call | flops 2415919104 | bytes 11796480 | tf_op jit(solution)/shard_map/final/pallas_call | solution.py:534
  (121 shorter events, 43.0 us)
Async XLA Ops:
  3.3 11.3 %collective-permute-start.3 = (bf16[128,3072]{1,0:T(8,128)(2,1)}, bf16[128,3072]{1,0:T(8,128)(2,1)S(1)}, u32[]{:S(2)}, u32[]{:S(2)}) collective-permute-start(bf16[128,3072]{1,0:T(8,128)(2,1)} %x), channel_id=1, source_target_pairs={{0,1},{1,0},{2,3},{3,2},{4,5},{5,4},{6,7},{7,6},{8,9},{9,8},{10,11... | collective-permute-start | bytes 2359304 | tf_op jit(solution)/shard_map/ppermute | solution.py:42
  3.4 7.3 %collective-permute-start = (bf16[4,3072]{1,0:T(4,128)(2,1)S(1)}, bf16[4,3072]{1,0:T(4,128)(2,1)S(1)}, u32[]{:S(2)}, u32[]{:S(2)}) collective-permute-start(bf16[4,3072]{1,0:T(4,128)(2,1)S(1)} %get-tuple-element.75.c0), channel_id=1, source_target_pairs={{0,1},{1,0},{2,3},{3,2},{4,5},{5,4},{6,7},{7,6},{8,9},{9,8},{10,11... | collective-permute-start | bytes 73736 | tf_op jit(solution)/shard_map/ppermute | solution.py:42
  12.5 23.7 %collective-permute-start.9 = (bf16[64,3072]{1,0:T(8,128)(2,1)S(1)}, bf16[64,3072]{1,0:T(8,128)(2,1)S(1)}, u32[]{:S(2)}, u32[]{:S(2)}) collective-permute-start(bf16[64,3072]{1,0:T(8,128)(2,1)S(1)} %get-tuple-element.87.refs_1_.refs_9_.refs_10_), channel_id=1, source_target_pairs={{0,2},{1,3},{2,0},{3,1},{4,6},{5,7},{6,4},{7,5},{8,10},{9,11},{10,... | collective-permute-start | bytes 1179656 | tf_op jit(solution)/shard_map/ppermute | solution.py:42
  14.0 22.4 %collective-permute-start.4 = (bf16[64,3072]{1,0:T(8,128)(2,1)S(1)}, bf16[64,3072]{1,0:T(8,128)(2,1)S(1)}, u32[]{:S(2)}, u32[]{:S(2)}) collective-permute-start(bf16[64,3072]{1,0:T(8,128)(2,1)S(1)} %get-tuple-element.81.refs_0_.refs_8_.refs_9_), channel_id=1, source_target_pairs={{0,2},{1,3},{2,0},{3,1},{4,6},{5,7},{6,4},{7,5},{8,10},{9,11},{10,... | collective-permute-start | bytes 1179656 | tf_op jit(solution)/shard_map/ppermute | solution.py:42
  14.6 18.5 %collective-permute-start.5 = (bf16[1,2,2,16,384]{4,3,2,1,0:T(8,128)(2,1)S(1)}, bf16[1,2,2,16,384]{4,3,2,1,0:T(8,128)(2,1)S(1)}, u32[]{:S(2)}, u32[]{:S(2)}) collective-permute-start(bf16[1,2,2,16,384]{4,3,2,1,0:T(8,128)(2,1)S(1)} %context_kv.1.refs_0_), channel_id=1, source_target_pairs={{0,64},{1,65},{2,66},{3,67},{4,68},{5,69},{6,70},{7,71},{8,72},{9,... | collective-permute-start | bytes 147464 | tf_op jit(solution)/shard_map/ppermute | solution.py:42
  36.3 10.6 %collective-permute-start.11 = (bf16[64,3072]{1,0:T(8,128)(2,1)S(1)}, bf16[64,3072]{1,0:T(8,128)(2,1)S(1)}, u32[]{:S(2)}, u32[]{:S(2)}) collective-permute-start(bf16[64,3072]{1,0:T(8,128)(2,1)S(1)} %collective-permute-done.9.refs_1_.refs_12_), channel_id=1, source_target_pairs={{0,1},{1,0},{2,3},{3,2},{4,5},{5,4},{6,7},{7,6},{8,9},{9,8},{10,11... | collective-permute-start | bytes 1179656 | tf_op jit(solution)/shard_map/ppermute | solution.py:42
  36.4 10.5 %collective-permute-start.10 = (bf16[64,3072]{1,0:T(8,128)(2,1)S(1)}, bf16[64,3072]{1,0:T(8,128)(2,1)S(1)}, u32[]{:S(2)}, u32[]{:S(2)}) collective-permute-start(bf16[64,3072]{1,0:T(8,128)(2,1)S(1)} %collective-permute-done.4.refs_0_.refs_11_), channel_id=1, source_target_pairs={{0,1},{1,0},{2,3},{3,2},{4,5},{5,4},{6,7},{7,6},{8,9},{9,8},{10,11... | collective-permute-start | bytes 1179656 | tf_op jit(solution)/shard_map/ppermute | solution.py:42
  50.1 77.7 %collective-permute-start.23 = (bf16[2,384,3072]{2,1,0:T(8,128)(2,1)S(1)}, bf16[2,384,3072]{2,1,0:T(8,128)(2,1)S(1)}, u32[]{:S(2)}, u32[]{:S(2)}) collective-permute-start(bf16[2,384,3072]{2,1,0:T(8,128)(2,1)S(1)} %bitcast.2), channel_id=1, source_target_pairs={{0,1},{1,0},{2,3},{3,2},{4,5},{5,4},{6,7},{7,6},{8,9},{9,8},{10,11... | collective-permute-start | bytes 14155784 | tf_op jit(solution)/shard_map/ppermute | solution.py:42
  50.2 15.9 %collective-permute-start.24 = (bf16[384,768]{1,0:T(8,128)(2,1)S(1)}, bf16[384,768]{1,0:T(8,128)(2,1)S(1)}, u32[]{:S(2)}, u32[]{:S(2)}) collective-permute-start(bf16[384,768]{1,0:T(8,128)(2,1)S(1)} %get-tuple-element.72), channel_id=1, source_target_pairs={{0,66},{1,67},{2,64},{3,65},{4,70},{5,71},{6,68},{7,69},{8,74},{9,... | collective-permute-start | bytes 1769480 | tf_op jit(solution)/shard_map/ppermute | solution.py:42
  52.2 25.6 %collective-permute-start.13 = (bf16[8,2,2,16,384]{4,3,2,1,0:T(8,128)(2,1)S(1)}, bf16[8,2,2,16,384]{4,3,2,1,0:T(8,128)(2,1)S(1)}, u32[]{:S(2)}, u32[]{:S(2)}) collective-permute-start(bf16[8,2,2,16,384]{4,3,2,1,0:T(8,128)(2,1)S(1)} %pack.7.c0.refs_7_), channel_id=1, source_target_pairs={{0,16},{1,17},{2,18},{3,19},{4,20},{5,21},{6,22},{7,23},{8,24},{9,... | collective-permute-start | bytes 1179656 | tf_op jit(solution)/shard_map/ppermute | solution.py:42
  53.8 26.1 %collective-permute-start.14 = (bf16[8,2,2,16,384]{4,3,2,1,0:T(8,128)(2,1)S(1)}, bf16[8,2,2,16,384]{4,3,2,1,0:T(8,128)(2,1)S(1)}, u32[]{:S(2)}, u32[]{:S(2)}) collective-permute-start(bf16[8,2,2,16,384]{4,3,2,1,0:T(8,128)(2,1)S(1)} %pack.7.c0.refs_7_), channel_id=1, source_target_pairs={{0,48},{1,49},{2,50},{3,51},{4,52},{5,53},{6,54},{7,55},{8,56},{9,... | collective-permute-start | bytes 1179656 | tf_op jit(solution)/shard_map/ppermute | solution.py:42
  55.4 24.4 %collective-permute-start.15 = (bf16[8,2,2,16,384]{4,3,2,1,0:T(8,128)(2,1)S(1)}, bf16[8,2,2,16,384]{4,3,2,1,0:T(8,128)(2,1)S(1)}, u32[]{:S(2)}, u32[]{:S(2)}) collective-permute-start(bf16[8,2,2,16,384]{4,3,2,1,0:T(8,128)(2,1)S(1)} %pack.7.c0.refs_7_), channel_id=1, source_target_pairs={{0,32},{1,33},{2,34},{3,35},{4,36},{5,37},{6,38},{7,39},{8,40},{9,... | collective-permute-start | bytes 1179656 | tf_op jit(solution)/shard_map/ppermute | solution.py:42
  66.1 11.7 %collective-permute-start.12 = (bf16[2,32,384]{2,1,0:T(8,128)(2,1)S(1)}, bf16[2,32,384]{2,1,0:T(8,128)(2,1)S(1)}, u32[]{:S(2)}, u32[]{:S(2)}) collective-permute-start(bf16[2,32,384]{2,1,0:T(8,128)(2,1)S(1)} %get-tuple-element.91), channel_id=1, source_target_pairs={{0,4},{1,5},{4,8},{5,9},{6,2},{7,3},{8,12},{9,13},{10,6},{11,7},{1... | collective-permute-start | bytes 147464 | tf_op jit(solution)/shard_map/ppermute | solution.py:42
  77.8 16.2 %collective-permute-start.26 = (bf16[384,768]{1,0:T(8,128)(2,1)S(1)}, bf16[384,768]{1,0:T(8,128)(2,1)S(1)}, u32[]{:S(2)}, u32[]{:S(2)}) collective-permute-start(bf16[384,768]{1,0:T(8,128)(2,1)S(1)} %collective-permute-done.24.refs_0_), channel_id=1, source_target_pairs={{0,48},{1,49},{2,50},{3,51},{4,52},{5,53},{6,54},{7,55},{8,56},{9,... | collective-permute-start | bytes 1769480 | tf_op jit(solution)/shard_map/ppermute | solution.py:42
  77.8 41.2 %collective-permute-start.25 = (bf16[384,768]{1,0:T(8,128)(2,1)S(1)}, bf16[384,768]{1,0:T(8,128)(2,1)S(1)}, u32[]{:S(2)}, u32[]{:S(2)}) collective-permute-start(bf16[384,768]{1,0:T(8,128)(2,1)S(1)} %collective-permute-done.24.refs_0_), channel_id=1, source_target_pairs={{0,16},{1,17},{2,18},{3,19},{4,20},{5,21},{6,22},{7,23},{8,24},{9,... | collective-permute-start | bytes 1769480 | tf_op jit(solution)/shard_map/ppermute | solution.py:42
  82.7 39.6 %collective-permute-start.27 = (bf16[384,768]{1,0:T(8,128)(2,1)S(1)}, bf16[384,768]{1,0:T(8,128)(2,1)S(1)}, u32[]{:S(2)}, u32[]{:S(2)}) collective-permute-start(bf16[384,768]{1,0:T(8,128)(2,1)S(1)} %collective-permute-done.24.refs_0_), channel_id=1, source_target_pairs={{0,32},{1,33},{2,34},{3,35},{4,36},{5,37},{6,38},{7,39},{8,40},{9,... | collective-permute-start | bytes 1769480 | tf_op jit(solution)/shard_map/ppermute | solution.py:42
  82.8 42.0 %collective-permute-start.47 = (bf16[384,768]{1,0:T(8,128)(2,1)S(1)}, bf16[384,768]{1,0:T(8,128)(2,1)S(1)}, u32[]{:S(2)}, u32[]{:S(2)}) collective-permute-start(bf16[384,768]{1,0:T(8,128)(2,1)S(1)} %get-tuple-element.133), channel_id=1, source_target_pairs={{0,66},{1,67},{2,64},{3,65},{4,70},{5,71},{6,68},{7,69},{8,74},{9,... | collective-permute-start | bytes 1769480 | tf_op jit(solution)/shard_map/ppermute | solution.py:42
  94.0 9.6 %collective-permute-start.16 = (bf16[2,32,384]{2,1,0:T(8,128)(2,1)S(1)}, bf16[2,32,384]{2,1,0:T(8,128)(2,1)S(1)}, u32[]{:S(2)}, u32[]{:S(2)}) collective-permute-start(bf16[2,32,384]{2,1,0:T(8,128)(2,1)S(1)} %get-tuple-element.96), channel_id=1, source_target_pairs={{2,6},{3,7},{4,0},{5,1},{6,10},{7,11},{8,4},{9,5},{10,14},{11,15},... | collective-permute-start | bytes 147464 | tf_op jit(solution)/shard_map/ppermute | solution.py:42
  103.6 18.7 %collective-permute-start.19 = (bf16[2,128,384]{2,1,0:T(8,128)(2,1)S(1)}, bf16[2,128,384]{2,1,0:T(8,128)(2,1)S(1)}, u32[]{:S(2)}, u32[]{:S(2)}) collective-permute-start(bf16[2,128,384]{2,1,0:T(8,128)(2,1)S(1)} %attend.2.refs_0_), channel_id=1, source_target_pairs={{0,2},{1,3},{2,0},{3,1},{4,6},{5,7},{6,4},{7,5},{8,10},{9,11},{10,... | collective-permute-start | bytes 589832 | tf_op jit(solution)/shard_map/ppermute | solution.py:42
  127.8 53.7 %collective-permute-start.50 = (bf16[384,768]{1,0:T(8,128)(2,1)S(1)}, bf16[384,768]{1,0:T(8,128)(2,1)S(1)}, u32[]{:S(2)}, u32[]{:S(2)}) collective-permute-start(bf16[384,768]{1,0:T(8,128)(2,1)S(1)} %collective-permute-done.47.refs_0_), channel_id=1, source_target_pairs={{0,8},{1,9},{2,10},{3,11},{4,12},{5,13},{6,14},{7,15},{8,0},{9,1},... | collective-permute-start | bytes 1769480 | tf_op jit(solution)/shard_map/ppermute | solution.py:42
  129.9 51.7 %collective-permute-start.49 = (bf16[384,768]{1,0:T(8,128)(2,1)S(1)}, bf16[384,768]{1,0:T(8,128)(2,1)S(1)}, u32[]{:S(2)}, u32[]{:S(2)}) collective-permute-start(bf16[384,768]{1,0:T(8,128)(2,1)S(1)} %collective-permute-done.47.refs_0_), channel_id=1, source_target_pairs={{0,12},{1,13},{2,14},{3,15},{4,0},{5,1},{6,2},{7,3},{8,4},{9,5},{1... | collective-permute-start | bytes 1769480 | tf_op jit(solution)/shard_map/ppermute | solution.py:42
  129.9 52.2 %collective-permute-start.48 = (bf16[384,768]{1,0:T(8,128)(2,1)S(1)}, bf16[384,768]{1,0:T(8,128)(2,1)S(1)}, u32[]{:S(2)}, u32[]{:S(2)}) collective-permute-start(bf16[384,768]{1,0:T(8,128)(2,1)S(1)} %collective-permute-done.47.refs_0_), channel_id=1, source_target_pairs={{0,4},{1,5},{2,6},{3,7},{4,8},{5,9},{6,10},{7,11},{8,12},{9,13},{1... | collective-permute-start | bytes 1769480 | tf_op jit(solution)/shard_map/ppermute | solution.py:42
  150.9 7.6 %collective-permute-start.33 = (bf16[2,1,2,16,384]{4,3,2,1,0:T(8,128)(2,1)S(1)}, bf16[2,1,2,16,384]{4,3,2,1,0:T(8,128)(2,1)S(1)}, u32[]{:S(2)}, u32[]{:S(2)}) collective-permute-start(bf16[2,1,2,16,384]{4,3,2,1,0:T(8,128)(2,1)S(1)} %pack.8.refs_0_), channel_id=1, source_target_pairs={{0,4},{1,5},{2,6},{3,7},{4,8},{5,9},{6,10},{7,11},{8,12},{9,13},{1... | collective-permute-start | bytes 147464 | tf_op jit(solution)/shard_map/ppermute | solution.py:42
  164.2 12.2 %collective-permute-start.36 = (bf16[4,32,384]{2,1,0:T(8,128)(2,1)S(1)}, bf16[4,32,384]{2,1,0:T(8,128)(2,1)S(1)}, u32[]{:S(2)}, u32[]{:S(2)}) collective-permute-start(bf16[4,32,384]{2,1,0:T(8,128)(2,1)S(1)} %pack.10), channel_id=1, source_target_pairs={{0,4},{1,5},{4,8},{5,9},{6,2},{7,3},{8,12},{9,13},{10,6},{11,7},{1... | collective-permute-start | bytes 294920 | tf_op jit(solution)/shard_map/ppermute | solution.py:42
  166.1 16.5 %collective-permute-start.38 = (bf16[8,1,2,16,384]{4,3,2,1,0:T(8,128)(2,1)S(1)}, bf16[8,1,2,16,384]{4,3,2,1,0:T(8,128)(2,1)S(1)}, u32[]{:S(2)}, u32[]{:S(2)}) collective-permute-start(bf16[8,1,2,16,384]{4,3,2,1,0:T(8,128)(2,1)S(1)} %pack.9.refs_7_), channel_id=1, source_target_pairs={{0,16},{1,17},{2,18},{3,19},{4,20},{5,21},{6,22},{7,23},{8,24},{9,... | collective-permute-start | bytes 589832 | tf_op jit(solution)/shard_map/ppermute | solution.py:42
  181.5 20.8 %collective-permute-start.54 = (bf16[384,768]{1,0:T(8,128)(2,1)S(1)}, bf16[384,768]{1,0:T(8,128)(2,1)S(1)}, u32[]{:S(2)}, u32[]{:S(2)}) collective-permute-start(bf16[384,768]{1,0:T(8,128)(2,1)S(1)} %collective-permute-done.50.refs_3_), channel_id=1, source_target_pairs={{0,1},{1,0},{2,3},{3,2},{4,5},{5,4},{6,7},{7,6},{8,9},{9,8},{10,11... | collective-permute-start | bytes 1769480 | tf_op jit(solution)/shard_map/ppermute | solution.py:42
  181.6 22.5 %collective-permute-start.53 = (bf16[384,768]{1,0:T(8,128)(2,1)S(1)}, bf16[384,768]{1,0:T(8,128)(2,1)S(1)}, u32[]{:S(2)}, u32[]{:S(2)}) collective-permute-start(bf16[384,768]{1,0:T(8,128)(2,1)S(1)} %collective-permute-done.49.refs_2_), channel_id=1, source_target_pairs={{0,1},{1,0},{2,3},{3,2},{4,5},{5,4},{6,7},{7,6},{8,9},{9,8},{10,11... | collective-permute-start | bytes 1769480 | tf_op jit(solution)/shard_map/ppermute | solution.py:42
  182.1 22.3 %collective-permute-start.52 = (bf16[384,768]{1,0:T(8,128)(2,1)S(1)}, bf16[384,768]{1,0:T(8,128)(2,1)S(1)}, u32[]{:S(2)}, u32[]{:S(2)}) collective-permute-start(bf16[384,768]{1,0:T(8,128)(2,1)S(1)} %collective-permute-done.48.refs_1_), channel_id=1, source_target_pairs={{0,1},{1,0},{2,3},{3,2},{4,5},{5,4},{6,7},{7,6},{8,9},{9,8},{10,11... | collective-permute-start | bytes 1769480 | tf_op jit(solution)/shard_map/ppermute | solution.py:42
  182.2 22.4 %collective-permute-start.51 = (bf16[384,768]{1,0:T(8,128)(2,1)S(1)}, bf16[384,768]{1,0:T(8,128)(2,1)S(1)}, u32[]{:S(2)}, u32[]{:S(2)}) collective-permute-start(bf16[384,768]{1,0:T(8,128)(2,1)S(1)} %collective-permute-done.47.refs_0_), channel_id=1, source_target_pairs={{0,1},{1,0},{2,3},{3,2},{4,5},{5,4},{6,7},{7,6},{8,9},{9,8},{10,11... | collective-permute-start | bytes 1769480 | tf_op jit(solution)/shard_map/ppermute | solution.py:42
  189.5 7.6 %collective-permute-start.40 = (bf16[8,1,2,16,384]{4,3,2,1,0:T(8,128)(2,1)S(1)}, bf16[8,1,2,16,384]{4,3,2,1,0:T(8,128)(2,1)S(1)}, u32[]{:S(2)}, u32[]{:S(2)}) collective-permute-start(bf16[8,1,2,16,384]{4,3,2,1,0:T(8,128)(2,1)S(1)} %pack.9.refs_7_), channel_id=1, source_target_pairs={{0,32},{1,33},{2,34},{3,35},{4,36},{5,37},{6,38},{7,39},{8,40},{9,... | collective-permute-start | bytes 589832 | tf_op jit(solution)/shard_map/ppermute | solution.py:42
  204.4 7.7 %collective-permute-start.42 = (bf16[128,384]{1,0:T(8,128)(2,1)S(1)}, bf16[128,384]{1,0:T(8,128)(2,1)S(1)}, u32[]{:S(2)}, u32[]{:S(2)}) collective-permute-start(bf16[128,384]{1,0:T(8,128)(2,1)S(1)} %get-tuple-element.125), channel_id=1, source_target_pairs={{0,2},{1,3},{2,0},{3,1},{4,6},{5,7},{6,4},{7,5},{8,10},{9,11},{10,... | collective-permute-start | bytes 294920 | tf_op jit(solution)/shard_map/ppermute | solution.py:42
  204.6 8.7 %collective-permute-start.43 = (bf16[128,384]{1,0:T(8,128)(2,1)S(1)}, bf16[128,384]{1,0:T(8,128)(2,1)S(1)}, u32[]{:S(2)}, u32[]{:S(2)}) collective-permute-start(bf16[128,384]{1,0:T(8,128)(2,1)S(1)} %get-tuple-element.126), channel_id=1, source_target_pairs={{0,3},{1,2},{2,1},{3,0},{4,7},{5,6},{6,5},{7,4},{8,11},{9,10},{10,... | collective-permute-start | bytes 294920 | tf_op jit(solution)/shard_map/ppermute | solution.py:42
  (33 other events, 271.0 us)
